TPU v7x, 32 devices: a whole 2x2x4 slice. The times are simulated.
32 devices in a mesh: dp: 8 (over z, y), mp: 4 (over x, core).
Axes of the slice: x: 2, y: 2, z: 4, core: 2. Of those that a mesh axis runs over, the one named last changes fastest.
Arguments:
- tokens: bfloat16 [16384, 768], P(('dp', 'mp')), may hold values from -6 to 6
- doc_lengths: int32 [8, 4], P('dp'), may hold values from 1 to 1024, 1792 in all within a row
- attn_gain: float32 [768], replicated, may hold values from 0.5 to 1.5
- attn_shift: float32 [768], replicated, may hold values from -1.75 to 1.75
- query_weight: bfloat16 [768, 768], P(None, 'mp'), may hold values from -0.21875 to 0.21875
- query_bias: float32 [768], P('mp'), may hold values from -1.75 to 1.75
- key_weight: bfloat16 [768, 64], replicated, may hold values from -0.21875 to 0.21875
- key_bias: float32 [64], replicated, may hold values from -3 to 3
- value_weight: bfloat16 [768, 64], replicated, may hold values from -0.21875 to 0.21875
- value_bias: float32 [64], replicated, may hold values from -1.75 to 1.75
- out_weight: bfloat16 [768, 768], P('mp'), may hold values from -0.875 to 0.875
- out_bias: float32 [768], replicated, may hold values from -1.75 to 1.75
- mlp_gain: float32 [768], replicated, may hold values from 0.5 to 1.5
- mlp_shift: float32 [768], replicated, may hold values from -1.75 to 1.75
- up_weight: bfloat16 [768, 3072], P(None, 'mp'), may hold values from -0.21875 to 0.21875
- up_bias: float32 [3072], P('mp'), may hold values from -1.75 to 1.75
- down_weight: bfloat16 [3072, 768], P('mp'), may hold values from -0.21875 to 0.21875
- down_bias: float32 [768], replicated, may hold values from -1.75 to 1.75
- out_grad: bfloat16 [16384, 768], P(('dp', 'mp')), may hold values from -6 to 6
Outputs:
- block_out: bfloat16 [16384, 768], P(('dp', 'mp'))
- input_grad: bfloat16 [16384, 768], P(('dp', 'mp'))
- attn_gain_grad: float32 [768], replicated
- attn_shift_grad: float32 [768], replicated
- query_weight_grad: float32 [768, 768], P(None, 'mp')
- query_bias_grad: float32 [768], P('mp')
- key_weight_grad: float32 [768, 64], replicated
- key_bias_grad: float32 [64], replicated
- value_weight_grad: float32 [768, 64], replicated
- value_bias_grad: float32 [64], replicated
- out_weight_grad: float32 [768, 768], P('mp')
- out_bias_grad: float32 [768], replicated
- mlp_gain_grad: float32 [768], replicated
- mlp_shift_grad: float32 [768], replicated
- up_weight_grad: float32 [768, 3072], P(None, 'mp')
- up_bias_grad: float32 [3072], P('mp')
- down_weight_grad: float32 [3072, 768], P('mp')
- down_bias_grad: float32 [768], replicated
All inputs are finite; a program needn't handle non-finite values.
Results may differ from a plain program's by a relative error of at most 0.02.
Values may be sent and summed in bfloat16 or wider, within the bound.
A program may use at most 128 MiB of HBM per device.

v0:
```python
from functools import partial

import jax
import jax.numpy as jnp
from jax import lax
from jax.sharding import PartitionSpec as P

HD = 64
ROT = 16
SLOT = 2048
DOCS = 4


epsilon = 1e-05


def normalize(values):
    average = jnp.mean(values, axis=-1, keepdims=True)
    centered = values - average
    inv_std = lax.rsqrt(jnp.mean(centered * centered, axis=-1, keepdims=True) + epsilon)
    return (centered * inv_std, inv_std)


def rotate(values, cos_table, sine_table):
    half_rot = ROT // 2
    lower_part = values[..., :half_rot]
    upper_part = values[..., half_rot:ROT]
    return jnp.concatenate(
        [
            lower_part * cos_table - upper_part * sine_table,
            upper_part * cos_table + lower_part * sine_table,
            values[..., ROT:],
        ],
        axis=-1,
    )


def row_layout(lengths):
    slot_index = jnp.arange(SLOT, dtype=jnp.int32)
    doc_ends = jnp.cumsum(lengths, axis=-1)
    doc_starts = doc_ends - lengths
    segment = jnp.sum((slot_index[:, None] >= doc_ends[..., None, :]).astype(jnp.int32), axis=-1)
    doc_begins = jnp.concatenate([doc_starts, doc_ends[..., -1:]], axis=-1)
    labels = jnp.arange(DOCS + 1, dtype=jnp.int32)
    picked = jnp.sum(jnp.where(segment[..., None] == labels, doc_begins[..., None, :], 0), axis=-1)
    return (segment, slot_index - picked)


def angles(position):
    half_rot = ROT // 2
    frequency = 10000.0 ** (-(2.0 * jnp.arange(half_rot, dtype=jnp.float32)) / ROT)
    angle_grid = position.astype(jnp.float32)[..., None] * frequency
    return (jnp.cos(angle_grid), jnp.sin(angle_grid))


def inner_rows(left, right):
    return lax.dot_general(
        left, right, (((0,), (0,)), ((), ())), preferred_element_type=jnp.float32
    )


def times_transposed(left, right):
    return lax.dot_general(
        left, right, (((1,), (1,)), ((), ())), preferred_element_type=jnp.float32
    )


def block_scores(query_block, key_row, seg_row, first_row):
    block_rows = query_block.shape[0]
    scores = jnp.einsum(
        "bhe,ke->hbk", query_block, key_row, preferred_element_type=jnp.float32
    ) * HD ** (-0.5)
    query_index = first_row + jnp.arange(block_rows, dtype=jnp.int32)
    key_index = jnp.arange(SLOT, dtype=jnp.int32)
    seg_rows = lax.dynamic_slice_in_dim(seg_row, first_row, block_rows)
    allowed = (seg_rows[:, None] == seg_row[None, :]) & (key_index[None, :] <= query_index[:, None])
    return (scores, allowed)


def attend_forward(queries, key_rows, value_rows, segment):
    total_rows, heads = (queries.shape[0], queries.shape[1])
    groups = total_rows // SLOT
    block_rows = min(512, SLOT)
    block_count = SLOT // block_rows
    key_groups = key_rows.reshape(groups, SLOT, HD)
    value_groups = value_rows.reshape(groups, SLOT, HD)

    def one_block(block_item):
        query_block, item_index = block_item
        row_index = item_index // block_count
        first_row = item_index % block_count * block_rows
        key_row = lax.dynamic_index_in_dim(key_groups, row_index, 0, keepdims=False)
        value_row = lax.dynamic_index_in_dim(value_groups, row_index, 0, keepdims=False)
        seg_row = lax.dynamic_index_in_dim(segment, row_index, 0, keepdims=False)
        scores, allowed = block_scores(query_block, key_row, seg_row, first_row)
        scores = jnp.where(allowed[None], scores, -1e30)
        peak = jnp.max(scores, axis=-1, keepdims=True)
        expo = jnp.exp(scores - peak)
        totals = jnp.sum(expo, axis=-1, keepdims=True)
        probs_low = (expo / totals).astype(jnp.bfloat16)
        context = jnp.einsum(
            "hbk,ke->bhe", probs_low, value_row, preferred_element_type=jnp.float32
        )
        return (context, (peak + jnp.log(totals))[..., 0])

    item_list = jnp.arange(groups * block_count, dtype=jnp.int32)
    context, summary = lax.map(
        one_block, (queries.reshape(groups * block_count, block_rows, heads, HD), item_list)
    )
    return (context.reshape(total_rows, heads * HD), summary)


def attend_backward(queries, key_rows, value_rows, segment, summary, context_grad):
    total_rows, heads = (queries.shape[0], queries.shape[1])
    groups = total_rows // SLOT
    block_rows = min(512, SLOT)
    block_count = SLOT // block_rows
    key_groups = key_rows.reshape(groups, SLOT, HD)
    value_groups = value_rows.reshape(groups, SLOT, HD)

    def one_block(block_item):
        query_block, grad_block, summary_block, item_index = block_item
        row_index = item_index // block_count
        first_row = item_index % block_count * block_rows
        key_row = lax.dynamic_index_in_dim(key_groups, row_index, 0, keepdims=False)
        value_row = lax.dynamic_index_in_dim(value_groups, row_index, 0, keepdims=False)
        seg_row = lax.dynamic_index_in_dim(segment, row_index, 0, keepdims=False)
        scores, allowed = block_scores(query_block, key_row, seg_row, first_row)
        probs = jnp.where(allowed[None], jnp.exp(scores - summary_block[..., None]), 0.0)
        probs_low = probs.astype(jnp.bfloat16)
        prob_grad = jnp.einsum(
            "bhe,ke->hbk", grad_block, value_row, preferred_element_type=jnp.float32
        )
        delta = jnp.sum(probs * prob_grad, axis=-1, keepdims=True)
        score_grad = (probs * (prob_grad - delta)).astype(jnp.bfloat16)
        query_part = jnp.einsum(
            "hbk,ke->bhe", score_grad, key_row, preferred_element_type=jnp.float32
        ) * HD ** (-0.5)
        key_part = jnp.einsum(
            "hbk,bhe->ke", score_grad, query_block, preferred_element_type=jnp.float32
        ) * HD ** (-0.5)
        value_part = jnp.einsum(
            "hbk,bhe->ke", probs_low, grad_block, preferred_element_type=jnp.float32
        )
        return (query_part, key_part, value_part)

    item_list = jnp.arange(groups * block_count, dtype=jnp.int32)
    query_part, key_part, value_part = lax.map(
        one_block,
        (
            queries.reshape(groups * block_count, block_rows, heads, HD),
            context_grad.reshape(groups * block_count, block_rows, heads, HD),
            summary,
            item_list,
        ),
    )
    key_grad = jnp.sum(key_part.reshape(groups, block_count, SLOT, HD), axis=1).reshape(
        total_rows, HD
    )
    value_grad = jnp.sum(value_part.reshape(groups, block_count, SLOT, HD), axis=1).reshape(
        total_rows, HD
    )
    return (query_part.reshape(total_rows, heads, HD), key_grad, value_grad)


def forward_local(gathered, segment, cos_table, sine_table, local_weights):
    (
        attn_gain,
        attn_shift,
        query_weight,
        query_bias,
        key_weight,
        key_bias,
        value_weight,
        value_bias,
        mlp_gain,
        mlp_shift,
        up_weight,
        up_bias,
    ) = local_weights
    total_rows = gathered.shape[0]
    heads = query_weight.shape[1] // HD
    normed, unused_std = normalize(gathered.astype(jnp.float32))
    attn_in = (normed * attn_gain + attn_shift).astype(jnp.bfloat16)
    mlp_in = (normed * mlp_gain + mlp_shift).astype(jnp.bfloat16)
    queries = jnp.dot(attn_in, query_weight, preferred_element_type=jnp.float32) + query_bias
    queries = rotate(
        queries.reshape(total_rows, heads, HD), cos_table[:, None, :], sine_table[:, None, :]
    ).astype(jnp.bfloat16)
    key_value = jnp.dot(
        attn_in,
        jnp.concatenate([key_weight, value_weight], axis=1),
        preferred_element_type=jnp.float32,
    )
    key_value = key_value + jnp.concatenate([key_bias, value_bias])
    key_rows = rotate(key_value[:, :HD], cos_table, sine_table).astype(jnp.bfloat16)
    value_rows = key_value[:, HD:].astype(jnp.bfloat16)
    context, summary = attend_forward(queries, key_rows, value_rows, segment)
    context = context.astype(jnp.bfloat16)
    hidden_pre = jnp.dot(mlp_in, up_weight, preferred_element_type=jnp.float32) + up_bias
    hidden = jax.nn.gelu(hidden_pre, approximate=False).astype(jnp.bfloat16)
    return (
        attn_in,
        mlp_in,
        queries,
        key_rows,
        value_rows,
        context,
        summary,
        hidden_pre,
        hidden,
        normed,
    )


def per_device(
    tokens,
    doc_lengths,
    attn_gain,
    attn_shift,
    query_weight,
    query_bias,
    key_weight,
    key_bias,
    value_weight,
    value_bias,
    out_weight,
    out_bias,
    mlp_gain,
    mlp_shift,
    up_weight,
    up_bias,
    down_weight,
    down_bias,
    out_grad,
):
    shard_rows = tokens.shape[0]
    my_first = lax.axis_index("mp") * shard_rows
    segment, position = row_layout(doc_lengths)
    cos_table, sine_table = angles(position.reshape(-1))
    shard_valid = lax.dynamic_slice_in_dim(segment.reshape(-1), my_first, shard_rows) < DOCS
    local_weights = (
        attn_gain,
        attn_shift,
        query_weight,
        query_bias,
        key_weight,
        key_bias,
        value_weight,
        value_bias,
        mlp_gain,
        mlp_shift,
        up_weight,
        up_bias,
    )
    gathered = lax.all_gather(tokens, "mp", axis=0, tiled=True)
    kept = forward_local(gathered, segment, cos_table, sine_table, local_weights)
    context_fwd, hidden_fwd = (kept[5], kept[8])
    branch_sum = lax.psum_scatter(
        jnp.dot(context_fwd, out_weight, preferred_element_type=jnp.float32)
        + jnp.dot(hidden_fwd, down_weight, preferred_element_type=jnp.float32),
        "mp",
        scatter_dimension=0,
        tiled=True,
    )
    token_values = tokens.astype(jnp.float32)
    block_out = (token_values + branch_sum + out_bias + down_bias).astype(jnp.bfloat16)
    grad_shard = out_grad * shard_valid[:, None].astype(jnp.bfloat16)
    regathered = lax.all_gather(tokens, "mp", axis=0, tiled=True)
    kept = forward_local(regathered, segment, cos_table, sine_table, local_weights)
    (
        attn_in,
        mlp_in,
        queries,
        key_rows,
        value_rows,
        context,
        summary,
        hidden_pre,
        hidden,
        normed_all,
    ) = kept
    grad_rows = lax.all_gather(grad_shard, "mp", axis=0, tiled=True)
    out_weight_grad = inner_rows(context, grad_rows)
    down_weight_grad = inner_rows(hidden, grad_rows)
    bias_grad = jnp.sum(grad_shard, axis=0, dtype=jnp.float32)
    context_grad = times_transposed(grad_rows, out_weight).astype(jnp.bfloat16)
    hidden_grad = times_transposed(grad_rows, down_weight)
    unused_out, gelu_pull = jax.vjp(partial(jax.nn.gelu, approximate=False), hidden_pre)
    pre_grad = gelu_pull(hidden_grad)[0].astype(jnp.bfloat16)
    up_weight_grad = inner_rows(mlp_in, pre_grad)
    up_bias_grad = jnp.sum(pre_grad, axis=0, dtype=jnp.float32)
    mlp_part = times_transposed(pre_grad, up_weight)
    query_grad, key_part, value_part = attend_backward(
        queries, key_rows, value_rows, segment, summary, context_grad
    )
    total_rows = query_grad.shape[0]
    query_grad = (
        rotate(query_grad, cos_table[:, None, :], -sine_table[:, None, :])
        .reshape(total_rows, -1)
        .astype(jnp.bfloat16)
    )
    key_part = rotate(key_part, cos_table, -sine_table)
    query_weight_grad = inner_rows(attn_in, query_grad)
    query_bias_grad = jnp.sum(query_grad, axis=0, dtype=jnp.float32)
    attn_part = times_transposed(query_grad, query_weight)
    normed, inv_std = normalize(token_values)
    attn_rows = lax.dynamic_slice_in_dim(attn_in, my_first, shard_rows)
    attn_grad, mlp_grad, key_grad, value_grad = (
        lax.psum_scatter(attn_part, "mp", scatter_dimension=0, tiled=True),
        lax.psum_scatter(mlp_part, "mp", scatter_dimension=0, tiled=True),
        lax.psum_scatter(key_part, "mp", scatter_dimension=0, tiled=True),
        lax.psum_scatter(value_part, "mp", scatter_dimension=0, tiled=True),
    )
    key_low = key_grad.astype(jnp.bfloat16)
    value_low = value_grad.astype(jnp.bfloat16)
    attn_grad = (
        attn_grad
        + times_transposed(key_low, key_weight)
        + times_transposed(value_low, value_weight)
    )
    attn_gain_grad = jnp.sum(attn_grad * normed, axis=0)
    attn_shift_grad = jnp.sum(attn_grad, axis=0)
    mlp_gain_grad = jnp.sum(mlp_grad * normed, axis=0)
    mlp_shift_grad = jnp.sum(mlp_grad, axis=0)
    normed_grad = attn_grad * attn_gain + mlp_grad * mlp_gain
    key_weight_grad = inner_rows(attn_rows, key_low)
    key_bias_grad = jnp.sum(key_low, axis=0, dtype=jnp.float32)
    value_weight_grad = inner_rows(attn_rows, value_low)
    value_bias_grad = jnp.sum(value_low, axis=0, dtype=jnp.float32)
    input_grad = inv_std * (
        normed_grad
        - jnp.mean(normed_grad, axis=-1, keepdims=True)
        - normed * jnp.mean(normed_grad * normed, axis=-1, keepdims=True)
    )
    input_grad = (input_grad + grad_shard.astype(jnp.float32)).astype(jnp.bfloat16)
    (
        key_weight_grad,
        key_bias_grad,
        value_weight_grad,
        value_bias_grad,
        attn_gain_grad,
        attn_shift_grad,
        mlp_gain_grad,
        mlp_shift_grad,
        bias_grad,
    ) = lax.psum(
        (
            key_weight_grad,
            key_bias_grad,
            value_weight_grad,
            value_bias_grad,
            attn_gain_grad,
            attn_shift_grad,
            mlp_gain_grad,
            mlp_shift_grad,
            bias_grad,
        ),
        ("dp", "mp"),
    )
    (
        query_weight_grad,
        query_bias_grad,
        out_weight_grad,
        up_weight_grad,
        up_bias_grad,
        down_weight_grad,
    ) = lax.psum(
        (
            query_weight_grad,
            query_bias_grad,
            out_weight_grad,
            up_weight_grad,
            up_bias_grad,
            down_weight_grad,
        ),
        "dp",
    )
    return (
        block_out,
        input_grad,
        attn_gain_grad,
        attn_shift_grad,
        query_weight_grad,
        query_bias_grad,
        key_weight_grad,
        key_bias_grad,
        value_weight_grad,
        value_bias_grad,
        out_weight_grad,
        bias_grad,
        mlp_gain_grad,
        mlp_shift_grad,
        up_weight_grad,
        up_bias_grad,
        down_weight_grad,
        bias_grad,
    )


def solution(mesh):
    placed = (
        P(("dp", "mp"), None),
        P("dp", None),
        P(),
        P(),
        P(None, "mp"),
        P("mp"),
        P(),
        P(),
        P(),
        P(),
        P("mp", None),
        P(),
        P(),
        P(),
        P(None, "mp"),
        P("mp"),
        P("mp", None),
        P(),
        P(("dp", "mp"), None),
    )
    return jax.shard_map(
        per_device,
        mesh=mesh,
        in_specs=placed,
        out_specs=(
            P(("dp", "mp"), None),
            P(("dp", "mp"), None),
            P(),
            P(),
            P(None, "mp"),
            P("mp"),
            P(),
            P(),
            P(),
            P(),
            P("mp", None),
            P(),
            P(),
            P(),
            P(None, "mp"),
            P("mp"),
            P("mp", None),
            P(),
        ),
        check_vma=False,
    )
```

profile of v0, /device:TPU:0, one launch (start us, length us, event | category | flops | bytes accessed | tf_op | source)
XLA Modules:
  0.0 958.1 jit_solution(4647311742938053690)
XLA Ops:
  14.9 26.0 %all-gather.3.cloned.1.call-done = bf16[2048,768]{1,0:T(8,128)(2,1)} async-done(((bf16[512,768]{1,0:T(8,128)(2,1)}), bf16[2048,768]{1,0:T(8,128)(2,1)}) %all-gather.3.cloned.1.call-update) | async-done | bytes 3145744 | tf_op jit(solution)/shard_map/all_gather | solution.py:256
  53.2 96.5 %while.43 = (s32[]{:T(128)}, bf16[4,512,3,64]{1,3,2,0:T(8,128)(2,1)S(1)}, f32[4,3,512]{2,1,0:T(4,128)S(1)}, s32[4]{0:T(128)S(1)}, s32[1,2048]{1,0:T(1,128)S(1)},...) while((s32[]{:T(128)}, ...), condition=%wide.region_15.16_spmd, body=%wide.region_12.15_spmd.sunk | while | flops 846199808 | bytes 43135804 | solution.py:107
  56.9 6.8 bitcast_reduce_fusion.3
  63.8 6.8 fusion.236
  81.1 6.8 bitcast_reduce_fusion.3
  105.2 6.8 bitcast_reduce_fusion.3
  129.3 6.8 bitcast_reduce_fusion.3
  159.1 181.0 %while.44 = (s32[]{:T(128)}, f32[4,512,3,64]{1,0,3,2:T(4,128)}, f32[4,2048,64]{1,2,0:T(8,128)}, f32[4,2048,64]{1,2,0:T(8,128)}, s32[4]{0:T(128)S(1)}, /*index=5*...) while((s32[]{:T(128)}, f32[4,512,3,64]{1,0,3,2:T(4,128)}, ...), condition=%wide.region_18.19_spmd, body=%wide.region_16.18_spmd.sunk | while | flops 2063825920 | bytes 182910384 | solution.py:148
  182.8 8.6 dynamic_update_slice.55
  196.3 8.3 fusion.252
  228.0 8.6 dynamic_update_slice.55
  241.5 8.3 fusion.252
  273.1 8.6 dynamic_update_slice.55
  286.7 8.3 fusion.252
  318.3 8.6 dynamic_update_slice.55
  331.8 8.3 fusion.252
  358.0 85.6 %while.42 = (s32[]{:T(128)}, bf16[4,512,3,64]{1,3,2,0:T(8,128)(2,1)}, s32[4]{0:T(128)S(1)}, s32[1,2048]{1,0:T(1,128)S(1)}, bf16[4,512,3,64]{1,3,2,0:T(8,128)(2,1...) while((s32[]{:T(128)}, ...), condition=%wide.region_8.9_spmd, body=%wide.region_5.8_spmd.sunk | while | flops 827329024 | bytes 28409132 | solution.py:107
  361.8 10.0 %fusion.232 = (f32[3,512]{1,0:T(4,128)S(1)}, f32[3,512,2048]{2,1,0:T(8,128)}) fusion(pred[512,2048]{1,0:T(8,128)(4,1)S(1)} %fusion.231, bf16[1,2048,64]{1,2,0:T(8,128)(2,1)S(1)} %get-tuple-element.756, bf16[4,512,3,64]{1,3,2,0:T(8,128)(2,1)} %get-tuple-element.755, s32[]{:T(128)} %get-tuple-element.738), kind=kOutput, calls=%fused_computation.219.clone.1 | convolution fusion | flops 415238144 | bytes 14096896 | tf_op jit(solution)/shard_map/while/body/eval_jaxpr/sub | solution.py:98
  371.8 7.6 fusion.233
  383.1 10.0 %fusion.232 = (f32[3,512]{1,0:T(4,128)S(1)}, f32[3,512,2048]{2,1,0:T(8,128)}) fusion(pred[512,2048]{1,0:T(8,128)(4,1)S(1)} %fusion.231, bf16[1,2048,64]{1,2,0:T(8,128)(2,1)S(1)} %get-tuple-element.756, bf16[4,512,3,64]{1,3,2,0:T(8,128)(2,1)} %get-tuple-element.755, s32[]{:T(128)} %get-tuple-element.738), kind=kOutput, calls=%fused_computation.219.clone.1 | convolution fusion | flops 415238144 | bytes 14096896 | tf_op jit(solution)/shard_map/while/body/eval_jaxpr/sub | solution.py:98
  393.2 7.6 fusion.233
  404.5 10.6 %fusion.232 = (f32[3,512]{1,0:T(4,128)S(1)}, f32[3,512,2048]{2,1,0:T(8,128)}) fusion(pred[512,2048]{1,0:T(8,128)(4,1)S(1)} %fusion.231, bf16[1,2048,64]{1,2,0:T(8,128)(2,1)S(1)} %get-tuple-element.756, bf16[4,512,3,64]{1,3,2,0:T(8,128)(2,1)} %get-tuple-element.755, s32[]{:T(128)} %get-tuple-element.738), kind=kOutput, calls=%fused_computation.219.clone.1 | convolution fusion | flops 415238144 | bytes 14096896 | tf_op jit(solution)/shard_map/while/body/eval_jaxpr/sub | solution.py:98
  415.2 7.3 fusion.233
  426.3 10.0 %fusion.232 = (f32[3,512]{1,0:T(4,128)S(1)}, f32[3,512,2048]{2,1,0:T(8,128)}) fusion(pred[512,2048]{1,0:T(8,128)(4,1)S(1)} %fusion.231, bf16[1,2048,64]{1,2,0:T(8,128)(2,1)S(1)} %get-tuple-element.756, bf16[4,512,3,64]{1,3,2,0:T(8,128)(2,1)} %get-tuple-element.755, s32[]{:T(128)} %get-tuple-element.738), kind=kOutput, calls=%fused_computation.219.clone.1 | convolution fusion | flops 415238144 | bytes 14096896 | tf_op jit(solution)/shard_map/while/body/eval_jaxpr/sub | solution.py:98
  436.3 7.3 fusion.233
  450.9 17.9 %convert_reduce_fusion.1 = (f32[768]{0:T(1024)S(1)}, bf16[2048,768]{1,0:T(8,128)(2,1)}, f32[2048,768]{1,0:T(8,128)S(1)}) fusion(f32[2048,768]{1,0:T(8,128)S(1)} %fusion.154, f32[768]{0:T(1024)S(1)} %copy-done.41, bf16[2048,768]{1,0:T(8,128)(2,1)S(1)} %copy-done.11, bf16[768,768]{1,0:T(8,128)(2,1)S(1)} %copy-done), kind=kOutput, calls=%fused_computation.108 | convolution fusion | flops 2533883136 | bytes 20060160 | tf_op jit(solution)/shard_map/dot_general | solution.py:63
  477.6 7.5 fusion.172
  509.5 21.8 %all-reduce.2 = (f32[192]{0:T(256)}, f32[768]{0:T(1024)}) all-reduce(f32[192]{0:T(256)S(1)} %reduce_sum.233, f32[768]{0:T(1024)S(1)} %get-tuple-element.519), channel_id=1, replica_groups=mesh['dp'=8,'mp'=4] {'dp'}, use_global_device_ids=true, to_apply=%region_33.34 | all-reduce | flops 960 | bytes 7680 | tf_op jit(solution)/shard_map/psum | solution.py:368
  534.6 60.9 %reduce-scatter.14.cloned.1.call-done = f32[512,768]{1,0:T(8,128)} async-done(((f32[2048,768]{1,0:T(8,128)}), f32[512,768]{1,0:T(8,128)}) %reduce-scatter.14.cloned.1.call-update) | async-done | bytes 1572880 | tf_op jit(solution)/shard_map/reduce_scatter | solution.py:311
  601.1 40.1 %all-reduce = (f32[768]{0:T(1024)}, f32[768]{0:T(1024)}, f32[64]{0:T(128)}, f32[64]{0:T(128)}, f32[768]{0:T(1024)S(1)}, /*index=5*/f32[768]{0:T(1024)}, f32[768]{0:T(1024)}) all-reduce(f32[768]{0:T(1024)S(1)} %get-tuple-element.536, f32[768]{0:T(1024)S(1)} %get-tuple-element.537, ...), channel_id=1, replica_groups=mesh['dp'=8,'mp'=4] {'dp','mp'}, use_global_device_ids=true, to_apply=%region_28.29 | all-reduce | flops 3968 | bytes 31744 | tf_op jit(solution)/shard_map/psum | solution.py:347
  644.1 87.1 %all-reduce.7.cloned.1.call-done = (f32[768,64]{0,1:T(8,128)}, f32[768,64]{0,1:T(8,128)}) async-done(((f32[768,64]{0,1:T(8,128)}, f32[768,64]{0,1:T(8,128)}), (f32[768,64]{0,1:T(8,128)}, f32[768,64]{0,1:T(8,128)})) %all-reduce.7.cloned.1.call-update) | async-done | bytes 393232 | tf_op jit(solution)/shard_map/psum | solution.py:347
  731.2 207.5 %all-reduce.9.cloned.1.call-done = (f32[768,192]{0,1:T(8,128)}, f32[192,768]{1,0:T(8,128)}, f32[768,768]{1,0:T(8,128)}, f32[768,768]{1,0:T(8,128)}) async-done(((f32[768,192]{0,1:T(8,128)}, f32[192,768]{1,0:T(8,128)}, f32[768,768]{1,0:T(8,128)}, f32[768,768]{1,0:T(8,128)}), (f32[768,192]{0,1:T(8,128)}, f32[192,768]{1,0:T(8,128)}, f32[768,768]{1,0:T(8,128)}, ...) | async-done | bytes 5898256 | tf_op jit(solution)/shard_map/psum | solution.py:368
  (315 shorter events, 277.3 us)
Async XLA Ops:
  7.2 443.7 %copy-start = (bf16[768,768]{1,0:T(8,128)(2,1)S(1)}, bf16[768,768]{1,0:T(8,128)(2,1)}, u32[]{:S(2)}) copy-start(bf16[768,768]{1,0:T(8,128)(2,1)} %param.41) | copy-start | bytes 3538948
  7.2 39.2 %copy-start.36 = (f32[768]{0:T(1024)S(1)}, f32[768]{0:T(1024)}, u32[]{:S(2)}) copy-start(f32[768]{0:T(1024)} %param.27) | copy-start | bytes 9220
  7.2 39.2 %copy-start.40 = (f32[768]{0:T(1024)S(1)}, f32[768]{0:T(1024)}, u32[]{:S(2)}) copy-start(f32[768]{0:T(1024)} %param.28) | copy-start | bytes 9220
  7.2 33.7 %all-gather.3.cloned.1.call-start = ((), (), s32[]{:S(2)}) async-start(), calls=%async_computation.5 | async-start | bytes 3932160 | tf_op jit(solution)/shard_map/all_gather | solution.py:256
  8.0 141.8 %all-gather.5.cloned.1.call-start = ((), (), s32[]{:S(2)}) async-start(), calls=%async_computation.7 | async-start | bytes 3932160 | tf_op jit(solution)/shard_map/all_gather | solution.py:283
  11.9 488.8 %reduce-scatter.10.cloned.1.call-start = ((), (), s32[]{:S(2)}) async-start(), calls=%async_computation.9 | async-start | bytes 655360 | tf_op jit(solution)/shard_map/reduce_scatter | solution.py:312
  13.2 37.3 %copy-start.47 = (f32[8]{0:T(128)}, f32[8]{0:T(128)S(1)}, u32[]{:S(2)}) copy-start(f32[8]{0:T(128)S(1)} %multiply_power_fusion) | copy-start | bytes 100
  14.1 36.4 %copy-start.32 = (f32[2048]{0:T(1024)}, f32[2048]{0:T(1024)S(1)}, u32[]{:S(2)}) copy-start(f32[2048]{0:T(1024)S(1)} %subtract_convert_fusion.1) | copy-start | bytes 24580
  14.9 33.1 %copy-start.24 = (bf16[768,64]{0,1:T(8,128)(2,1)S(1)}, bf16[768,64]{0,1:T(8,128)(2,1)}, u32[]{:S(2)}) copy-start(bf16[768,64]{0,1:T(8,128)(2,1)} %param.33) | copy-start | bytes 294916
  14.9 33.1 %copy-start.26 = (bf16[768,64]{0,1:T(8,128)(2,1)S(1)}, bf16[768,64]{0,1:T(8,128)(2,1)}, u32[]{:S(2)}) copy-start(bf16[768,64]{0,1:T(8,128)(2,1)} %param.31) | copy-start | bytes 294916
  53.1 96.6 %copy-start.28 = (bf16[192,768]{1,0:T(8,128)(2,1)S(1)}, bf16[192,768]{1,0:T(8,128)(2,1)}, u32[]{:S(2)}) copy-start(bf16[192,768]{1,0:T(8,128)(2,1)} %param.35) | copy-start | bytes 884740
  159.1 182.9 %copy-start.33 = (f32[2048]{0:T(1024)S(1)}, f32[2048]{0:T(1024)}, u32[]{:S(2)}) copy-start(f32[2048]{0:T(1024)} %copy-done.32) | copy-start | bytes 24580
  159.1 182.9 %copy-start.48 = (f32[8]{0:T(128)S(1)}, f32[8]{0:T(128)}, u32[]{:S(2)}) copy-start(f32[8]{0:T(128)} %copy-done.47) | copy-start | bytes 100
  343.2 159.7 %reduce-scatter.12.cloned.1.call-start = ((), (), s32[]{:S(2)}) async-start(), calls=%async_computation.10 | async-start | bytes 655360 | tf_op jit(solution)/shard_map/reduce_scatter | solution.py:313
  345.8 187.3 %reduce-scatter.8.cloned.1.call-start = ((), (), s32[]{:S(2)}) async-start(), calls=%async_computation.8 | async-start | bytes 7864320 | tf_op jit(solution)/shard_map/reduce_scatter | solution.py:310
  357.0 177.6 %reduce-scatter.6.cloned.1.call-start = ((), (), s32[]{:S(2)}) async-start(), calls=%async_computation.6 | async-start | bytes 7864320 | tf_op jit(solution)/shard_map/reduce_scatter | solution.py:259
  358.0 87.5 %copy-start.31 = (f32[2048]{0:T(1024)S(1)}, f32[2048]{0:T(1024)}, u32[]{:S(2)}) copy-start(f32[2048]{0:T(1024)} %copy-done.30) | copy-start | bytes 24580
  358.0 87.6 %copy-start.35 = (f32[2048]{0:T(1024)S(1)}, f32[2048]{0:T(1024)}, u32[]{:S(2)}) copy-start(f32[2048]{0:T(1024)} %copy-done.34) | copy-start | bytes 24580
  358.0 87.6 %copy-start.42 = (f32[768]{0:T(1024)S(1)}, f32[768]{0:T(1024)}, u32[]{:S(2)}) copy-start(f32[768]{0:T(1024)} %param.37) | copy-start | bytes 9220
  358.0 87.6 %copy-start.50 = (f32[768]{0:T(1024)S(1)}, f32[768]{0:T(1024)}, u32[]{:S(2)}) copy-start(f32[768]{0:T(1024)} %param.38) | copy-start | bytes 9220
  476.3 119.2 %reduce-scatter.14.cloned.1.call-start = ((), (), s32[]{:S(2)}) async-start(), calls=%async_computation.11 | async-start | bytes 7864320 | tf_op jit(solution)/shard_map/reduce_scatter | solution.py:311
  485.1 246.1 %all-reduce.7.cloned.1.call-start = ((), (), s32[]{:S(2)}) async-start(), calls=%async_computation.12 | async-start | bytes 786432 | tf_op jit(solution)/shard_map/psum | solution.py:347
  505.0 26.4 %copy-start.18 = (f32[512,64]{0,1:T(8,128)S(1)}, f32[512,64]{0,1:T(8,128)}, u32[]{:S(2)}) copy-start(f32[512,64]{0,1:T(8,128)} %reduce-scatter.12.cloned.1.call-done) | copy-start | bytes 393220
  505.0 26.5 %copy-start.27 = (bf16[768,64]{0,1:T(8,128)(2,1)S(1)}, bf16[768,64]{0,1:T(8,128)(2,1)}, u32[]{:S(2)}) copy-start(bf16[768,64]{0,1:T(8,128)(2,1)} %param.31) | copy-start | bytes 294916
  505.1 433.7 %all-reduce.9.cloned.1.call-start = ((), (), s32[]{:S(2)}) async-start(), calls=%async_computation.13 | async-start | bytes 11796480 | tf_op jit(solution)/shard_map/psum | solution.py:368
  505.1 90.4 %copy-start.25 = (bf16[768,64]{0,1:T(8,128)(2,1)S(1)}, bf16[768,64]{0,1:T(8,128)(2,1)}, u32[]{:S(2)}) copy-start(bf16[768,64]{0,1:T(8,128)(2,1)} %param.33) | copy-start | bytes 294916
  505.1 90.4 %copy-start.37 = (f32[768]{0:T(1024)S(1)}, f32[768]{0:T(1024)}, u32[]{:S(2)}) copy-start(f32[768]{0:T(1024)} %param.27) | copy-start | bytes 9220
  505.1 90.4 %copy-start.43 = (f32[768]{0:T(1024)S(1)}, f32[768]{0:T(1024)}, u32[]{:S(2)}) copy-start(f32[768]{0:T(1024)} %param.42) | copy-start | bytes 9220
  505.2 90.4 %copy-start.44 = (f32[768]{0:T(1024)S(1)}, f32[768]{0:T(1024)}, u32[]{:S(2)}) copy-start(f32[768]{0:T(1024)} %param.36) | copy-start | bytes 9220
  509.0 92.1 %copy-start.38 = (f32[768]{0:T(1024)S(1)}, f32[768]{0:T(1024)}, u32[]{:S(2)}) copy-start(f32[768]{0:T(1024)} %get-tuple-element.524) | copy-start | bytes 9220
  509.0 132.1 %copy-start.10 = (bf16[512,768]{1,0:T(8,128)(2,1)S(1)}, bf16[512,768]{1,0:T(8,128)(2,1)}, u32[]{:S(2)}) copy-start(bf16[512,768]{1,0:T(8,128)(2,1)} %get-tuple-element.525) | copy-start | bytes 2359300
  641.2 310.0 %copy-start.46 = (f32[768]{0:T(1024)}, f32[768]{0:T(1024)S(1)}, u32[]{:S(2)}) copy-start(f32[768]{0:T(1024)S(1)} %get-tuple-element.904) | copy-start | bytes 9220
  (38 other events, 246.4 us)
Sparse Core Ops, SparseCore 0:
  9.6 31.2 all-gather.2
  43.0 28.5 all-gather.4
  343.3 21.6 reduce-scatter.9
  368.0 21.6 reduce-scatter.11
  392.1 58.4 reduce-scatter.7
  476.5 58.0 reduce-scatter.5
  537.1 58.3 reduce-scatter.13
  603.1 128.1 all-reduce.6
  737.0 201.6 all-reduce.8
where the time goes:
time: 964 us; the launch traced here: 958 us
  waiting for transfers between devices  384 us (40%)
  matrix products  296 us (31%)
  other arithmetic  90.6 us (9%)
  local copies, waits for them, and re-layouts  85.2 us (9%)
  blocking collectives  61.9 us (6%)
  loops' own time  24.6 us (3%)
  between operations  15.1 us (2%)
    psum x1, waiting for transfers between devices, per_device(): lax.psum((query_weight_grad, query_bias_grad, out_weight_grad, up_weight_...  208 us
    psum x1, waiting for transfers between devices, per_device(): lax.psum((key_weight_grad, key_bias_grad, value_weight_grad, value_bias_g...  87.1 us
    reduce_scatter x1, waiting for transfers between devices, per_device(): lax.psum_scatter(mlp_part, 'mp', scatter_dimension=0, tiled=True)  60.9 us
    dot_general x8, matrix products, one_block(): jnp.einsum('hbk,ke->bhe', probs_low, value_row, preferred_element_type=jn...  56.8 us
    sub x4, matrix products, one_block(): expo = jnp.exp(scores - peak)  40.6 us
    dot_general x6, matrix products, times_transposed(): lax.dot_general(left, right, (((1,), (1,)), ((), ())), preferred_element_...  40.4 us
    psum x1, blocking collectives, per_device(): lax.psum((key_weight_grad, key_bias_grad, value_weight_grad, value_bias_g...  40.1 us
    dot_general x8, matrix products, block_scores(): jnp.einsum('bhe,ke->hbk', query_block, key_row, preferred_element_type=jn...  38.3 us
  transfers between devices with their start and end apart: 9, of which 5 were waited for; matrix products, arithmetic and copies ran while one was open for 28% of the time, Pallas kernels for 0%

commit v1 on v0

v1 whole, which is shorter than its diff:
```python
from functools import partial

import jax
import jax.numpy as jnp
from jax import lax
from jax.experimental import pallas as pl
from jax.experimental.pallas import tpu as pltpu
from jax.sharding import PartitionSpec as P

HD = 64
ROT = 16
HALF = ROT // 2
SLOT = 2048
VALID = 1792
LONGEST = 1024
DOCS = 4
EPS = 1e-05
BLK = 256
NBLK = SLOT // BLK
BAND = LONGEST // BLK
PADBLK = VALID // BLK
LANES = 128
F32 = jnp.float32
BF16 = jnp.bfloat16


def dot(a, b):
    return lax.dot_general(a, b, (((1,), (0,)), ((), ())), preferred_element_type=F32)


def dot_t(a, b):
    return lax.dot_general(a, b, (((1,), (1,)), ((), ())), preferred_element_type=F32)


def t_dot(a, b):
    return lax.dot_general(a, b, (((0,), (0,)), ((), ())), preferred_element_type=F32)


def key_blocks(i):
    if i >= PADBLK:
        return list(range(PADBLK, i + 1))
    return list(range(max(0, i - BAND), i + 1))


SLOTS = {}
for _i in range(NBLK):
    for _j in key_blocks(_i):
        SLOTS[(_i, _j)] = len(SLOTS)
NSLOT = len(SLOTS)


def doc_begin(slot, ends):
    begin = jnp.zeros_like(slot)
    for end in ends:
        begin = jnp.where(slot >= end, end, begin)
    return begin


def doc_ends(doc_ref):
    ends = []
    total = 0
    for d in range(DOCS):
        total = total + doc_ref[0, d]
        ends.append(total)
    return ends


def build_tables(doc_ref, cos_ref, sa_ref, sb_ref):
    ends = doc_ends(doc_ref)
    slot = lax.broadcasted_iota(jnp.int32, (HALF, SLOT), 1)
    freq_index = lax.broadcasted_iota(jnp.int32, (HALF, SLOT), 0)
    position = (slot - doc_begin(slot, ends)).astype(F32)
    freq = jnp.zeros((HALF, SLOT), F32)
    for i in range(HALF):
        freq = jnp.where(freq_index == i, 10000.0 ** (-(2.0 * i) / ROT), freq)
    angle = position * freq
    lane = lax.broadcasted_iota(jnp.int32, (3 * HALF, LANES), 1) % HD
    row = lax.broadcasted_iota(jnp.int32, (3 * HALF, LANES), 0) % HALF
    low = (lane == row).astype(BF16)
    high = (lane == row + HALF).astype(BF16)
    rest = lax.broadcasted_iota(jnp.int32, (SLOT, LANES), 1) % HD >= ROT

    def parts(v):
        a = v.astype(BF16)
        r = v - a.astype(F32)
        b = r.astype(BF16)
        c = (r - b.astype(F32)).astype(BF16)
        return jnp.concatenate([a, b, c], axis=0)

    cos = parts(jnp.cos(angle))
    sine = parts(jnp.sin(angle))
    cos_ref[...] = jnp.where(rest, 1.0, t_dot(cos, low + high))
    sa_ref[...] = -t_dot(sine, low)
    sb_ref[...] = t_dot(sine, high)


def rope(v, cos, sa, sb):
    return v * cos + pltpu.roll(v, LANES - HALF, 1) * sa + pltpu.roll(v, HALF, 1) * sb


def unrope(v, cos, sa, sb):
    return v * cos - pltpu.roll(v, LANES - HALF, 1) * sa - pltpu.roll(v, HALF, 1) * sb


def mlp_kernel(
    heads,
    doc_ref, x_ref, g_ref, ag_ref, as_ref, wq_ref, bq_ref, wk_ref, bk_ref, wv_ref, bv_ref, wo_ref, mg_ref, ms_ref, wu_ref, bu_ref, wd_ref,
    q_ref, kv_ref, dctx_ref, xh_ref, gm_ref, outp_ref, em_ref, gup_ref, gdown_ref, bup_ref, cos_ref, sa_ref, sb_ref,
    ain, min_, hp, hid, dg, dpre, wq, wkv, wo, bq, bkv,
):
    pairs = (heads + 1) // 2
    width = pairs * LANES
    rows = 512
    depth = x_ref.shape[1]
    ff = wu_ref.shape[1]
    build_tables(doc_ref, cos_ref, sa_ref, sb_ref)
    used = heads * HD
    wq[:, :used] = wq_ref[...]
    bq[:, :used] = bq_ref[...]
    wo[:used, :] = wo_ref[...]
    if used < width:
        wq[:, used:] = jnp.zeros((depth, width - used), BF16)
        bq[:, used:] = jnp.zeros((1, width - used), F32)
        wo[used:, :] = jnp.zeros((width - used, depth), BF16)
    wkv[:, :HD] = wk_ref[...]
    wkv[:, HD:] = wv_ref[...]
    bkv[:, :HD] = bk_ref[...]
    bkv[:, HD:] = bv_ref[...]
    gup_ref[...] = jnp.zeros_like(gup_ref)
    gdown_ref[...] = jnp.zeros_like(gdown_ref)
    bup_ref[...] = jnp.zeros_like(bup_ref)

    def chunk(c, carry):
        first = pl.multiple_of(c * rows, rows)
        here = pl.ds(first, rows)

        def norm(r, carry):
            at = pl.ds(pl.multiple_of(first + r * 32, 32), 32)
            to = pl.ds(pl.multiple_of(r * 32, 32), 32)
            v = x_ref[at, :].astype(F32)
            mean = jnp.mean(v, axis=-1, keepdims=True)
            v = v - mean
            inv = lax.rsqrt(jnp.mean(v * v, axis=-1, keepdims=True) + EPS)
            v = v * inv
            xh_ref[at, :] = v.astype(BF16)
            ain[to, :] = (v * ag_ref[...] + as_ref[...]).astype(BF16)
            min_[to, :] = (v * mg_ref[...] + ms_ref[...]).astype(BF16)
            slot = first + r * 32 + lax.broadcasted_iota(jnp.int32, (32, depth), 0)
            gm_ref[at, :] = jnp.where(slot < VALID, g_ref[at, :].astype(F32), 0.0).astype(BF16)
            return carry

        lax.fori_loop(0, rows // 32, norm, 0)
        cos, sa, sb = cos_ref[here, :], sa_ref[here, :], sb_ref[here, :]
        qf = dot(ain[...], wq[...]) + bq[...]
        for p in range(pairs):
            q_ref[p, here, :] = (rope(qf[:, p * LANES : (p + 1) * LANES], cos, sa, sb) * HD**-0.5).astype(BF16)
        kvf = dot(ain[...], wkv[...]) + bkv[...]
        is_key = lax.broadcasted_iota(jnp.int32, (rows, LANES), 1) < HD
        kv_ref[here, :] = jnp.where(is_key, rope(kvf, cos, sa, sb), kvf).astype(BF16)
        hp[...] = dot(min_[...], wu_ref[...])

        def act(r, carry):
            to = pl.ds(pl.multiple_of(r * 16, 16), 16)
            v = hp[to, :] + bu_ref[...]
            cdf = 0.5 * (1.0 + lax.erf(v * (0.5**0.5)))
            pdf = jnp.exp(-0.5 * v * v) * (2.0 * jnp.pi) ** -0.5
            hid[to, :] = (v * cdf).astype(BF16)
            dg[to, :] = (cdf + v * pdf).astype(BF16)
            return carry

        lax.fori_loop(0, rows // 16, act, 0)
        outp_ref[here, :] = dot(hid[...], wd_ref[...]).astype(BF16)
        g = gm_ref[here, :]
        dc = dot_t(g, wo[...]).astype(BF16)
        for p in range(pairs):
            dctx_ref[p, here, :] = dc[:, p * LANES : (p + 1) * LANES]
        hp[...] = dot_t(g, wd_ref[...])

        def back(r, acc):
            to = pl.ds(pl.multiple_of(r * 16, 16), 16)
            v = hp[to, :] * dg[to, :].astype(F32)
            dpre[to, :] = v.astype(BF16)
            return acc + v[:8] + v[8:]

        acc = lax.fori_loop(0, rows // 16, back, jnp.zeros((8, ff), F32))
        bup_ref[...] += jnp.sum(acc, axis=0, keepdims=True)
        em_ref[here, :] = (dot_t(dpre[...], wu_ref[...]) * mg_ref[...]).astype(BF16)
        gup_ref[...] += t_dot(xh_ref[here, :], dpre[...])
        gdown_ref[...] += t_dot(hid[...], g)
        return carry

    lax.fori_loop(0, SLOT // rows, chunk, 0)


def attention_kernel(
    heads,
    doc_ref, q_ref, kv_ref, dctx_ref, cos_ref, sa_ref, sb_ref,
    ctx_ref, dqkv_ref,
    kx, vx, probs, scores, total, left, dq, dk, dv, dcn,
):
    pairs = (heads + 1) // 2
    ends = doc_ends(doc_ref)
    lane = lax.broadcasted_iota(jnp.int32, (BLK, LANES), 1)
    low = lane < HD
    for b in range(NBLK):
        at = pl.ds(b * BLK, BLK)
        kv = kv_ref[at, :].astype(F32)
        vk = pltpu.roll(kv, HD, 1)
        zero = jnp.zeros_like(kv)
        kx[0, at, :] = jnp.where(low, kv, zero).astype(BF16)
        kx[1, at, :] = jnp.where(low, zero, vk).astype(BF16)
        vx[0, at, :LANES] = jnp.where(low, vk, zero).astype(BF16)
        vx[1, at, :LANES] = jnp.where(low, zero, kv).astype(BF16)
        vx[0, at, LANES:] = jnp.where(low, 1.0, 0.0).astype(BF16)
        vx[1, at, LANES:] = jnp.where(low, 0.0, 1.0).astype(BF16)
    dk[...] = jnp.zeros_like(dk)
    dv[...] = jnp.zeros_like(dv)

    for i in range(NBLK):
        at = pl.ds(i * BLK, BLK)
        blocks = key_blocks(i)
        slot = i * BLK + lax.broadcasted_iota(jnp.int32, (BLK, 1), 0)
        begin = doc_begin(slot, ends)
        total[...] = jnp.zeros_like(total)

        def head_fwd(h, carry):
            p, half = h // 2, h % 2
            qb = q_ref[p, at, :]
            peak = jnp.full((BLK, BLK), -1e30, F32)
            for n, j in enumerate(blocks):
                s = dot_t(qb, kx[half, pl.ds(j * BLK, BLK), :])
                key = j * BLK + lax.broadcasted_iota(jnp.int32, (BLK, BLK), 1)
                ok = key >= begin
                if i == j:
                    ok = ok & (key <= slot)
                s = jnp.where(ok, s, -1e30)
                scores[:, n * BLK : (n + 1) * BLK] = s
                peak = jnp.maximum(peak, s)
            top = jnp.max(peak, axis=-1, keepdims=True)
            acc = total[p]
            for n, j in enumerate(blocks):
                e = jnp.exp(scores[:, n * BLK : (n + 1) * BLK] - top).astype(BF16)
                probs[h, SLOTS[(i, j)]] = e
                acc = acc + dot(e, vx[half, pl.ds(j * BLK, BLK), :])
            total[p] = acc
            return carry

        lax.fori_loop(0, heads, head_fwd, 0)
        for p in range(pairs):
            norm = total[p, :, LANES:]
            norm = 1.0 / jnp.where(norm == 0.0, 1.0, norm)
            ctx = total[p, :, :LANES] * norm
            ctx_ref[p, at, :] = ctx.astype(BF16)
            dcs = (dctx_ref[p, at, :].astype(F32) * norm).astype(BF16)
            dcn[p, at, :] = dcs
            prod = dcs.astype(F32) * ctx
            extra = jnp.zeros((BLK, LANES), F32)
            for half, first in ((0, 0), (1, HD)):
                d = -jnp.sum(jnp.where(low if half == 0 else ~low, prod, 0.0), axis=-1, keepdims=True)
                d_top = d.astype(BF16).astype(F32)
                extra = jnp.where(lane == first, d_top, extra)
                extra = jnp.where(lane == first + 1, d - d_top, extra)
            left[p, at, :LANES] = dcs
            left[p, at, LANES:] = extra.astype(BF16)

    dq[...] = jnp.zeros_like(dq)
    for i in range(PADBLK):
        at = pl.ds(i * BLK, BLK)
        blocks = key_blocks(i)

        def head_bwd(h, carry):
            p, half = h // 2, h % 2
            lb = left[p, at, :]
            qb = q_ref[p, at, :]
            dc = dcn[p, at, :]
            acc = dq[p, at, :]
            for j in blocks:
                jat = pl.ds(j * BLK, BLK)
                e = probs[h, SLOTS[(i, j)]]
                ds = (e.astype(F32) * dot_t(lb, vx[half, jat, :])).astype(BF16)
                acc = acc + dot(ds, kx[half, jat, :])
                dk[half, jat, :] += t_dot(ds, qb)
                dv[half, jat, :] += t_dot(e, dc)
            dq[p, at, :] = acc
            return carry

        lax.fori_loop(0, heads, head_bwd, 0)

    for b in range(NBLK):
        at = pl.ds(b * BLK, BLK)
        cos, sa, sb = cos_ref[at, :], sa_ref[at, :], sb_ref[at, :]
        for p in range(pairs):
            dqkv_ref[at, p * LANES : (p + 1) * LANES] = (unrope(dq[p, at, :], cos, sa, sb) * HD**-0.5).astype(BF16)
        keys = dk[0, at, :] + pltpu.roll(dk[1, at, :], HD, 1)
        values = pltpu.roll(dv[0, at, :], HD, 1) + dv[1, at, :]
        both = jnp.where(low, unrope(keys, cos, sa, sb), values)
        dqkv_ref[at, pairs * LANES :] = both.astype(BF16)


VM = pl.BlockSpec(memory_space=pltpu.VMEM)
SM = pl.BlockSpec(memory_space=pltpu.SMEM)


def run_mlp(heads, doc, x_all, g_all, params):
    depth = x_all.shape[1]
    ff = params[-2].shape[1]
    pairs = (heads + 1) // 2
    width = pairs * LANES
    sh = jax.ShapeDtypeStruct
    return pl.pallas_call(
        partial(mlp_kernel, heads),
        out_shape=(
            sh((pairs, SLOT, LANES), BF16), sh((SLOT, LANES), BF16), sh((pairs, SLOT, LANES), BF16),
            sh((SLOT, depth), BF16), sh((SLOT, depth), BF16), sh((SLOT, depth), BF16), sh((SLOT, depth), BF16),
            sh((depth, ff), F32), sh((ff, depth), F32), sh((1, ff), F32),
            sh((SLOT, LANES), F32), sh((SLOT, LANES), F32), sh((SLOT, LANES), F32),
        ),
        in_specs=[SM] + [VM] * 16,
        out_specs=[VM] * 13,
        scratch_shapes=[
            pltpu.VMEM((512, depth), BF16), pltpu.VMEM((512, depth), BF16), pltpu.VMEM((512, ff), F32),
            pltpu.VMEM((512, ff), BF16), pltpu.VMEM((512, ff), BF16), pltpu.VMEM((512, ff), BF16),
            pltpu.VMEM((depth, width), BF16), pltpu.VMEM((depth, LANES), BF16), pltpu.VMEM((width, depth), BF16),
            pltpu.VMEM((1, width), F32), pltpu.VMEM((1, LANES), F32),
        ],
        compiler_params=pltpu.CompilerParams(vmem_limit_bytes=63 * 1024 * 1024),
        name="mlp",
    )(doc, x_all, g_all, *params)


def run_attention(heads, doc, q, kv, dctx, cos, sa, sb):
    pairs = (heads + 1) // 2
    sh = jax.ShapeDtypeStruct
    return pl.pallas_call(
        partial(attention_kernel, heads),
        out_shape=(sh((pairs, SLOT, LANES), BF16), sh((SLOT, (pairs + 1) * LANES), BF16)),
        in_specs=[SM] + [VM] * 6,
        out_specs=[VM] * 2,
        scratch_shapes=[
            pltpu.VMEM((2, SLOT, LANES), BF16), pltpu.VMEM((2, SLOT, 2 * LANES), BF16),
            pltpu.VMEM((heads, NSLOT, BLK, BLK), BF16), pltpu.VMEM((BLK, (BAND + 1) * BLK), F32),
            pltpu.VMEM((pairs, BLK, 2 * LANES), F32), pltpu.VMEM((pairs, SLOT, 2 * LANES), BF16),
            pltpu.VMEM((pairs, SLOT, LANES), F32), pltpu.VMEM((2, SLOT, LANES), F32), pltpu.VMEM((2, SLOT, LANES), F32),
            pltpu.VMEM((pairs, SLOT, LANES), BF16),
        ],
        compiler_params=pltpu.CompilerParams(vmem_limit_bytes=63 * 1024 * 1024),
        name="attention",
    )(doc, q, kv, dctx, cos, sa, sb)


def per_device(
    tokens, doc_lengths, attn_gain, attn_shift, query_weight, query_bias, key_weight, key_bias, value_weight, value_bias,
    out_weight, out_bias, mlp_gain, mlp_shift, up_weight, up_bias, down_weight, down_bias, out_grad,
):
    shard = tokens.shape[0]
    first = lax.axis_index("mp") * shard
    heads = query_weight.shape[1] // HD
    used = heads * HD
    pairs = (heads + 1) // 2
    row = lambda v: v.reshape(1, -1)
    x_all = lax.all_gather(tokens, "mp", axis=0, tiled=True)
    g_all = lax.all_gather(out_grad, "mp", axis=0, tiled=True)
    params = (
        row(attn_gain), row(attn_shift), query_weight, row(query_bias), key_weight, row(key_bias), value_weight, row(value_bias),
        out_weight, row(mlp_gain), row(mlp_shift), up_weight, row(up_bias), down_weight,
    )
    q, kv, dctx, xh, gm, outp, em, gup, gdown, bup, cos, sa, sb = run_mlp(heads, doc_lengths, x_all, g_all, params)
    gup, gdown = lax.optimization_barrier((gup.astype(BF16), gdown.astype(BF16)))
    gup, gdown = lax.psum((gup, gdown), "dp")
    ctx, dqkv = run_attention(heads, doc_lengths, q, kv, dctx, cos, sa, sb)
    ctx = jnp.concatenate([ctx[p] for p in range(pairs)], axis=1)[:, :used]
    branch = dot(ctx, out_weight) + outp.astype(F32)
    branch = lax.psum_scatter(branch.astype(BF16), "mp", scatter_dimension=0, tiled=True)
    gout = t_dot(ctx, gm)
    qkv_weight = jnp.concatenate([query_weight, jnp.zeros((query_weight.shape[0], pairs * LANES - used), BF16), key_weight, value_weight], axis=1)
    e = dot_t(dqkv, qkv_weight) * attn_gain + em.astype(F32)
    e = lax.psum_scatter(e.astype(BF16), "mp", scatter_dimension=0, tiled=True).astype(F32)
    gqkv = t_dot(xh, dqkv)
    bqkv = jnp.sum(dqkv, axis=0, dtype=F32)
    g_sum = jnp.sum(gm, axis=0, dtype=F32)
    split = pairs * LANES
    gq, gout, gkv = lax.psum((gqkv[:, :used].astype(BF16), gout.astype(BF16), gqkv[:, split:].astype(BF16)), "dp")
    vectors = lax.psum(jnp.concatenate([bqkv, g_sum, bup[0]]), "dp")
    gq, gout, gkv, gup, gdown = (v.astype(F32) for v in (gq, gout, gkv, gup, gdown))
    depth = tokens.shape[1]
    bqkv, g_sum, bup = vectors[: split + LANES], vectors[split + LANES : split + LANES + depth], vectors[split + LANES + depth :]
    bq, bkv = bqkv[:used], bqkv[split:]
    wq32, wu32 = query_weight.astype(F32), up_weight.astype(F32)
    kv_weight = jnp.concatenate([key_weight, value_weight], axis=1).astype(F32)
    sums = jnp.concatenate(
        [
            (gkv).reshape(-1),
            bkv,
            jnp.sum(gq * wq32, axis=1) + jnp.sum(gkv * kv_weight, axis=1),
            jnp.sum(bq * wq32, axis=1) + jnp.sum(bkv * kv_weight, axis=1),
            jnp.sum(gup * wu32, axis=1),
            jnp.sum(bup * wu32, axis=1),
        ]
    )
    sums = lax.psum(sums, "mp")
    n = depth * LANES
    gkv, bkv = sums[:n].reshape(depth, LANES), sums[n : n + LANES]
    attn_gain_grad, attn_shift_grad, mlp_gain_grad, mlp_shift_grad = sums[n + LANES :].reshape(4, depth)
    query_weight_grad = attn_gain[:, None] * gq + attn_shift[:, None] * bq
    kv_weight_grad = attn_gain[:, None] * gkv + attn_shift[:, None] * bkv
    up_weight_grad = mlp_gain[:, None] * gup + mlp_shift[:, None] * bup
    x = tokens.astype(F32)
    block_out = (x + branch.astype(F32) + out_bias + down_bias).astype(BF16)
    mean = jnp.mean(x, axis=-1, keepdims=True)
    xc = x - mean
    inv = lax.rsqrt(jnp.mean(xc * xc, axis=-1, keepdims=True) + EPS)
    xn = xc * inv
    slot = first + lax.broadcasted_iota(jnp.int32, (shard, 1), 0)
    g = jnp.where(slot < VALID, out_grad.astype(F32), 0.0)
    dx = inv * (e - jnp.mean(e, axis=-1, keepdims=True) - xn * jnp.mean(e * xn, axis=-1, keepdims=True))
    input_grad = (g + dx).astype(BF16)
    return (
        block_out, input_grad, attn_gain_grad, attn_shift_grad, query_weight_grad, bq, kv_weight_grad[:, :HD], bkv[:HD],
        kv_weight_grad[:, HD:], bkv[HD:], gout, g_sum, mlp_gain_grad, mlp_shift_grad, up_weight_grad, bup, gdown, g_sum,
    )


def solution(mesh):
    rows = P(("dp", "mp"), None)
    placed = (
        rows, P("dp", None), P(), P(), P(None, "mp"), P("mp"), P(), P(), P(), P(), P("mp", None), P(), P(), P(),
        P(None, "mp"), P("mp"), P("mp", None), P(), rows,
    )
    outs = (
        rows, rows, P(), P(), P(None, "mp"), P("mp"), P(), P(), P(), P(), P("mp", None), P(), P(), P(),
        P(None, "mp"), P("mp"), P("mp", None), P(),
    )
    return jax.shard_map(per_device, mesh=mesh, in_specs=placed, out_specs=outs, check_vma=False)
```

time: 964 us -> 451 us (0.47)
  matrix products: 296 us -> 14.8 us
  waiting for transfers between devices: 384 us -> 252 us
  Pallas kernels: 0 us -> 105 us
  other arithmetic: 90.6 us -> 20.2 us
  local copies, waits for them, and re-layouts: 85.2 us -> 20.8 us
  blocking collectives: 61.9 us -> 23.2 us
  loops' own time: 24.6 us -> 0 us
    dot_general x49 -> x4, matrix products: 256 us -> 14.8 us  [the longest x1 5.53 us: dot_t(): lax.dot_general(a, b, (((1,), (1,)), ((), ())), preferred_element_type=F32)]
    psum x2, waiting for transfers between devices: 295 us -> 121 us  [the longest x1 105 us: per_device(): lax.psum((gqkv[:, :used].astype(BF16), gout.astype(BF16), gqkv[:, split:]...]
    pallas_call x0 -> x2, Pallas kernels: none -> 105 us  [the longest x1 53.8 us: run_attention(): pl.pallas_call(partial(attention_kernel, heads), out_shape=(sh((pairs, SL...]
    sub x4 -> x0, matrix products: 40.6 us -> none  [one_block(): expo = jnp.exp(scores - peak)]
    psum x2 -> x1, blocking collectives: 61.9 us -> 23.2 us  [per_device(): vectors = lax.psum(jnp.concatenate([bqkv, g_sum, bup[0]]), 'dp')]
    dynamic_update_slice x8 -> x0, local copies, waits for them, and re-layouts: 36.1 us -> none  [attend_forward(): lax.map(one_block, (queries.reshape(groups * block_count, block_rows, hea...]
    reduce_sum x16 -> x8, other arithmetic: 41.5 us -> 10.6 us  [the longest x1 3.78 us: per_device(): jnp.sum(bup * wu32, axis=1)]
    all_gather x2, waiting for transfers between devices: 26 us -> 56.8 us  [the longest x1 30.1 us: per_device(): g_all = lax.all_gather(out_grad, 'mp', axis=0, tiled=True)]
  transfers between devices with their start and end apart: 9 -> 6, of which waited for: 5 -> 6; matrix products, arithmetic and copies ran while one was open for 28% -> 7% of each run, Pallas kernels for 0% -> 0%
where the time goes in v1:
time: 451 us; the launch traced here: 450 us
  waiting for transfers between devices  252 us (56%)
  Pallas kernels  105 us (23%)
  blocking collectives  23.2 us (5%)
  local copies, waits for them, and re-layouts  20.8 us (5%)
  other arithmetic  20.2 us (4%)
  matrix products  14.8 us (3%)
  between operations  14.5 us (3%)
    psum x1, waiting for transfers between devices, per_device(): lax.psum((gqkv[:, :used].astype(BF16), gout.astype(BF16), gqkv[:, split:]...  105 us
    pallas_call x1, Pallas kernels, run_attention(): pl.pallas_call(partial(attention_kernel, heads), out_shape=(sh((pairs, SL...  53.8 us
    pallas_call x1, Pallas kernels, run_mlp(): pl.pallas_call(partial(mlp_kernel, heads), out_shape=(sh((pairs, SLOT, LA...  51.3 us
    reduce_scatter x1, waiting for transfers between devices, per_device(): lax.psum_scatter(branch.astype(BF16), 'mp', scatter_dimension=0, tiled=True)  38.6 us
    reduce_scatter x1, waiting for transfers between devices, per_device(): lax.psum_scatter(e.astype(BF16), 'mp', scatter_dimension=0, tiled=True)  34.1 us
    all_gather x1, waiting for transfers between devices, per_device(): g_all = lax.all_gather(out_grad, 'mp', axis=0, tiled=True)  30.1 us
    all_gather x1, waiting for transfers between devices, per_device(): x_all = lax.all_gather(tokens, 'mp', axis=0, tiled=True)  26.6 us
    psum x1, blocking collectives, per_device(): vectors = lax.psum(jnp.concatenate([bqkv, g_sum, bup[0]]), 'dp')  23.2 us
  transfers between devices with their start and end apart: 6, of which 6 were waited for; matrix products, arithmetic and copies ran while one was open for 7% of the time, Pallas kernels for 0%

profile of v1, /device:TPU:0, one launch (start us, length us, event | category | flops | bytes accessed | tf_op | source)
XLA Modules:
  0.0 450.5 jit_solution(2736682461491103330)
XLA Ops:
  8.8 0.9 copy.40.wq_ref
  14.3 26.6 %all-gather.3.cloned.1.call-done.x_ref = bf16[2048,768]{1,0:T(8,128)(2,1)} async-done(((bf16[512,768]{1,0:T(8,128)(2,1)}), bf16[2048,768]{1,0:T(8,128)(2,1)}) %all-gather.3.cloned.1.call-update) | async-done | bytes 3145744 | tf_op jit(solution)/shard_map/all_gather | solution.py:361
  40.9 30.1 %all-gather.5.cloned.1.call-done.g_ref = bf16[2048,768]{1,0:T(8,128)(2,1)} async-done(((bf16[512,768]{1,0:T(8,128)(2,1)}), bf16[2048,768]{1,0:T(8,128)(2,1)}) %all-gather.5.cloned.1.call-update) | async-done | bytes 3145744 | tf_op jit(solution)/shard_map/all_gather | solution.py:362
  71.1 51.3 %mlp.1 = (bf16[2,2048,128]{2,1,0:T(8,128)(2,1)}, bf16[2048,128]{1,0:T(8,128)(2,1)}, bf16[2,2048,128]{2,1,0:T(8,128)(2,1)}, bf16[2048,768]{1,0:T(8,128)(2,1)}, bf...) custom-call(s32[1,4]{1,0:T(1,128)} %doc_ref.3, ...), custom_call_target="tpu_custom_call" | custom-call | tf_op jit(solution)/shard_map/mlp/pallas_call | solution.py:310
  122.4 53.8 %attention.1 = (bf16[2,2048,128]{2,1,0:T(8,128)(2,1)}, bf16[2048,384]{1,0:T(8,128)(2,1)}) custom-call(s32[1,4]{1,0:T(1,128)} %doc_ref.3, bf16[2,2048,128]{2,1,0:T(8,128)(2,1)} %get-tuple-element.35.q_ref, bf16[2048,128]{1,0:T(8,128)(2,1)} %get-tuple-element.36.kv_ref, bf16[2,2048,128]{2,1,0:T(8,128)(2,1)} %get-tuple-element.37.dctx_ref, ...), custom_call_target="tpu_custom_call" | custom-call | tf_op jit(solution)/shard_map/attention/pallas_call | solution.py:334
  176.1 3.9 convolution_convert_fusion
  181.9 1.1 convert_element_type.87
  183.0 1.0 copy-done.6
  184.0 1.1 convert_element_type.88
  185.1 1.2 copy-done.4
  186.3 1.5 convolution_convert_fusion.1
  189.3 1.7 convert_reduce_fusion.1
  191.5 23.2 %psum.50 = f32[1920]{0:T(1024)S(1)} all-reduce(f32[1920]{0:T(1024)S(1)} %pad_maximum_fusion.4), channel_id=1, replica_groups=mesh['dp'=8,'mp'=4] {'dp'}, use_global_device_ids=true, to_apply=%region_9.0 | all-reduce | flops 1920 | bytes 15360 | tf_op jit(solution)/shard_map/psum | solution.py:383
  214.8 104.7 %all-reduce.6.cloned.1.call-done = (bf16[768,128]{0,1:T(8,128)(2,1)}, bf16[768,192]{0,1:T(8,128)(2,1)}, bf16[768,768]{1,0:T(8,128)(2,1)}, bf16[192,768]{1,0:T(8,128)(2,1)}, bf16[768,768]{1,0:T(8,128)(2,1)}) async-done(((bf16[768,128]{0,1:T(8,128)(2,1)}, bf16[768,192]{0,1:T(8,128)(2,1)}, bf16[768,768]{1,0:T(8,128)(2,1)}, bf16[192,768]{1,0:T(8,128)(2,1)}, bf16[768,768]{1,0:T(8,128)(2,1)}), ...) | async-done | bytes 3145744 | tf_op jit(solution)/shard_map/psum | solution.py:382
  319.6 1.1 copy.43
  320.7 1.1 fusion.25
  321.8 3.8 fusion.2
  325.6 1.0 fusion.17
  327.6 5.5 %add_convert_fusion = bf16[2048,768]{1,0:T(8,128)(2,1)} fusion(bf16[2048,768]{1,0:T(8,128)(2,1)} %get-tuple-element.44, bf16[2048,384]{1,0:T(8,128)(2,1)S(1)} %copy-done.11, f32[768]{0:T(1024)S(1)} %copy-done.20, bf16[768,64]{0,1:T(8,128)(2,1)S(1)} %copy-done.17, bf16[768,64]{0,1:T(8,128)(2,1)S(1)} %copy-done.15, bf16[768,192]{0,1:T(8,128)(2,1)S(1)} %copy-done.13, ...), kind=kOutput, calls=%fused_computation.1 | convolution fusion | flops 1216610304 | bytes 8359680 | tf_op jit(solution)/shard_map/dot_general | solution.py:32
  333.2 1.8 copy-done.5
  335.0 3.9 add_convert_fusion.1
  338.9 1.1 copy-done
  340.6 1.6 convert_element_type.93
  342.2 0.9 convert_element_type.92
  343.0 15.9 %all-reduce.4.cloned.1.call-done = f32[101504]{0:T(1024)} async-done(((f32[101504]{0:T(1024)}), f32[101504]{0:T(1024)}) %all-reduce.4.cloned.1.call-update) | async-done | bytes 406032 | tf_op jit(solution)/shard_map/psum | solution.py:400
  359.6 1.3 fusion.27
  362.8 1.3 fusion.33
  364.1 1.4 fusion.32
  365.5 34.1 %reduce-scatter.5.cloned.1.call-done = bf16[512,768]{1,0:T(8,128)(2,1)} async-done(((bf16[2048,768]{1,0:T(8,128)(2,1)}), bf16[512,768]{1,0:T(8,128)(2,1)}) %reduce-scatter.5.cloned.1.call-update) | async-done | bytes 786448 | tf_op jit(solution)/shard_map/reduce_scatter | solution.py:377
  399.6 1.9 convert_reduce_fusion.2
  401.5 38.6 %reduce-scatter.3.cloned.1.call-done = bf16[512,768]{1,0:T(8,128)(2,1)} async-done(((bf16[2048,768]{1,0:T(8,128)(2,1)}), bf16[512,768]{1,0:T(8,128)(2,1)}) %reduce-scatter.3.cloned.1.call-update) | async-done | bytes 786448 | tf_op jit(solution)/shard_map/reduce_scatter | solution.py:373
  440.2 2.9 fusion.9
  (106 shorter events, 14.5 us)
Async XLA Ops:
  7.2 2.5 copy-start.15
  7.2 3.3 copy-start.16
  7.2 4.1 copy-start.20
  7.2 4.7 %copy-start.21 = (f32[768]{0:T(1024)S(1)}, f32[768]{0:T(1024)}, u32[]{:S(2)}) copy-start(f32[768]{0:T(1024)} %param.22) | copy-start | bytes 9220
  7.2 5.3 %copy-start.23 = (f32[768]{0:T(1024)S(1)}, f32[768]{0:T(1024)}, u32[]{:S(2)}) copy-start(f32[768]{0:T(1024)} %param.31) | copy-start | bytes 9220
  7.3 5.9 %copy-start.24 = (f32[768]{0:T(1024)S(1)}, f32[768]{0:T(1024)}, u32[]{:S(2)}) copy-start(f32[768]{0:T(1024)} %param.32) | copy-start | bytes 9220
  7.3 6.4 %copy-start.29 = (f32[768]{0:T(1024)S(1)}, f32[768]{0:T(1024)}, u32[]{:S(2)}) copy-start(f32[768]{0:T(1024)} %param.34) | copy-start | bytes 9220
  7.3 33.7 %all-gather.3.cloned.1.call-start = ((), (), s32[]{:S(2)}) async-start(), calls=%async_computation.2 | async-start | bytes 3932160 | tf_op jit(solution)/shard_map/all_gather | solution.py:361
  8.0 63.0 %all-gather.5.cloned.1.call-start = ((), (), s32[]{:S(2)}) async-start(), calls=%async_computation.3 | async-start | bytes 3932160 | tf_op jit(solution)/shard_map/all_gather | solution.py:362
  8.8 310.8 %all-reduce.6.cloned.1.call-start = ((), (), s32[]{:S(2)}) async-start(), calls=%async_computation.7 | async-start | bytes 6291456 | tf_op jit(solution)/shard_map/psum | solution.py:382
  176.1 5.3 %copy-start.14 = (bf16[2,2048,128]{2,1,0:T(8,128)(2,1)S(1)}, bf16[2,2048,128]{2,1,0:T(8,128)(2,1)}, u32[]{:S(2)}) copy-start(bf16[2,2048,128]{2,1,0:T(8,128)(2,1)} %get-tuple-element.41) | copy-start | bytes 3145732
  181.5 3.6 copy-start.8
  181.5 3.6 copy-start.9
  181.9 2.1 copy-start.6
  184.0 2.3 copy-start.4
  187.9 171.1 %all-reduce.4.cloned.1.call-start = ((), (), s32[]{:S(2)}) async-start(), calls=%async_computation.6 | async-start | bytes 819200 | tf_op jit(solution)/shard_map/psum | solution.py:400
  191.5 130.3 %copy-start.1 = (bf16[768,768]{1,0:T(8,128)(2,1)S(1)}, bf16[768,768]{1,0:T(8,128)(2,1)}, u32[]{:S(2)}) copy-start(bf16[768,768]{1,0:T(8,128)(2,1)} %wu_ref.1) | copy-start | bytes 3538948
  191.5 130.3 %copy-start.25 = (f32[768]{0:T(1024)S(1)}, f32[768]{0:T(1024)}, u32[]{:S(2)}) copy-start(f32[768]{0:T(1024)} %param.32) | copy-start | bytes 9220
  214.8 110.8 %copy-start.30 = (f32[192]{0:T(256)}, f32[192]{0:T(256)S(1)}, u32[]{:S(2)}) copy-start(f32[192]{0:T(256)S(1)} %slice.90) | copy-start | bytes 2308
  214.8 110.8 %copy-start.26 = (f32[768]{0:T(1024)}, f32[768]{0:T(1024)S(1)}, u32[]{:S(2)}) copy-start(f32[768]{0:T(1024)S(1)} %get-tuple-element.136) | copy-start | bytes 9220
  214.8 228.2 %copy-start.22 = (f32[768]{0:T(1024)}, f32[768]{0:T(1024)S(1)}, u32[]{:S(2)}) copy-start(f32[768]{0:T(1024)S(1)} %get-tuple-element.138) | copy-start | bytes 9220
  321.8 3.8 copy-start.19
  321.8 5.7 %copy-start.17 = (bf16[768,64]{0,1:T(8,128)(2,1)S(1)}, bf16[768,64]{0,1:T(8,128)(2,1)}, u32[]{:S(2)}) copy-start(bf16[768,64]{0,1:T(8,128)(2,1)} %param.27) | copy-start | bytes 294916
  325.6 1.9 copy-start.11
  325.6 2.0 copy-start.31
  327.5 72.1 %reduce-scatter.5.cloned.1.call-start = ((), (), s32[]{:S(2)}) async-start(), calls=%async_computation.5 | async-start | bytes 3932160 | tf_op jit(solution)/shard_map/reduce_scatter | solution.py:377
  333.1 1.9 copy-start.5
  333.1 107.0 %reduce-scatter.3.cloned.1.call-start = ((), (), s32[]{:S(2)}) async-start(), calls=%async_computation.4 | async-start | bytes 3932160 | tf_op jit(solution)/shard_map/reduce_scatter | solution.py:373
  361.1 79.1 %copy-start.2 = (bf16[512,768]{1,0:T(8,128)(2,1)S(1)}, bf16[512,768]{1,0:T(8,128)(2,1)}, u32[]{:S(2)}) copy-start(bf16[512,768]{1,0:T(8,128)(2,1)} %param.37) | copy-start | bytes 2359300
  361.1 79.1 %copy-start.27 = (f32[768]{0:T(1024)S(1)}, f32[768]{0:T(1024)}, u32[]{:S(2)}) copy-start(f32[768]{0:T(1024)} %param.36) | copy-start | bytes 9220
  361.1 79.1 %copy-start.28 = (f32[768]{0:T(1024)S(1)}, f32[768]{0:T(1024)}, u32[]{:S(2)}) copy-start(f32[768]{0:T(1024)} %param.30) | copy-start | bytes 9220
  399.6 40.6 %copy-start.3 = (bf16[512,768]{1,0:T(8,128)(2,1)S(1)}, bf16[512,768]{1,0:T(8,128)(2,1)}, u32[]{:S(2)}) copy-start(bf16[512,768]{1,0:T(8,128)(2,1)} %reduce-scatter.5.cloned.1.call-done) | copy-start | bytes 2359300
  (6 other events, 8.6 us)
Sparse Core Ops, SparseCore 0:
  9.7 31.2 all-gather.2
  42.5 28.5 all-gather.4
  188.0 131.5 all-reduce.5
  327.6 31.3 all-reduce.3
  361.3 38.1 reduce-scatter.4
  402.1 37.9 reduce-scatter.2

commit v2 on v1

v2 whole, which is shorter than its diff:
```python
from functools import partial

import jax
import jax.numpy as jnp
from jax import lax
from jax.experimental import pallas as pl
from jax.experimental.pallas import tpu as pltpu
from jax.sharding import PartitionSpec as P

HD = 64
ROT = 16
HALF = ROT // 2
SLOT = 2048
VALID = 1792
LONGEST = 1024
DOCS = 4
EPS = 1e-05
BLK = 256
NBLK = SLOT // BLK
BAND = LONGEST // BLK
PADBLK = VALID // BLK
LANES = 128
MP = 4
SHARD = SLOT // MP
RING = 8
EVENTS = 2 * RING - 1
F32 = jnp.float32
BF16 = jnp.bfloat16
MESH = pl.DeviceIdType.MESH


def dot(a, b):
    return lax.dot_general(a, b, (((1,), (0,)), ((), ())), preferred_element_type=F32)


def dot_t(a, b):
    return lax.dot_general(a, b, (((1,), (1,)), ((), ())), preferred_element_type=F32)


def t_dot(a, b):
    return lax.dot_general(a, b, (((0,), (0,)), ((), ())), preferred_element_type=F32)


def key_blocks(i):
    if i >= PADBLK:
        return list(range(PADBLK, i + 1))
    return list(range(max(0, i - BAND), i + 1))


SLOTS = {}
for _i in range(NBLK):
    for _j in key_blocks(_i):
        SLOTS[(_i, _j)] = len(SLOTS)
NSLOT = len(SLOTS)


def doc_begin(slot, ends):
    begin = jnp.zeros_like(slot)
    for end in ends:
        begin = jnp.where(slot >= end, end, begin)
    return begin


def doc_ends(doc_ref):
    ends = []
    total = 0
    for d in range(DOCS):
        total = total + doc_ref[0, d]
        ends.append(total)
    return ends


def build_tables(doc_ref, cos_ref, sine_ref):
    ends = doc_ends(doc_ref)
    slot = lax.broadcasted_iota(jnp.int32, (HALF, SLOT), 1)
    freq_index = lax.broadcasted_iota(jnp.int32, (HALF, SLOT), 0)
    position = (slot - doc_begin(slot, ends)).astype(F32)
    freq = jnp.zeros((HALF, SLOT), F32)
    for i in range(HALF):
        freq = jnp.where(freq_index == i, 10000.0 ** (-(2.0 * i) / ROT), freq)
    angle = position * freq
    lane = lax.broadcasted_iota(jnp.int32, (3 * HALF, LANES), 1) % HD
    row = lax.broadcasted_iota(jnp.int32, (3 * HALF, LANES), 0) % HALF
    low = jnp.where(lane == row, 1.0, 0.0)
    high = jnp.where(lane == row + HALF, 1.0, 0.0)
    rest = lax.broadcasted_iota(jnp.int32, (SLOT, LANES), 1) % HD >= ROT

    def parts(v):
        a = v.astype(BF16)
        r = v - a.astype(F32)
        b = r.astype(BF16)
        c = (r - b.astype(F32)).astype(BF16)
        return jnp.concatenate([a, b, c], axis=0)

    cos_ref[...] = jnp.where(rest, 1.0, t_dot(parts(jnp.cos(angle)), (low + high).astype(BF16)))
    sine_ref[...] = t_dot(parts(jnp.sin(angle)), (high - low).astype(BF16))


def partner(v):
    lane = lax.broadcasted_iota(jnp.int32, v.shape, 1) % HD
    return jnp.where(lane < HALF, pltpu.roll(v, LANES - HALF, 1), pltpu.roll(v, HALF, 1))


def rope(v, cos, sine):
    return v * cos + partner(v) * sine


def unrope(v, cos, sine):
    return v * cos - partner(v) * sine


def top_and_rest(v):
    top = v.astype(BF16)
    return top, (v - top.astype(F32)).astype(BF16)


def rows_of(first, count):
    return pl.ds(pl.multiple_of(first, count), count)


class Ring:
    def __init__(self, source, stage, slots, final, recv, send, place, right, left):
        self.source, self.stage, self.slots, self.final = source, stage, slots, final
        self.recv, self.send, self.place = recv, send, place
        self.to = (right, left)
        self.rows = stage.shape[1]

    def copy(self, way, src, dst, step):
        return pltpu.make_async_remote_copy(
            src_ref=src, dst_ref=dst, send_sem=self.send.at[way], recv_sem=self.recv.at[way, step],
            device_id={"dp": self.to[way]}, device_id_type=MESH,
        )

    def at(self, chunk, way):
        return rows_of((chunk * 2 + way) * self.rows, self.rows)

    def chunk(self, way, back):
        return lax.rem(self.place + 2 * RING - back, RING) if way == 0 else lax.rem(self.place + RING + back, RING)

    def event(self, e):
        last = RING - 1
        for way in range(2):
            stage, slots, source, final = self.stage, self.slots, self.source, self.final

            @pl.when(e == 0)
            def _():
                stage[way] = source[self.at(self.chunk(way, 0), way), :].astype(BF16)
                self.copy(way, stage.at[way], slots.at[way, 0], 0).start()

            @pl.when((e >= 1) & (e <= last))
            def _():
                got = slots.at[way, e - 1]
                self.copy(way, stage.at[way], got, e - 1).wait_recv()
                own = self.at(self.chunk(way, e), way)
                total = (slots[way, e - 1].astype(F32) + source[own, :]).astype(BF16)
                self.copy(way, stage.at[way], got, e - 1).wait_send()

                @pl.when(e < last)
                def _():
                    slots[way, e - 1] = total
                    self.copy(way, got, slots.at[way, e], e).start()

                @pl.when(e == last)
                def _():
                    final[own, :] = total
                    self.copy(way, final.at[own, :], final.at[own, :], e).start()

            @pl.when(e > last)
            def _():
                here = final.at[self.at(self.chunk(way, e - RING), way), :]
                self.copy(way, stage.at[way], here, e - 1).wait_recv()
                self.copy(way, here, here, e - 1).wait_send()

                @pl.when(e < EVENTS - 1)
                def _():
                    self.copy(way, here, here, e).start()


class Scatter:
    def __init__(self, part, mate_in, cross_in, send, recv, m, mate, cross):
        self.part, self.mate_in, self.cross_in, self.send, self.recv = part, mate_in, cross_in, send, recv
        self.m, self.mate, self.cross = m, mate, cross

    def copy(self, src, dst, index, to):
        return pltpu.make_async_remote_copy(
            src_ref=src, dst_ref=dst, send_sem=self.send.at[index], recv_sem=self.recv.at[index],
            device_id={"mp": to}, device_id_type=MESH,
        )

    def to_mate(self, b):
        index = (b // 4) * 2 + b % 2
        return self.copy(self.part.at[pl.ds(b * BLK, BLK), :], self.mate_in.at[index], index, self.mate)

    def to_cross(self, b):
        index = (b // 4) * 2 + b % 2
        return self.copy(self.mate_in.at[index], self.cross_in.at[b % 2], 4 + b % 2, self.cross)

    def mine(self, b):
        return self.m % 2 == (b // 2) % 2

    def offer(self, b):
        @pl.when(jnp.logical_not(self.mine(b)))
        def _():
            self.to_mate(b).start()

    def collect(self, b):
        index = (b // 4) * 2 + b % 2

        @pl.when(self.mine(b))
        def _():
            self.to_mate(b).wait_recv()

            @pl.when(self.m // 2 != b // 4)
            def _():
                def add(r, carry):
                    at = rows_of(r * 32, 32)
                    own = self.part[rows_of(b * BLK + r * 32, 32), :].astype(F32)
                    self.mate_in[index, at, :] = (self.mate_in[index, at, :].astype(F32) + own).astype(BF16)
                    return carry

                lax.fori_loop(0, BLK // 32, add, 0)
                self.to_cross(b).start()

    def total(self, k, at):
        own = self.part[rows_of((2 * self.m + k) * BLK + at, 32), :].astype(F32)
        index = (self.m // 2) * 2 + k
        return own + self.mate_in[index, rows_of(at, 32), :].astype(F32) + self.cross_in[k, rows_of(at, 32), :].astype(F32)

    def arrived(self, k):
        self.copy(self.mate_in.at[0], self.cross_in.at[k], 4 + k, self.cross).wait_recv()

    def drain(self, b):
        @pl.when(jnp.logical_not(self.mine(b)))
        def _():
            self.to_mate(b).wait_send()

        @pl.when(self.mine(b) & (self.m // 2 != b // 4))
        def _():
            self.to_cross(b).wait_send()


def layer_kernel(
    heads,
    doc_ref, tok_hbm, grad_hbm, ag_ref, as_ref, wq_ref, bq_ref, wk_ref, bk_ref, wv_ref, bv_ref, wo_ref, ob_ref, mg_ref, ms_ref,
    wu_hbm, bu_ref, wd_hbm,
    bout_hbm, ingrad_hbm, fdown_hbm, fup_hbm, fout_hbm, fqkv_hbm, kvg_hbm, vec_hbm,
    xs, gm, outp, em, gdown, gup, gout, gqkv, q, kv, dctx, dd, cos, sine, ctx, dqh, dk, dv, dqkv, wqkv, wo, wu, wd, bqkv, gsum,
    own_x, io,
    st_d, sl_d, f_d, st_u, sl_u, f_u, st_o, sl_o, f_o, st_q, sl_q, f_q,
    mo, co, me_, ce, kvx, vecx, kvg,
    loc, ag_send, ag_recv, rr, rs_, so_s, so_r, se_s, se_r, bf_s, bf_r,
):
    pairs = (heads + 1) // 2
    width = pairs * LANES
    used = heads * HD
    depth = tok_hbm.shape[1]
    ff = wu.shape[1]
    m = lax.axis_index("mp")
    d = lax.axis_index("dp")
    mate = m + 1 - 2 * (m % 2)
    cross = (m + 2) % MP
    far = (mate + 2) % MP
    inner, outer = d % RING, d // RING
    place = jnp.where(inner % 2 == 0, inner // 2, RING - 1 - inner // 2)

    def seat(p):
        return outer * RING + jnp.where(p < RING // 2, 2 * p, 2 * (RING - 1 - p) + 1)

    right, left = seat((place + 1) % RING), seat((place + RING - 1) % RING)

    local = [
        pltpu.make_async_copy(tok_hbm, xs.at[rows_of(m * SHARD, SHARD), :], loc.at[0]),
        pltpu.make_async_copy(wu_hbm, wu, loc.at[1]),
        pltpu.make_async_copy(wd_hbm, wd, loc.at[2]),
        pltpu.make_async_copy(tok_hbm, own_x, loc.at[3]),
    ]
    for c in local:
        c.start()
    local_g = [
        pltpu.make_async_copy(grad_hbm.at[pl.ds(k * BLK, BLK), :], gm.at[rows_of(m * SHARD + k * BLK, BLK), :], loc.at[4 + k])
        for k in range(2)
    ]

    def valid(shard, k):
        return 2 * shard + k < PADBLK

    for k in range(2):
        @pl.when(valid(m, k))
        def _():
            local_g[k].start()
    gm[VALID:, :] = jnp.zeros((SLOT - VALID, depth), BF16)

    barrier = pltpu.get_barrier_semaphore()
    for to in ({"mp": mate}, {"mp": cross}, {"dp": right}, {"dp": left}):
        pl.semaphore_signal(barrier, inc=1, device_id=to, device_id_type=MESH)
    pl.semaphore_wait(barrier, 4)

    def send(src, dst, index, to):
        return pltpu.make_async_remote_copy(
            src_ref=src, dst_ref=dst, send_sem=ag_send.at[index], recv_sem=ag_recv.at[index], device_id={"mp": to}, device_id_type=MESH
        )

    def half(ref, shard, k):
        return ref.at[rows_of(shard * SHARD + k * BLK, BLK), :]

    def x_cross(shard, k):
        return send(tok_hbm.at[pl.ds(k * BLK, BLK), :], half(xs, shard, k), k, cross)

    def x_mate(shard, k):
        return send(tok_hbm.at[pl.ds(k * BLK, BLK), :], half(xs, shard, k), 2 + k, mate)

    def g_cross(shard, k):
        return send(grad_hbm.at[pl.ds(k * BLK, BLK), :], half(gm, shard, k), 4 + k, cross)

    def g_mate(shard, k):
        return send(grad_hbm.at[pl.ds(k * BLK, BLK), :], half(gm, shard, k), 6 + k, mate)

    def x_pass(shard, k):
        return send(half(xs, shard, k), half(xs, shard, k), 8 + k, mate)

    def g_pass(shard, k):
        return send(half(gm, shard, k), half(gm, shard, k), 10 + k, mate)

    for k in range(2):
        x_cross(m, k).start()
    for k in range(2):
        x_mate(m, k).start()
    for k in range(2):
        @pl.when(valid(m, k))
        def _():
            g_mate(m, k).start()
    for k in range(2):
        @pl.when(valid(m, k))
        def _():
            g_cross(m, k).start()

    build_tables(doc_ref, cos, sine)
    wqkv[:, :used] = wq_ref[...]
    bqkv[:, :used] = bq_ref[...]
    wo[:used, :] = wo_ref[...]
    if used < width:
        wqkv[:, used:width] = jnp.zeros((depth, width - used), BF16)
        bqkv[:, used:width] = jnp.zeros((1, width - used), F32)
        wo[used:, :] = jnp.zeros((width - used, depth), BF16)
    wqkv[:, width : width + HD] = wk_ref[...]
    wqkv[:, width + HD :] = wv_ref[...]
    bqkv[:, width : width + HD] = bk_ref[...]
    bqkv[:, width + HD :] = bv_ref[...]
    gup[...] = jnp.zeros_like(gup)
    gdown[...] = jnp.zeros_like(gdown)
    gout[...] = jnp.zeros_like(gout)
    gsum[...] = jnp.zeros_like(gsum)
    dqkv[VALID:, :] = jnp.zeros((SLOT - VALID, width + LANES), BF16)

    def feed_forward(ain, min_, hp, hid, dg, dpre):
        def forward(c, slot):
            first = pl.multiple_of(c * SHARD, SHARD)
            here = pl.ds(first, SHARD)

            def norm(r, carry):
                at = rows_of(first + r * 32, 32)
                to = rows_of(r * 32, 32)
                v = xs[at, :].astype(F32)
                v = v - jnp.mean(v, axis=-1, keepdims=True)
                v = v * lax.rsqrt(jnp.mean(v * v, axis=-1, keepdims=True) + EPS)
                xs[at, :] = v.astype(BF16)
                ain[to, :] = (v * ag_ref[...] + as_ref[...]).astype(BF16)
                min_[to, :] = (v * mg_ref[...] + ms_ref[...]).astype(BF16)
                return carry

            lax.fori_loop(0, SHARD // 32, norm, 0)
            ct, st = cos[here, :], sine[here, :]
            qf = dot(ain[...], wqkv[:, :width]) + bqkv[:, :width]
            for p in range(pairs):
                q[p, here, :] = (rope(qf[:, p * LANES : (p + 1) * LANES], ct, st) * HD**-0.5).astype(BF16)
            kvf = dot(ain[...], wqkv[:, width:]) + bqkv[:, width:]
            is_key = lax.broadcasted_iota(jnp.int32, (SHARD, LANES), 1) < HD
            kv[here, :] = jnp.where(is_key, rope(kvf, ct, st), kvf).astype(BF16)
            hp[...] = dot(min_[...], wu[...])

            def act(r, carry):
                to = rows_of(r * 16, 16)
                v = hp[to, :] + bu_ref[...]
                cdf = 0.5 * (1.0 + lax.erf(v * (0.5**0.5)))
                pdf = jnp.exp(-0.5 * v * v) * (2.0 * jnp.pi) ** -0.5
                hid[slot, to, :] = (v * cdf).astype(BF16)
                dg[slot, to, :] = (cdf + v * pdf).astype(BF16)
                return carry

            lax.fori_loop(0, SHARD // 16, act, 0)
            outp[here, :] = dot(hid[slot], wd[...]).astype(BF16)

        def backward(c, slot):
            first = pl.multiple_of(c * SHARD, SHARD)
            here = pl.ds(first, SHARD)
            g = gm[here, :]
            dc = dot_t(g, wo[...]).astype(BF16)
            for p in range(pairs):
                dctx[p, here, :] = dc[:, p * LANES : (p + 1) * LANES]
            hp[...] = dot_t(g, wd[...])

            def back(r, carry):
                acc, gacc = carry
                to = rows_of(r * 16, 16)
                v = hp[to, :] * dg[slot, to, :].astype(F32)
                dpre[to, :] = v.astype(BF16)
                gv = gm[rows_of(first + r * 16, 16), :].astype(F32)
                return acc + v[:8] + v[8:], gacc + gv[:8] + gv[8:]

            acc, gacc = lax.fori_loop(0, SHARD // 16, back, (jnp.zeros((8, ff), F32), jnp.zeros((8, depth), F32)))
            gsum[:8, :] += gacc
            gsum[8:, :] += acc
            em[here, :] = (dot_t(dpre[...], wu[...]) * mg_ref[...]).astype(BF16)
            gup[...] += t_dot(xs[here, :], dpre[...])
            gdown[...] += t_dot(hid[slot], g)

        def step(s, carry):
            early = s < 4
            which = jnp.where(early, s // 2, 2 + s % 2)
            is_forward = jnp.where(early, s % 2 == 0, s < 6)
            shard = jnp.where(which == 0, m, jnp.where(which == 1, mate, jnp.where(which == 2, cross, far)))

            @pl.when(s == 0)
            def _():
                for c in local:
                    c.wait()

            @pl.when(s == 1)
            def _():
                for k in range(2):
                    @pl.when(valid(m, k))
                    def _():
                        local_g[k].wait()

            @pl.when(s == 2)
            def _():
                for k in range(2):
                    x_mate(mate, k).wait_recv()

            @pl.when(s == 3)
            def _():
                for k in range(2):
                    x_cross(cross, k).wait_recv()
                    x_pass(cross, k).start()
                for k in range(2):
                    @pl.when(valid(mate, k))
                    def _():
                        g_mate(mate, k).wait_recv()

            @pl.when(s == 5)
            def _():
                for k in range(2):
                    x_pass(far, k).wait_recv()

            @pl.when(s == 4)
            def _():
                for k in range(2):
                    x_pass(cross, k).wait_send()

            @pl.when(s == 6)
            def _():
                for k in range(2):
                    @pl.when(valid(cross, k))
                    def _():
                        g_cross(cross, k).wait_recv()
                        g_pass(cross, k).start()

            @pl.when(s == 7)
            def _():
                for k in range(2):
                    @pl.when(valid(far, k))
                    def _():
                        g_pass(far, k).wait_recv()

            @pl.when(is_forward)
            def _():
                forward(shard, which % 2)

            @pl.when(jnp.logical_not(is_forward))
            def _():
                backward(shard, which % 2)

            return carry

        lax.fori_loop(0, 8, step, 0)

    sh16 = pltpu.VMEM((SHARD, depth), BF16)
    pl.run_scoped(
        feed_forward, sh16, sh16, pltpu.VMEM((SHARD, ff), F32), pltpu.VMEM((2, SHARD, ff), BF16), pltpu.VMEM((2, SHARD, ff), BF16),
        pltpu.VMEM((SHARD, ff), BF16),
    )
    for k in range(2):
        x_cross(m, k).wait_send()
        x_mate(m, k).wait_send()

        @pl.when(valid(m, k))
        def _():
            g_cross(m, k).wait_send()
            g_mate(m, k).wait_send()

        @pl.when(valid(cross, k))
        def _():
            g_pass(cross, k).wait_send()

    gout[used : used + 8, :] = jnp.concatenate(
        [jnp.sum(gsum[:8, :], axis=0, keepdims=True), jnp.sum(gsum[8:, :], axis=0, keepdims=True), jnp.zeros((6, depth), F32)], axis=0
    )
    ring = lambda n, *refs: Ring(*refs, rr.at[n], rs_.at[n], place, right, left)
    ring_d = ring(0, gdown, st_d, sl_d, f_d)
    ring_u = ring(1, gup, st_u, sl_u, f_u)
    ring_o = ring(2, gout, st_o, sl_o, f_o)
    ring_q = ring(3, gqkv, st_q, sl_q, f_q)
    scat_o = Scatter(outp, mo, co, so_s, so_r, m, mate, cross)
    scat_e = Scatter(em, me_, ce, se_s, se_r, m, mate, cross)
    ends = doc_ends(doc_ref)
    lane = lax.broadcasted_iota(jnp.int32, (BLK, LANES), 1)
    low = lane < HD
    fwd_steps = NBLK * heads
    bwd_steps = PADBLK * heads
    steps = fwd_steps + bwd_steps

    def attention(kx, vx, probs, scores, total):
        for b in range(NBLK):
            at = pl.ds(b * BLK, BLK)
            v = kv[at, :].astype(F32)
            t = pltpu.roll(v, HD, 1)
            kx[at, :] = jnp.where(low, v, t).astype(BF16)
            vx[at, :LANES] = jnp.where(low, t, v).astype(BF16)
            vx[at, LANES:] = jnp.ones((BLK, LANES), BF16)
        dk[...] = jnp.zeros_like(dk)
        dv[...] = jnp.zeros_like(dv)

        def head_lanes(ref, p, at, side):
            return jnp.where(lane // HD == side, ref[p, at, :].astype(F32), 0.0).astype(BF16)

        def forward(i, h):
            at = pl.ds(i * BLK, BLK)
            blocks = key_blocks(i)
            slot = i * BLK + lax.broadcasted_iota(jnp.int32, (BLK, 1), 0)
            begin = doc_begin(slot, ends)
            qb = head_lanes(q, h // 2, at, h % 2)
            peak = jnp.full((BLK, BLK), -1e30, F32)
            for n, j in enumerate(blocks):
                s = dot_t(qb, kx[pl.ds(j * BLK, BLK), :])
                key = j * BLK + lax.broadcasted_iota(jnp.int32, (BLK, BLK), 1)
                ok = key >= begin
                if i == j:
                    ok = ok & (key <= slot)
                s = jnp.where(ok, s, -1e30)
                scores[:, n * BLK : (n + 1) * BLK] = s
                peak = jnp.maximum(peak, s)
            top = jnp.max(peak, axis=-1, keepdims=True)
            acc = jnp.zeros((BLK, 2 * LANES), F32)
            for n, j in enumerate(blocks):
                e = jnp.exp(scores[:, n * BLK : (n + 1) * BLK] - top).astype(BF16)
                probs[h, SLOTS[(i, j)]] = e
                acc = acc + dot(e, vx[pl.ds(j * BLK, BLK), :])
            total[h] = acc

            @pl.when(h == heads - 1)
            def _():
                extra = jnp.zeros((BLK, LANES), F32)
                context = []
                for p in range(pairs):
                    full = 2 * p + 1 < heads
                    norm = jnp.where(low, total[2 * p, :, LANES:], total[2 * p + 1, :, LANES:] if full else 1.0)
                    c = jnp.where(low, total[2 * p, :, :LANES], total[2 * p + 1, :, :LANES] if full else 0.0)
                    norm = 1.0 / norm
                    c = c * norm
                    context.append(c.astype(BF16))
                    ctx[at, p * LANES : (p + 1) * LANES] = context[p]
                    if i < PADBLK:
                        dcs = (dctx[p, at, :].astype(F32) * norm).astype(BF16)
                        dctx[p, at, :] = dcs
                        prod = dcs.astype(F32) * c
                        for side in range(2 if full else 1):
                            first = 2 * (2 * p + side)
                            r = -jnp.sum(jnp.where(low if side == 0 else ~low, prod, 0.0), axis=-1, keepdims=True)
                            r_top = r.astype(BF16).astype(F32)
                            extra = jnp.where(lane == first, r_top, jnp.where(lane == first + 1, r - r_top, extra))
                if i < PADBLK:
                    dd[at, :] = extra.astype(BF16)
                outp[at, :] = (dot(jnp.concatenate(context, axis=1), wo[...]) + outp[at, :].astype(F32)).astype(BF16)
                scat_o.offer(i)
                if i > 0:
                    scat_o.collect(i - 1)

        def backward(i, h):
            at = pl.ds(i * BLK, BLK)
            dc = head_lanes(dctx, h // 2, at, h % 2)
            rest = jnp.where(lane // 2 == h, dd[at, :].astype(F32), 0.0).astype(BF16)
            lhs = jnp.concatenate([dc, rest], axis=1)
            qb = head_lanes(q, h // 2, at, h % 2)
            acc = jnp.zeros((BLK, LANES), F32)
            for j in key_blocks(i):
                jat = pl.ds(j * BLK, BLK)
                e = probs[h, SLOTS[(i, j)]]
                ds = (e.astype(F32) * dot_t(lhs, vx[jat, :])).astype(BF16)
                acc = acc + dot(ds, kx[jat, :])
                dk[jat, :] += t_dot(ds, qb)
                dv[jat, :] += t_dot(e, dc)
            dqh[h] = acc

            @pl.when(h == heads - 1)
            def _():
                ct, st = cos[at, :], sine[at, :]
                for p in range(pairs):
                    full = 2 * p + 1 < heads
                    v = jnp.where(low, dqh[2 * p], dqh[2 * p + 1] if full else 0.0)
                    dqkv[at, p * LANES : (p + 1) * LANES] = (unrope(v, ct, st) * HD**-0.5).astype(BF16)
                keys = dk[at, :]
                values = dv[at, :]
                keys = keys + pltpu.roll(keys, HD, 1)
                values = values + pltpu.roll(values, HD, 1)
                dqkv[at, width:] = jnp.where(low, unrope(keys, ct, st), values).astype(BF16)
                em[at, :] = (dot_t(dqkv[at, :], wqkv[...]) * ag_ref[...] + em[at, :].astype(F32)).astype(BF16)
                scat_e.offer(i)
                if i < PADBLK - 1:
                    scat_e.collect(i + 1)

        def events(r, t, begin, count):
            lo = jnp.maximum(t - begin, 0) * EVENTS // count
            hi = jnp.minimum(jnp.maximum(t + 1 - begin, 0) * EVENTS // count, EVENTS)

            @pl.when(lo < hi)
            def _():
                r.event(lo)

        def step(t, carry):
            events(ring_d, t, 0, steps)
            events(ring_u, t, -1, steps)

            @pl.when(t < fwd_steps)
            def _():
                lax.switch(t // heads, [partial(forward, i) for i in range(NBLK)], t % heads)

            @pl.when(t == fwd_steps)
            def _():
                scat_o.collect(NBLK - 1)
                gout[:used, :] = t_dot(ctx[...], gm[...])[:used, :]

            @pl.when(t >= fwd_steps)
            def _():
                events(ring_o, t, fwd_steps + 1, EVENTS)
                lax.switch((t - fwd_steps) // heads, [partial(backward, i) for i in reversed(range(PADBLK))], (t - fwd_steps) % heads)

            return carry

        lax.fori_loop(0, steps, step, 0)

    pl.run_scoped(
        attention, pltpu.VMEM((SLOT, LANES), BF16), pltpu.VMEM((SLOT, 2 * LANES), BF16), pltpu.VMEM((heads, NSLOT, BLK, BLK), BF16),
        pltpu.VMEM((BLK, (BAND + 1) * BLK), F32), pltpu.VMEM((heads, BLK, 2 * LANES), F32),
    )

    out_down = pltpu.make_async_copy(f_d, fdown_hbm, loc.at[0])
    out_up = pltpu.make_async_copy(f_u, fup_hbm, loc.at[1])
    out_out = pltpu.make_async_copy(f_o, fout_hbm, loc.at[2])
    out_down.start()
    out_up.start()
    out_out.start()
    scat_e.collect(0)
    grads = t_dot(xs[:VALID, :], dqkv[:VALID, :])
    gqkv[...] = grads
    sums = jnp.sum(dqkv[:VALID, :].astype(F32), axis=0, keepdims=True)
    for piece in range((width + LANES) // HD):
        part = sums[:, piece // 2 * LANES : piece // 2 * LANES + LANES]
        part = jnp.broadcast_to(part, (8, LANES))
        if piece % 2 == 0:
            part = pltpu.roll(part, HD, 1)
        gqkv[piece * 8 : piece * 8 + 8, used:width] = part[:, HD:]
    ring_q.event(0)

    for k in range(2):
        scat_o.arrived(k)

        def finish_out(r, carry):
            at = pl.multiple_of(r * 32, 32)
            v = own_x[rows_of(k * BLK + at, 32), :].astype(F32) + scat_o.total(k, at) + ob_ref[...]
            io[rows_of(k * BLK + at, 32), :] = v.astype(BF16)
            return carry

        lax.fori_loop(0, BLK // 32, finish_out, 0)
    out_block = pltpu.make_async_copy(io, bout_hbm, loc.at[3])
    out_block.start()

    def tail(e, carry):
        ring_q.event(e)
        return carry

    lax.fori_loop(1, EVENTS, tail, 0)
    out_block.wait()
    for k in range(2):
        @pl.when(valid(m, k))
        def _():
            scat_e.arrived(k)

            def finish_in(r, carry):
                at = pl.multiple_of(r * 32, 32)
                v = own_x[rows_of(k * BLK + at, 32), :].astype(F32)
                v = v - jnp.mean(v, axis=-1, keepdims=True)
                inv = lax.rsqrt(jnp.mean(v * v, axis=-1, keepdims=True) + EPS)
                v = v * inv
                e = scat_e.total(k, at)
                e = inv * (e - jnp.mean(e, axis=-1, keepdims=True) - v * jnp.mean(e * v, axis=-1, keepdims=True))
                g = gm[rows_of((2 * m + k) * BLK + at, 32), :].astype(F32)
                io[rows_of(k * BLK + at, 32), :] = (e + g).astype(BF16)
                return carry

            lax.fori_loop(0, BLK // 32, finish_in, 0)

        @pl.when(jnp.logical_not(valid(m, k)))
        def _():
            io[pl.ds(k * BLK, BLK), :] = jnp.zeros((BLK, depth), BF16)
    out_in = pltpu.make_async_copy(io, ingrad_hbm, loc.at[4])
    out_in.start()
    out_q = pltpu.make_async_copy(f_q, fqkv_hbm, loc.at[3])
    out_q.start()

    ones = jnp.ones((8, 2 * LANES), BF16)

    def row_sums(weight, grad, n):
        acc = jnp.zeros((8, depth), F32)
        for c in range(0, n, LANES):
            for part in top_and_rest(weight[:, c : c + LANES].astype(F32) * grad[:, c : c + LANES].astype(F32)):
                acc = acc + dot_t(ones[:, :LANES], part)
        return acc[:1]

    def times(vector, weight):
        acc = jnp.zeros((8, depth), F32)
        for part in top_and_rest(jnp.broadcast_to(vector, (8, vector.shape[1]))):
            acc = acc + dot_t(part, weight[...])
        return acc[:1]

    lane_row = lax.broadcasted_iota(jnp.int32, (1, LANES), 1)
    biases = []
    for c in range((width + LANES) // LANES):
        a = f_q[16 * c : 16 * c + 16, width - LANES : width].astype(F32)
        first, second = pltpu.roll(a[:8], HD, 1)[:1], a[8:9]
        biases.append(jnp.where(lane_row < HD, first, second))
    up_bias = f_o[used : used + 16, :].astype(F32)[1:2]
    vecx[0] = jnp.concatenate(
        [
            row_sums(wqkv, f_q, width + LANES),
            times(jnp.concatenate(biases, axis=1), wqkv),
            row_sums(wu, f_u, ff),
            times(up_bias, wu),
            jnp.concatenate([biases[-1], jnp.zeros((1, depth - LANES), F32)], axis=1),
            jnp.zeros((3, depth), F32),
        ],
        axis=0,
    )
    kvx[0] = f_q[:, width:]

    def swap(stage, to):
        def one(ref, index):
            return pltpu.make_async_remote_copy(
                src_ref=ref.at[2 * stage], dst_ref=ref.at[2 * stage + 1], send_sem=bf_s.at[index], recv_sem=bf_r.at[index],
                device_id={"mp": to}, device_id_type=MESH,
            )

        return one(kvx, 2 * stage), one(vecx, 2 * stage + 1)

    for stage, to in ((0, mate), (1, cross)):
        both = swap(stage, to)
        for c in both:
            c.start()
        for c in both:
            c.wait()
        a, b = 2 * stage, 2 * stage + 1
        kv_sum = kvx[a].astype(F32) + kvx[b].astype(F32)
        vec_sum = vecx[a] + vecx[b]
        if stage == 0:
            kvx[2] = kv_sum.astype(BF16)
            vecx[2] = vec_sum
        else:
            kvg[...] = kv_sum
            vecx[4] = vec_sum
    finals = [pltpu.make_async_copy(kvg, kvg_hbm, loc.at[5]), pltpu.make_async_copy(vecx.at[4], vec_hbm, loc.at[6])]
    for c in finals:
        c.start()
    for b in range(NBLK):
        scat_o.drain(b)
        if b < PADBLK:
            scat_e.drain(b)
    for c in finals + [out_down, out_up, out_out, out_q, out_in]:
        c.wait()


VM = pl.BlockSpec(memory_space=pltpu.VMEM)
SM = pl.BlockSpec(memory_space=pltpu.SMEM)
ANY = pl.BlockSpec(memory_space=pl.ANY)


def run_layer(heads, doc, tokens, grads, small, wu, bu, wd):
    depth = tokens.shape[1]
    ff = wu.shape[1]
    pairs = (heads + 1) // 2
    width = pairs * LANES
    wide = width + LANES
    sh = jax.ShapeDtypeStruct
    vm = pltpu.VMEM
    dma = pltpu.SemaphoreType.DMA

    def ring_refs(rows, columns):
        half = rows // (2 * RING)
        return [vm((2, half, columns), BF16), vm((2, RING - 1, half, columns), BF16), vm((rows, columns), BF16)]

    scratch = [
        vm((SLOT, depth), BF16), vm((SLOT, depth), BF16), vm((SLOT, depth), BF16), vm((SLOT, depth), BF16),
        vm((ff, depth), F32), vm((depth, ff), F32), vm((width, depth), F32), vm((depth, wide), F32),
        vm((pairs, SLOT, LANES), BF16), vm((SLOT, LANES), BF16), vm((pairs, SLOT, LANES), BF16), vm((SLOT, LANES), BF16),
        vm((SLOT, LANES), F32), vm((SLOT, LANES), F32), vm((SLOT, width), BF16), vm((heads, BLK, LANES), F32),
        vm((SLOT, LANES), F32), vm((SLOT, LANES), F32), vm((SLOT, wide), BF16), vm((depth, wide), BF16), vm((width, depth), BF16),
        vm((depth, ff), BF16), vm((ff, depth), BF16), vm((1, wide), F32), vm((16, depth), F32),
        vm((SHARD, depth), BF16), vm((SHARD, depth), BF16),
        *ring_refs(ff, depth), *ring_refs(depth, ff), *ring_refs(width, depth), *ring_refs(depth, wide),
        vm((4, BLK, depth), BF16), vm((2, BLK, depth), BF16), vm((4, BLK, depth), BF16), vm((2, BLK, depth), BF16),
        vm((4, depth, LANES), BF16), vm((5, 8, depth), F32), vm((depth, LANES), F32),
        dma((8,)), dma((12,)), dma((12,)), dma((4, 2, EVENTS - 1)), dma((4, 2)), dma((6,)), dma((6,)), dma((6,)), dma((6,)),
        dma((4,)), dma((4,)),
    ]
    return pl.pallas_call(
        partial(layer_kernel, heads),
        out_shape=(
            sh((SHARD, depth), BF16), sh((SHARD, depth), BF16), sh((ff, depth), BF16), sh((depth, ff), BF16), sh((width, depth), BF16),
            sh((depth, wide), BF16), sh((depth, LANES), F32), sh((8, depth), F32),
        ),
        in_specs=[SM, ANY, ANY] + [VM] * 12 + [ANY, VM, ANY],
        out_specs=[ANY] * 8,
        scratch_shapes=scratch,
        compiler_params=pltpu.CompilerParams(vmem_limit_bytes=67043328, collective_id=0, has_side_effects=True),
        name="layer",
    )(doc, tokens, grads, *small, wu, bu, wd)


def per_device(
    ways,
    tokens, doc_lengths, attn_gain, attn_shift, query_weight, query_bias, key_weight, key_bias, value_weight, value_bias,
    out_weight, out_bias, mlp_gain, mlp_shift, up_weight, up_bias, down_weight, down_bias, out_grad,
):
    heads = query_weight.shape[1] // HD
    used = heads * HD
    pairs = (heads + 1) // 2
    width = pairs * LANES
    row = lambda v: v.reshape(1, -1)
    small = (
        row(attn_gain), row(attn_shift), query_weight, row(query_bias), key_weight, row(key_bias), value_weight, row(value_bias),
        out_weight, row(out_bias + down_bias), row(mlp_gain), row(mlp_shift),
    )
    block_out, input_grad, gdown, gup, gout, gqkv, gkv, vectors = run_layer(
        heads, doc_lengths, tokens, out_grad, small, up_weight, row(up_bias), down_weight
    )
    gdown, gup, gout, gqkv = (v.astype(F32) for v in (gdown, gup, gout, gqkv))
    if ways > RING:
        groups = [[i + RING * o for o in range(ways // RING)] for i in range(RING)]
        gdown, gup, gout, gqkv, gkv, vectors = lax.psum((gdown, gup, gout, gqkv, gkv, vectors), "dp", axis_index_groups=groups)
    biases = gqkv[: 8 * heads : 8, used:width].reshape(used)
    kv_bias = vectors[4, :LANES]
    g_sum, bup = gout[used], gout[used + 1]
    query_weight_grad = attn_gain[:, None] * gqkv[:, :used] + attn_shift[:, None] * biases
    kv_weight_grad = attn_gain[:, None] * gkv + attn_shift[:, None] * kv_bias
    up_weight_grad = mlp_gain[:, None] * gup + mlp_shift[:, None] * bup
    return (
        block_out, input_grad, vectors[0], vectors[1], query_weight_grad, biases, kv_weight_grad[:, :HD], kv_bias[:HD],
        kv_weight_grad[:, HD:], kv_bias[HD:], gout[:used], g_sum, vectors[2], vectors[3], up_weight_grad, bup, gdown, g_sum,
    )


def solution(mesh):
    rows = P(("dp", "mp"), None)
    placed = (
        rows, P("dp", None), P(), P(), P(None, "mp"), P("mp"), P(), P(), P(), P(), P("mp", None), P(), P(), P(),
        P(None, "mp"), P("mp"), P("mp", None), P(), rows,
    )
    outs = (
        rows, rows, P(), P(), P(None, "mp"), P("mp"), P(), P(), P(), P(), P("mp", None), P(), P(), P(),
        P(None, "mp"), P("mp"), P("mp", None), P(),
    )
    return jax.shard_map(partial(per_device, mesh.shape["dp"]), mesh=mesh, in_specs=placed, out_specs=outs, check_vma=False)
```

time: 451 us -> 226 us (0.50)
  waiting for transfers between devices: 252 us -> 0 us
  Pallas kernels: 105 us -> 195 us
  blocking collectives: 23.2 us -> 0 us
  matrix products: 14.8 us -> 0 us
  between operations: 14.5 us -> 0.75 us
  other arithmetic: 20.2 us -> 6.85 us
    psum x2 -> x0, waiting for transfers between devices: 121 us -> none  [the longest x1 105 us: per_device(): lax.psum((gqkv[:, :used].astype(BF16), gout.astype(BF16), gqkv[:, split:]...]
    pallas_call x2 -> x1, Pallas kernels: 105 us -> 195 us  [run_layer(): pl.pallas_call(partial(layer_kernel, heads), out_shape=(sh((SHARD, depth)...]
    reduce_scatter x2 -> x0, waiting for transfers between devices: 72.7 us -> none  [the longest x1 38.6 us: per_device(): lax.psum_scatter(branch.astype(BF16), 'mp', scatter_dimension=0, tiled=True)]
    all_gather x2 -> x0, waiting for transfers between devices: 56.8 us -> none  [the longest x1 30.1 us: per_device(): g_all = lax.all_gather(out_grad, 'mp', axis=0, tiled=True)]
    psum x1 -> x0, blocking collectives: 23.2 us -> none  [per_device(): vectors = lax.psum(jnp.concatenate([bqkv, g_sum, bup[0]]), 'dp')]
    dot_general x4 -> x0, matrix products: 14.8 us -> none  [the longest x1 5.53 us: dot_t(): lax.dot_general(a, b, (((1,), (1,)), ((), ())), preferred_element_type=F32)]
    reduce_sum x8 -> x0, other arithmetic: 10.6 us -> none  [the longest x1 3.78 us: per_device(): jnp.sum(bup * wu32, axis=1)]
    unnamed x72 -> x35, local copies, waits for them, and re-layouts: 11.1 us -> 10.4 us
  transfers between devices with their start and end apart: 6 -> 0, of which waited for: 6 -> 0; matrix products, arithmetic and copies ran while one was open for 7% -> 0% of each run, Pallas kernels for 0% -> 0%
where the time goes in v2:
time: 226 us; the launch traced here: 225 us
  Pallas kernels  195 us (86%)
  local copies, waits for them, and re-layouts  22.8 us (10%)
  other arithmetic  6.85 us (3%)
    pallas_call x1, Pallas kernels, run_layer(): pl.pallas_call(partial(layer_kernel, heads), out_shape=(sh((SHARD, depth)...  195 us
    unnamed x35, local copies, waits for them, and re-layouts  10.4 us
    reshape x6, local copies, waits for them, and re-layouts, per_device(): row = lambda v: v.reshape(1, -1)  6.92 us

profile of v2, /device:TPU:0, one launch (start us, length us, event | category | flops | bytes accessed | tf_op | source)
XLA Modules:
  0.0 225.2 jit_solution(1711509242907250251)
XLA Ops:
  0.7 1.3 reshape.71.ag_ref
  1.9 1.3 reshape.72.as_ref
  3.2 1.9 copy.37.wq_ref
  5.1 1.7 copy.38.wk_ref
  6.8 1.7 copy.39.wv_ref
  8.5 0.7 add.12
  9.2 0.6 reshape.76.ob_ref
  9.8 1.3 reshape.77.mg_ref
  11.0 1.3 reshape.78.ms_ref
  12.3 1.3 reshape.79.bu_ref
  13.6 194.8 %layer.1 = (bf16[512,768]{1,0:T(8,128)(2,1)}, bf16[512,768]{1,0:T(8,128)(2,1)}, bf16[768,768]{1,0:T(8,128)(2,1)}, bf16[768,768]{1,0:T(8,128)(2,1)}, bf16[256,768...) custom-call(s32[1,4]{1,0:T(1,128)} %doc_ref.1, bf16[512,768]{1,0:T(8,128)(2,1)} %tok_hbm.1, ...), custom_call_target="tpu_custom_call" | custom-call | tf_op jit(solution)/shard_map/layer/pallas_call | solution.py:823
  208.4 0.0 copy-start.6
  208.4 0.0 copy-start.7
  208.4 1.1 convert_element_type.13
  209.5 1.5 slice_reduce_fusion
  211.1 1.2 convert_element_type.12
  212.3 0.8 slice.53
  213.0 0.1 mul.72
  213.1 0.3 fusion
  213.4 1.1 copy.40
  214.5 0.7 slice_bitcast_fusion.2
  215.2 0.3 multiply_add_fusion.1
  215.4 0.2 fusion.1
  215.6 0.8 copy.41
  216.5 1.3 slice_bitcast_fusion
  217.8 0.8 copy.42
  218.6 0.9 slice.69
  219.5 1.8 multiply_add_fusion
  221.3 1.6 convert_element_type.15
  222.9 0.6 copy.46
  223.5 0.9 copy.47
  224.3 0.9 copy.48
  (24 shorter events, 0.0 us)
Async XLA Ops:
  208.4 4.7 %copy-start.6 = (f32[768]{0:T(1024)S(1)}, f32[768]{0:T(1024)}, u32[]{:S(2)}) copy-start(f32[768]{0:T(1024)} %param.21) | copy-start | bytes 9220
  208.4 4.7 %copy-start.7 = (f32[768]{0:T(1024)S(1)}, f32[768]{0:T(1024)}, u32[]{:S(2)}) copy-start(f32[768]{0:T(1024)} %param.22) | copy-start | bytes 9220
  211.1 8.4 %copy-start.11 = (f32[768]{0:T(1024)}, f32[768]{0:T(1024)S(1)}, u32[]{:S(2)}) copy-start(f32[768]{0:T(1024)S(1)} %get-tuple-element.135) | copy-start | bytes 9220
  211.1 11.8 %copy-start.8 = (f32[768]{0:T(1024)}, f32[768]{0:T(1024)S(1)}, u32[]{:S(2)}) copy-start(f32[768]{0:T(1024)S(1)} %get-tuple-element.131) | copy-start | bytes 9220
  211.1 4.1 %copy-start.5 = (f32[768,128]{1,0:T(8,128)S(1)}, f32[768,128]{1,0:T(8,128)}, u32[]{:S(2)}) copy-start(f32[768,128]{1,0:T(8,128)} %get-tuple-element.30) | copy-start | bytes 1179652
  213.1 2.5 %copy-start.12 = (f32[192]{0:T(256)}, f32[192]{0:T(256)S(1)}, u32[]{:S(2)}) copy-start(f32[192]{0:T(256)S(1)} %mul.72) | copy-start | bytes 2308
  213.4 5.2 %copy-start = (bf16[256,768]{1,0:T(8,128)(2,1)S(1)}, bf16[256,768]{1,0:T(8,128)(2,1)}, u32[]{:S(2)}) copy-start(bf16[256,768]{1,0:T(8,128)(2,1)} %get-tuple-element.31) | copy-start | bytes 1179652
  215.2 4.3 %copy-start.2 = (bf16[768,768]{1,0:T(8,128)(2,1)S(1)}, bf16[768,768]{1,0:T(8,128)(2,1)}, u32[]{:S(2)}) copy-start(bf16[768,768]{1,0:T(8,128)(2,1)} %get-tuple-element.32) | copy-start | bytes 3538948
  215.2 4.3 %copy-start.9 = (f32[768]{0:T(1024)S(1)}, f32[768]{0:T(1024)}, u32[]{:S(2)}) copy-start(f32[768]{0:T(1024)} %param.31) | copy-start | bytes 9220
  215.2 4.3 %copy-start.10 = (f32[768]{0:T(1024)S(1)}, f32[768]{0:T(1024)}, u32[]{:S(2)}) copy-start(f32[768]{0:T(1024)} %param.32) | copy-start | bytes 9220
  218.6 2.7 %copy-start.1 = (bf16[768,768]{1,0:T(8,128)(2,1)S(1)}, bf16[768,768]{1,0:T(8,128)(2,1)}, u32[]{:S(2)}) copy-start(bf16[768,768]{1,0:T(8,128)(2,1)} %get-tuple-element.33) | copy-start | bytes 3538948
  221.3 2.2 copy-start.4
  221.3 3.1 %copy-start.3 = (bf16[512,768]{1,0:T(8,128)(2,1)S(1)}, bf16[512,768]{1,0:T(8,128)(2,1)}, u32[]{:S(2)}) copy-start(bf16[512,768]{1,0:T(8,128)(2,1)} %get-tuple-element.121) | copy-start | bytes 2359300

commit v3 on v2

v3 whole, which is shorter than its diff:
```python
from functools import partial

import jax
import jax.numpy as jnp
from jax import lax
from jax.experimental import pallas as pl
from jax.experimental.pallas import tpu as pltpu
from jax.sharding import PartitionSpec as P

HD = 64
ROT = 16
HALF = ROT // 2
SLOT = 2048
VALID = 1792
LONGEST = 1024
DOCS = 4
BIG = 1e30
EPS = 1e-05
BLK = 256
NBLK = SLOT // BLK
BAND = LONGEST // BLK
PADBLK = VALID // BLK
LANES = 128
MP = 4
SHARD = SLOT // MP
RING = 8
EVENTS = RING + 1
F32 = jnp.float32
BF16 = jnp.bfloat16
MESH = pl.DeviceIdType.MESH


def dot(a, b):
    return lax.dot_general(a, b, (((1,), (0,)), ((), ())), preferred_element_type=F32)


def dot_t(a, b):
    return lax.dot_general(a, b, (((1,), (1,)), ((), ())), preferred_element_type=F32)


def t_dot(a, b):
    return lax.dot_general(a, b, (((0,), (0,)), ((), ())), preferred_element_type=F32)


def key_blocks(i):
    if i >= PADBLK:
        return list(range(PADBLK, i + 1))
    return list(range(max(0, i - BAND), i + 1))


SLOTS = {}
for _i in range(NBLK):
    for _j in key_blocks(_i):
        SLOTS[(_i, _j)] = len(SLOTS)
NSLOT = len(SLOTS)
KV_ROW, Q_ROW = 256, 384


def doc_begin(slot, ends):
    begin = jnp.zeros_like(slot)
    for end in ends:
        begin = jnp.where(slot >= end, end, begin)
    return begin


def doc_ends(doc_ref):
    ends = []
    total = 0
    for d in range(DOCS):
        total = total + doc_ref[0, d]
        ends.append(total)
    return ends


def build_tables(doc_ref, cos_ref, sine_ref):
    ends = doc_ends(doc_ref)
    slot = lax.broadcasted_iota(jnp.int32, (HALF, SLOT), 1)
    freq_index = lax.broadcasted_iota(jnp.int32, (HALF, SLOT), 0)
    position = (slot - doc_begin(slot, ends)).astype(F32)
    freq = jnp.zeros((HALF, SLOT), F32)
    for i in range(HALF):
        freq = jnp.where(freq_index == i, 10000.0 ** (-(2.0 * i) / ROT), freq)
    angle = position * freq
    lane = lax.broadcasted_iota(jnp.int32, (3 * HALF, LANES), 1) % HD
    row = lax.broadcasted_iota(jnp.int32, (3 * HALF, LANES), 0) % HALF
    low = jnp.where(lane == row, 1.0, 0.0)
    high = jnp.where(lane == row + HALF, 1.0, 0.0)
    rest = lax.broadcasted_iota(jnp.int32, (SLOT, LANES), 1) % HD >= ROT

    def parts(v):
        a = v.astype(BF16)
        r = v - a.astype(F32)
        b = r.astype(BF16)
        c = (r - b.astype(F32)).astype(BF16)
        return jnp.concatenate([a, b, c], axis=0)

    cos_ref[...] = jnp.where(rest, 1.0, t_dot(parts(jnp.cos(angle)), (low + high).astype(BF16)))
    sine_ref[...] = t_dot(parts(jnp.sin(angle)), (high - low).astype(BF16))


def partner(v):
    lane = lax.broadcasted_iota(jnp.int32, v.shape, 1) % HD
    return jnp.where(lane < HALF, pltpu.roll(v, LANES - HALF, 1), pltpu.roll(v, HALF, 1))


def rope(v, cos, sine):
    return v * cos + partner(v) * sine


def unrope(v, cos, sine):
    return v * cos - partner(v) * sine


def top_and_rest(v):
    top = v.astype(BF16)
    return top, (v - top.astype(F32)).astype(BF16)


def rows_of(first, count):
    return pl.ds(pl.multiple_of(first, count), count)


class Rings:
    CHAINS = ((0, 4, 0), (1, 3, 0), (0, 3, 1), (1, 4, 1))

    def __init__(self, source, stage, slots, final, recv, send, place, right, left):
        self.source, self.stage, self.slots, self.final = source, stage, slots, final
        self.recv, self.send, self.place = recv, send, place
        self.to = (right, left)
        self.rows, self.lanes = stage.shape[2], stage.shape[3]

    def copy(self, r, chain, src, dst, step):
        return pltpu.make_async_remote_copy(
            src_ref=src, dst_ref=dst, send_sem=self.send.at[r, chain], recv_sem=self.recv.at[r, chain, step],
            device_id={"dp": self.to[self.CHAINS[chain][0]]}, device_id_type=MESH,
        )

    def at(self, r, ahead):
        chunk = lax.rem(self.place + 2 * RING + ahead, RING)
        return rows_of((r * RING + chunk) * self.rows, self.rows)

    def event(self, r, e):
        stage, slots, source, final = self.stage, self.slots, self.source, self.final
        for chain, (left, hops, side) in enumerate(self.CHAINS):
            sign = -1 if left else 1
            lanes = pl.ds(side * self.lanes, self.lanes)
            own = self.at(r, sign * (hops - e))

            @pl.when(e == 0)
            def _():
                stage[r, chain] = source[own, lanes].astype(BF16)
                self.copy(r, chain, stage.at[r, chain], slots.at[r, chain, 0], 0).start()

            @pl.when((e >= 1) & (e < hops))
            def _():
                got = slots.at[r, chain, e - 1]
                self.copy(r, chain, stage.at[r, chain], got, e - 1).wait_recv()
                slots[r, chain, e - 1] = (slots[r, chain, e - 1].astype(F32) + source[own, lanes]).astype(BF16)
                self.copy(r, chain, stage.at[r, chain], got, e - 1).wait_send()
                self.copy(r, chain, got, slots.at[r, chain, e], e).start()

        @pl.when(e == 4)
        def _():
            self.settle(r)
            self.release(r)

        for chain, (left, hops, side) in enumerate(self.CHAINS):
            sign = -1 if left else 1
            here = final.at[self.at(r, sign * (4 - e)), pl.ds(side * self.lanes, self.lanes)]

            @pl.when((e > 4) & (e <= 4 + hops))
            def _():
                self.copy(r, chain, stage.at[r, chain], here, e - 1).wait_recv()
                self.copy(r, chain, here, here, e - 1).wait_send()

            @pl.when((e > 4) & (e < 4 + hops))
            def _():
                self.copy(r, chain, here, here, e).start()

    def settle(self, r):
        for chain, (left, hops, side) in enumerate(self.CHAINS):
            got = self.slots.at[r, chain, hops - 1]
            self.copy(r, chain, self.stage.at[r, chain], got, hops - 1).wait_recv()
            self.copy(r, chain, self.stage.at[r, chain], got, hops - 1).wait_send()
        mine = self.at(r, 0)
        for side in range(2):
            lanes = pl.ds(side * self.lanes, self.lanes)
            pair = [self.slots[r, c, self.CHAINS[c][1] - 1].astype(F32) for c in (2 * side, 2 * side + 1)]
            self.final[mine, lanes] = (self.source[mine, lanes] + pair[0] + pair[1]).astype(BF16)

    def release(self, r):
        for chain, (left, hops, side) in enumerate(self.CHAINS):
            here = self.final.at[self.at(r, 0), pl.ds(side * self.lanes, self.lanes)]
            self.copy(r, chain, here, here, 4).start()


class Scatter:
    def __init__(self, part, mate_in, cross_in, send, recv, m, mate, cross):
        self.part, self.mate_in, self.cross_in, self.send, self.recv = part, mate_in, cross_in, send, recv
        self.m, self.mate, self.cross = m, mate, cross

    def copy(self, src, dst, index, to):
        return pltpu.make_async_remote_copy(
            src_ref=src, dst_ref=dst, send_sem=self.send.at[index], recv_sem=self.recv.at[index],
            device_id={"mp": to}, device_id_type=MESH,
        )

    def to_mate(self, b):
        index = (b // 4) * 2 + b % 2
        return self.copy(self.part.at[pl.ds(b * BLK, BLK), :], self.mate_in.at[index], index, self.mate)

    def to_cross(self, b):
        index = (b // 4) * 2 + b % 2
        return self.copy(self.mate_in.at[index], self.cross_in.at[b % 2], 4 + b % 2, self.cross)

    def mine(self, b):
        return self.m % 2 == (b // 2) % 2

    def offer(self, b):
        @pl.when(jnp.logical_not(self.mine(b)))
        def _():
            self.to_mate(b).start()

    def collect(self, b):
        index = (b // 4) * 2 + b % 2

        @pl.when(self.mine(b))
        def _():
            self.to_mate(b).wait_recv()

            @pl.when(self.m // 2 != b // 4)
            def _():
                def add(r, carry):
                    at = rows_of(r * 32, 32)
                    own = self.part[rows_of(b * BLK + r * 32, 32), :].astype(F32)
                    self.mate_in[index, at, :] = (self.mate_in[index, at, :].astype(F32) + own).astype(BF16)
                    return carry

                lax.fori_loop(0, BLK // 32, add, 0)
                self.to_cross(b).start()

    def total(self, k, at):
        own = self.part[rows_of((2 * self.m + k) * BLK + at, 32), :].astype(F32)
        index = (self.m // 2) * 2 + k
        return own + self.mate_in[index, rows_of(at, 32), :].astype(F32) + self.cross_in[k, rows_of(at, 32), :].astype(F32)

    def arrived(self, k):
        self.copy(self.mate_in.at[0], self.cross_in.at[k], 4 + k, self.cross).wait_recv()

    def drain(self, b):
        @pl.when(jnp.logical_not(self.mine(b)))
        def _():
            self.to_mate(b).wait_send()

        @pl.when(self.mine(b) & (self.m // 2 != b // 4))
        def _():
            self.to_cross(b).wait_send()


def layer_kernel(
    heads,
    doc_ref, tok_hbm, grad_hbm, ag_in, as_in, wq_ref, bq_in, wk_ref, bk_in, wv_ref, bv_in, wo_ref, ob_in, db_in, mg_in, ms_in,
    wu_hbm, bu_in, wd_hbm,
    bout_hbm, ingrad_hbm, fa_hbm, fb_hbm,
    xs, gm, outp, em, ga, gb, q, qt, kx, vx, dctx, dct, left_in, cos, sine, ctx, dqh, dkv, dqkv, wqkv, wo, wu, wd, bqkv, gsum, rows_in,
    own_x, io,
    st_a, sl_a, f_a, st_b, sl_b, f_b,
    mo, co, me_, ce, swap,
    loc, ag_send, ag_recv, ra_r, ra_s, rb_r, rb_s, so_s, so_r, se_s, se_r, bf_s, bf_r,
):
    pairs = (heads + 1) // 2
    width = pairs * LANES
    used = heads * HD
    depth = tok_hbm.shape[1]
    ff = wu.shape[1]
    misc = Q_ROW + used
    m = lax.axis_index("mp")
    d = lax.axis_index("dp")
    mate = m + 1 - 2 * (m % 2)
    cross = (m + 2) % MP
    far = (mate + 2) % MP
    inner, outer = d % RING, d // RING
    place = jnp.where(inner % 2 == 0, inner // 2, RING - 1 - inner // 2)

    def seat(p):
        return outer * RING + jnp.where(p < RING // 2, 2 * p, 2 * (RING - 1 - p) + 1)

    right, left = seat((place + 1) % RING), seat((place + RING - 1) % RING)
    rings_a = Rings(ga, st_a, sl_a, f_a, ra_r, ra_s, place, right, left)
    rings_b = Rings(gb, st_b, sl_b, f_b, rb_r, rb_s, place, right, left)

    local = [
        pltpu.make_async_copy(tok_hbm, xs.at[rows_of(m * SHARD, SHARD), :], loc.at[0]),
        pltpu.make_async_copy(wu_hbm, wu, loc.at[1]),
        pltpu.make_async_copy(wd_hbm, wd, loc.at[2]),
        pltpu.make_async_copy(tok_hbm, own_x, loc.at[3]),
    ]
    for c in local:
        c.start()
    local_g = [
        pltpu.make_async_copy(grad_hbm.at[pl.ds(k * BLK, BLK), :], gm.at[rows_of(m * SHARD + k * BLK, BLK), :], loc.at[4 + k])
        for k in range(2)
    ]

    def valid(shard, k):
        return 2 * shard + k < PADBLK

    for k in range(2):
        @pl.when(valid(m, k))
        def _():
            local_g[k].start()
    gm[VALID:, :] = jnp.zeros((SLOT - VALID, depth), BF16)

    barrier = pltpu.get_barrier_semaphore()
    for to in ({"mp": mate}, {"mp": cross}, {"dp": right}, {"dp": left}):
        pl.semaphore_signal(barrier, inc=1, device_id=to, device_id_type=MESH)
    pl.semaphore_wait(barrier, 4)

    def send(src, dst, index, to):
        return pltpu.make_async_remote_copy(
            src_ref=src, dst_ref=dst, send_sem=ag_send.at[index], recv_sem=ag_recv.at[index], device_id={"mp": to}, device_id_type=MESH
        )

    def half(ref, shard, k):
        return ref.at[rows_of(shard * SHARD + k * BLK, BLK), :]

    def x_cross(shard, k):
        return send(tok_hbm.at[pl.ds(k * BLK, BLK), :], half(xs, shard, k), k, cross)

    def x_mate(shard, k):
        return send(tok_hbm.at[pl.ds(k * BLK, BLK), :], half(xs, shard, k), 2 + k, mate)

    def g_cross(shard, k):
        return send(grad_hbm.at[pl.ds(k * BLK, BLK), :], half(gm, shard, k), 4 + k, cross)

    def g_mate(shard, k):
        return send(grad_hbm.at[pl.ds(k * BLK, BLK), :], half(gm, shard, k), 6 + k, mate)

    def x_pass(shard, k):
        return send(half(xs, shard, k), half(xs, shard, k), 8 + k, mate)

    def g_pass(shard, k):
        return send(half(gm, shard, k), half(gm, shard, k), 10 + k, mate)

    for k in range(2):
        x_cross(m, k).start()
    for k in range(2):
        x_mate(m, k).start()
    for k in range(2):
        @pl.when(valid(m, k))
        def _():
            g_mate(m, k).start()
    build_tables(doc_ref, cos, sine)
    for n, ref in enumerate((ag_in, as_in, mg_in, ms_in, bu_in)):
        rows_in[n : n + 1, :] = ref[...].reshape(1, depth)
    ag_row, as_row, mg_row, ms_row, bu_row = (rows_in.at[n : n + 1, :] for n in range(5))
    rows_in[5:6, :] = ob_in[...].reshape(1, depth) + db_in[...].reshape(1, depth)
    wqkv[:used, :] = wq_ref[...]
    bqkv[:, :used] = bq_in[...].reshape(1, used)
    wo[:used, :] = wo_ref[...]
    if used < width:
        wqkv[used:width, :] = jnp.zeros((width - used, depth), BF16)
        bqkv[:, used:width] = jnp.zeros((1, width - used), F32)
        wo[used:, :] = jnp.zeros((width - used, depth), BF16)
    wqkv[width : width + HD, :] = wk_ref[...]
    wqkv[width + HD :, :] = wv_ref[...]
    bqkv[:, width : width + HD] = bk_in[...].reshape(1, HD)
    bqkv[:, width + HD :] = bv_in[...].reshape(1, HD)
    ga[...] = jnp.zeros_like(ga)
    gb[...] = jnp.zeros_like(gb)
    gsum[...] = jnp.zeros_like(gsum)
    dqkv[VALID:, :] = jnp.zeros((SLOT - VALID, width + LANES), BF16)
    fwd_steps = NBLK * heads
    bwd_steps = PADBLK * heads
    steps = fwd_steps + bwd_steps
    lead = MP
    down_at, up_at = pl.ds(0, ff), pl.ds(ff, depth)

    def times(vector, weight, product):
        acc = jnp.zeros((8, depth), F32)
        for part in top_and_rest(jnp.broadcast_to(vector, (8, vector.shape[1]))):
            acc = acc + product(part, weight[...])
        return acc[:1]

    def early_rings(t):
        total = 4 * EVENTS
        hooks = lead + steps

        def one(n, carry):
            rings_a.event(n % 4, n // 4)
            return carry

        lax.fori_loop(t * total // hooks, (t + 1) * total // hooks, one, 0)

    def feed_forward(ain, min_, hp, hid, dg):
        def forward(c, which):
            half = which % 2
            first = pl.multiple_of(c * SHARD, SHARD)
            here = pl.ds(first, SHARD)

            def norm(r, carry):
                at = rows_of(first + r * 32, 32)
                to = rows_of(r * 32, 32)
                v = xs[at, :].astype(F32)
                v = v - jnp.mean(v, axis=-1, keepdims=True)
                v = v * lax.rsqrt(jnp.mean(v * v, axis=-1, keepdims=True) + EPS)
                xs[at, :] = v.astype(BF16)
                ain[to, :] = (v * ag_row[...] + as_row[...]).astype(BF16)
                min_[to, :] = (v * mg_row[...] + ms_row[...]).astype(BF16)
                return carry

            lax.fori_loop(0, SHARD // 32, norm, 0)
            ct, st = cos[here, :], sine[here, :]
            qf = dot_t(ain[...], wqkv[:width, :]) + bqkv[:, :width]
            slot = first + lax.broadcasted_iota(jnp.int32, (SHARD, LANES), 0)
            lane = lax.broadcasted_iota(jnp.int32, (SHARD, LANES), 1)
            low = lane < HD
            doc = jnp.zeros((SHARD, LANES), jnp.int32)
            for end in doc_ends(doc_ref):
                doc = jnp.where(slot >= end, doc + 1, doc)
            same = lane % HD == doc
            mark = jnp.where(same, -BIG, 0.0)
            for p in range(pairs):
                v = rope(qf[:, p * LANES : (p + 1) * LANES], ct, st) * HD**-0.5
                qt[p * LANES : (p + 1) * LANES, here] = jnp.transpose(v).astype(BF16)
                q[2 * p, here, :] = jnp.where(low, v, mark).astype(BF16)
                if 2 * p + 1 < heads:
                    q[2 * p + 1, here, :] = jnp.where(low, mark, v).astype(BF16)
            kvf = dot_t(ain[...], wqkv[width:, :]) + bqkv[:, width:]
            keys = rope(kvf, ct, st)
            other = jnp.where(same | (lane % HD > DOCS), 0.0, 1.0)
            kx[0, here, :] = jnp.where(low, keys, other).astype(BF16)
            kx[1, here, :] = jnp.where(low, other, pltpu.roll(keys, HD, 1)).astype(BF16)
            vx[0, here, :] = jnp.where(low, pltpu.roll(kvf, HD, 1), 1.0).astype(BF16)
            vx[1, here, :] = jnp.where(low, 1.0, kvf).astype(BF16)
            hp[...] = dot(min_[...], wu[...])

            def act(r, carry):
                to = rows_of(r * 16, 16)
                v = hp[to, :] + bu_row[...]
                cdf = 0.5 * (1.0 + lax.erf(v * (0.5**0.5)))
                pdf = jnp.exp(-0.5 * v * v) * (2.0 * jnp.pi) ** -0.5
                hid[half, to, :] = (v * cdf).astype(BF16)
                dg[which, to, :] = (cdf + v * pdf).astype(BF16)
                return carry

            lax.fori_loop(0, SHARD // 16, act, 0)
            outp[here, :] = dot(hid[half], wd[...]).astype(BF16)

        def backward(c, which):
            first = pl.multiple_of(c * SHARD, SHARD)
            here = pl.ds(first, SHARD)
            g = gm[here, :]
            hp[...] = dot_t(g, wd[...])

            def back(r, carry):
                acc, gacc = carry
                to = rows_of(r * 16, 16)
                v = hp[to, :] * dg[which, to, :].astype(F32)
                dg[which, to, :] = v.astype(BF16)
                gv = gm[rows_of(first + r * 16, 16), :].astype(F32)
                return acc + v[:8] + v[8:], gacc + gv[:8] + gv[8:]

            acc, gacc = lax.fori_loop(0, SHARD // 16, back, (jnp.zeros((8, ff), F32), jnp.zeros((8, depth), F32)))
            gsum[:8, :] += gacc
            gsum[8:, :] += acc
            ga[down_at, :] += t_dot(hid[which % 2], g)
            ga[up_at, :] += t_dot(xs[here, :], dg[which])

        def shard_of(which):
            return jnp.where(which == 0, m, jnp.where(which == 1, mate, jnp.where(which == 2, cross, far)))

        def after(which, hook):
            hook(0)
            here = rows_of(shard_of(which) * SHARD, SHARD)
            em[here, :] = (dot_t(dg[which], wu[...]) * mg_row[...]).astype(BF16)
            hook(1)
            dc = dot_t(gm[here, :], wo[...]).astype(BF16)
            for p in range(pairs):
                dctx[p, here, :] = dc[:, p * LANES : (p + 1) * LANES]

        def step(s, carry):
            early = s < 4
            which = jnp.where(early, s // 2, 2 + s % 2)
            is_forward = jnp.where(early, s % 2 == 0, s < 6)
            shard = shard_of(which)

            @pl.when(s == 0)
            def _():
                for c in local:
                    c.wait()

            @pl.when(s == 1)
            def _():
                for k in range(2):
                    @pl.when(valid(m, k))
                    def _():
                        local_g[k].wait()

            @pl.when(s == 2)
            def _():
                for k in range(2):
                    x_mate(mate, k).wait_recv()

            @pl.when(s == 3)
            def _():
                for k in range(2):
                    x_cross(m, k).wait_send()

                    @pl.when(valid(m, k))
                    def _():
                        g_cross(m, k).start()

                for k in range(2):
                    x_cross(cross, k).wait_recv()
                    x_pass(cross, k).start()
                for k in range(2):
                    @pl.when(valid(mate, k))
                    def _():
                        g_mate(mate, k).wait_recv()

            @pl.when(s == 5)
            def _():
                for k in range(2):
                    x_pass(far, k).wait_recv()

            @pl.when(s == 4)
            def _():
                for k in range(2):
                    x_pass(cross, k).wait_send()

            @pl.when(s == 6)
            def _():
                def ahead(which, carry):
                    after(which, lambda n: None)
                    return carry

                lax.fori_loop(0, 2, ahead, 0)
                for k in range(2):
                    @pl.when(valid(cross, k))
                    def _():
                        g_cross(cross, k).wait_recv()
                        g_pass(cross, k).start()

            @pl.when(s == 7)
            def _():
                for k in range(2):
                    @pl.when(valid(far, k))
                    def _():
                        g_pass(far, k).wait_recv()

            @pl.when(is_forward)
            def _():
                forward(shard, which)

            @pl.when(jnp.logical_not(is_forward))
            def _():
                backward(shard, which)

            return carry

        lax.fori_loop(0, 8, step, 0)
        up_bias = jnp.sum(gsum[8:, :], axis=0, keepdims=True)
        gb[used : used + 8, :] = jnp.concatenate(
            [jnp.sum(gsum[:8, :], axis=0, keepdims=True), up_bias, jnp.zeros((6, depth), F32)], axis=0
        )
        ones = jnp.ones((8, LANES), BF16)
        gain = jnp.zeros((8, depth), F32)
        for c in range(0, ff, LANES):
            for part in top_and_rest(wu[:, c : c + LANES].astype(F32) * ga[up_at, c : c + LANES]):
                gain = gain + dot_t(ones, part)
        gb[misc + 11 : misc + 12, :] = gain[:1]
        gb[misc + 12 : misc + 13, :] = times(up_bias, wu, dot_t)

        def behind(which, carry):
            after(which, lambda n: early_rings(2 * (which - 2) + n))
            return carry

        lax.fori_loop(2, MP, behind, 0)

    sh16 = pltpu.VMEM((SHARD, depth), BF16)
    pl.run_scoped(
        feed_forward, sh16, sh16, pltpu.VMEM((SHARD, ff), F32), pltpu.VMEM((2, SHARD, ff), BF16), pltpu.VMEM((MP, SHARD, ff), BF16),
    )
    for k in range(2):
        x_mate(m, k).wait_send()

        @pl.when(valid(m, k))
        def _():
            g_cross(m, k).wait_send()
            g_mate(m, k).wait_send()

        @pl.when(valid(cross, k))
        def _():
            g_pass(cross, k).wait_send()

    scat_o = Scatter(outp, mo, co, so_s, so_r, m, mate, cross)
    scat_e = Scatter(em, me_, ce, se_s, se_r, m, mate, cross)
    ends = doc_ends(doc_ref)
    lane = lax.broadcasted_iota(jnp.int32, (BLK, LANES), 1)
    low = lane < HD

    def attention(probs, scores, total):
        dkv[...] = jnp.zeros_like(dkv)
        causal = lax.broadcasted_iota(jnp.int32, (BLK, BLK), 1) <= lax.broadcasted_iota(jnp.int32, (BLK, BLK), 0)

        def forward(i, h):
            at = pl.ds(i * BLK, BLK)
            blocks = key_blocks(i)
            qb = q[h, at, :]
            half = h % 2
            peak = None
            for n, j in enumerate(blocks):
                s = dot_t(qb, kx[half, pl.ds(j * BLK, BLK), :])
                if i == j:
                    s = jnp.where(causal, s, -BIG)
                scores[:, n * BLK : (n + 1) * BLK] = s
                peak = s if peak is None else jnp.maximum(peak, s)
            top = jnp.max(peak, axis=-1, keepdims=True)
            acc = jnp.zeros((BLK, LANES), F32)
            for n, j in enumerate(blocks):
                e = jnp.exp(scores[:, n * BLK : (n + 1) * BLK] - top).astype(BF16)
                probs[h, SLOTS[(i, j)]] = e
                acc = acc + dot(e, vx[half, pl.ds(j * BLK, BLK), :])
            total[h] = acc

            @pl.when(h == heads - 1)
            def _():
                context = []
                for p in range(pairs):
                    full = 2 * p + 1 < heads
                    first, second = total[2 * p], total[2 * p + 1] if full else None
                    norm = jnp.where(low, pltpu.roll(first, HD, 1), pltpu.roll(second, HD, 1) if full else 1.0)
                    norm = 1.0 / norm
                    c = jnp.where(low, first, second if full else 0.0) * norm
                    context.append(c.astype(BF16))
                    ctx[at, p * LANES : (p + 1) * LANES] = context[p]
                    if i < PADBLK:
                        scaled = dctx[p, at, :].astype(F32) * norm
                        dcs = scaled.astype(BF16).astype(F32)
                        dct[p * LANES : (p + 1) * LANES, at] = jnp.transpose(dcs).astype(BF16)
                        prod = dcs * c
                        for side in range(2 if full else 1):
                            inside = low if side == 0 else ~low
                            r = -jnp.sum(jnp.where(inside, prod, 0.0), axis=-1, keepdims=True)
                            r_top = r.astype(BF16).astype(F32)
                            extra = jnp.where(lane % HD == 0, r_top, jnp.where(lane % HD == 1, r - r_top, 0.0))
                            left_in[2 * p + side, at, :] = jnp.where(inside, dcs, extra).astype(BF16)
                outp[at, :] = (dot(jnp.concatenate(context, axis=1), wo[...]) + outp[at, :].astype(F32)).astype(BF16)
                scat_o.offer(i)
                if i > 0:
                    scat_o.collect(i - 1)

        def backward(i, h):
            at = pl.ds(i * BLK, BLK)
            half = h % 2
            lhs = left_in[h, at, :]
            mine = rows_of(h * HD, HD)
            q_turned, d_turned = qt[mine, at], dct[mine, at]
            acc = jnp.zeros((BLK, LANES), F32)
            for j in key_blocks(i):
                jat = pl.ds(j * BLK, BLK)
                e = probs[h, SLOTS[(i, j)]]
                ds = (e.astype(F32) * dot_t(lhs, vx[half, jat, :])).astype(BF16)
                acc = acc + dot(ds, kx[half, jat, :])
                dkv[:HD, jat] += dot(q_turned, ds)
                dkv[HD:, jat] += dot(d_turned, e)
            dqh[h] = acc

            @pl.when(h == heads - 1)
            def _():
                ct, st = cos[at, :], sine[at, :]
                for p in range(pairs):
                    full = 2 * p + 1 < heads
                    v = jnp.where(low, dqh[2 * p], dqh[2 * p + 1] if full else 0.0)
                    dqkv[at, p * LANES : (p + 1) * LANES] = (unrope(v, ct, st) * HD**-0.5).astype(BF16)
                v = jnp.transpose(dkv[:, at])
                dqkv[at, width:] = jnp.where(low, unrope(v, ct, st), v).astype(BF16)
                em[at, :] = (dot(dqkv[at, :], wqkv[...]) * ag_row[...] + em[at, :].astype(F32)).astype(BF16)
                scat_e.offer(i)
                if i < PADBLK - 1:
                    scat_e.collect(i + 1)

        def out_rings(n):
            @pl.when(n < 2 * EVENTS)
            def _():
                rings_b.event(n % 2, n // 2)

        def step(t, carry):
            early_rings(lead + t)

            @pl.when(t < fwd_steps)
            def _():
                lax.switch(t // heads, [partial(forward, i) for i in range(NBLK)], t % heads)

            @pl.when(t == fwd_steps)
            def _():
                scat_o.collect(NBLK - 1)
                gb[:used, :] = t_dot(ctx[...], gm[...])[:used, :]

            @pl.when(t >= fwd_steps)
            def _():
                out_rings(t - fwd_steps)
                lax.switch((t - fwd_steps) // heads, [partial(backward, i) for i in reversed(range(PADBLK))], (t - fwd_steps) % heads)

            return carry

        lax.fori_loop(0, steps, step, 0)

    pl.run_scoped(
        attention, pltpu.VMEM((heads, NSLOT, BLK, BLK), BF16), pltpu.VMEM((BLK, (BAND + 1) * BLK), F32),
        pltpu.VMEM((heads, BLK, LANES), F32),
    )

    out_a = pltpu.make_async_copy(f_a, fa_hbm, loc.at[0])
    out_a.start()
    scat_e.collect(0)
    rows = VALID
    gb[KV_ROW : KV_ROW + LANES, :] = t_dot(dqkv[:rows, width:], xs[:rows, :])
    gb[Q_ROW:misc, :] = t_dot(dqkv[:rows, :width], xs[:rows, :])[:used, :]
    sums = jnp.sum(dqkv[:rows, :].astype(F32), axis=0, keepdims=True)
    gb[misc : misc + 1, : width + LANES] = sums
    gb[misc + 8 : misc + 9, :LANES] = sums[:, width:]
    gain = jnp.sum(wqkv[:used, :].astype(F32) * gb[Q_ROW:misc, :], axis=0, keepdims=True)
    gb[misc + 9 : misc + 10, :] = gain + jnp.sum(
        wqkv[width:, :].astype(F32) * gb[KV_ROW : KV_ROW + LANES, :], axis=0, keepdims=True
    )
    gb[misc + 10 : misc + 11, :] = times(sums, wqkv, dot)

    def tail(n, carry):
        rings_b.event(2 + n % 3, n // 3)
        return carry

    def advance(first, last):
        lax.fori_loop(3 * first, 3 * last, tail, 0)

    advance(0, 1)
    for k in range(2):
        scat_o.arrived(k)

        def finish_out(r, carry):
            at = pl.multiple_of(r * 32, 32)
            v = own_x[rows_of(k * BLK + at, 32), :].astype(F32) + scat_o.total(k, at) + rows_in[5:6, :]
            io[rows_of(k * BLK + at, 32), :] = v.astype(BF16)
            return carry

        lax.fori_loop(0, BLK // 32, finish_out, 0)
    out_block = pltpu.make_async_copy(io, bout_hbm, loc.at[1])
    out_block.start()
    advance(1, 4)

    rings_b.settle(2)
    rings_b.settle(4)
    swap[0, :16, :] = f_b[rings_b.at(2, 0), :]
    swap[0, 16:, :] = f_b[rings_b.at(4, 0), :]

    def exchange(stage, to):
        copy = pltpu.make_async_remote_copy(
            src_ref=swap.at[2 * stage], dst_ref=swap.at[2 * stage + 1], send_sem=bf_s.at[stage], recv_sem=bf_r.at[stage],
            device_id={"mp": to}, device_id_type=MESH,
        )
        copy.start()
        return copy

    copy = exchange(0, mate)
    rings_b.event(3, 4)
    copy.wait()
    swap[2] = (swap[0].astype(F32) + swap[1].astype(F32)).astype(BF16)
    exchange(1, cross).wait()
    both = swap[2].astype(F32) + swap[3].astype(F32)
    f_b[rings_b.at(2, 0), :] = both[:16].astype(BF16)
    last = lax.broadcasted_iota(jnp.int32, (16, depth), 0) >= jnp.where(place == used // 16 % RING, 8, 16)
    f_b[rings_b.at(4, 0), :] = jnp.where(last, both[16:], swap[0, 16:, :].astype(F32)).astype(BF16)
    rings_b.release(2)
    rings_b.release(4)
    advance(5, 6)
    for k in range(2):
        @pl.when(valid(m, k))
        def _():
            scat_e.arrived(k)

            def finish_in(r, carry):
                at = pl.multiple_of(r * 32, 32)
                v = own_x[rows_of(k * BLK + at, 32), :].astype(F32)
                v = v - jnp.mean(v, axis=-1, keepdims=True)
                inv = lax.rsqrt(jnp.mean(v * v, axis=-1, keepdims=True) + EPS)
                v = v * inv
                e = scat_e.total(k, at)
                e = inv * (e - jnp.mean(e, axis=-1, keepdims=True) - v * jnp.mean(e * v, axis=-1, keepdims=True))
                g = gm[rows_of((2 * m + k) * BLK + at, 32), :].astype(F32)
                own_x[rows_of(k * BLK + at, 32), :] = (e + g).astype(BF16)
                return carry

            lax.fori_loop(0, BLK // 32, finish_in, 0)

        @pl.when(jnp.logical_not(valid(m, k)))
        def _():
            own_x[pl.ds(k * BLK, BLK), :] = jnp.zeros((BLK, depth), BF16)
    out_in = pltpu.make_async_copy(own_x, ingrad_hbm, loc.at[2])
    out_in.start()
    advance(6, EVENTS)
    out_b = pltpu.make_async_copy(f_b, fb_hbm, loc.at[3])
    out_b.start()

    for b in range(NBLK):
        scat_o.drain(b)
        if b < PADBLK:
            scat_e.drain(b)
    for c in (out_a, out_b, out_block, out_in):
        c.wait()


VM = pl.BlockSpec(memory_space=pltpu.VMEM)
SM = pl.BlockSpec(memory_space=pltpu.SMEM)
ANY = pl.BlockSpec(memory_space=pl.ANY)


def run_layer(heads, doc, tokens, grads, small, wu, bu, wd):
    depth = tokens.shape[1]
    ff = wu.shape[1]
    pairs = (heads + 1) // 2
    width = pairs * LANES
    wide = width + LANES
    sh = jax.ShapeDtypeStruct
    vm = pltpu.VMEM
    dma = pltpu.SemaphoreType.DMA
    a_rows, b_rows = ff + depth, KV_ROW + 384

    def ring_refs(rows, count):
        chunk = rows // (count * RING)
        return [vm((count, 4, chunk, depth // 2), BF16), vm((count, 4, 4, chunk, depth // 2), BF16), vm((rows, depth), BF16)]

    scratch = [
        vm((SLOT, depth), BF16), vm((SLOT, depth), BF16), vm((SLOT, depth), BF16), vm((SLOT, depth), BF16),
        vm((a_rows, depth), F32), vm((b_rows, depth), F32),
        vm((heads, SLOT, LANES), BF16), vm((width, SLOT), BF16), vm((2, SLOT, LANES), BF16), vm((2, SLOT, LANES), BF16),
        vm((pairs, SLOT, LANES), BF16), vm((width, VALID), BF16), vm((heads, VALID, LANES), BF16),
        vm((SLOT, LANES), F32), vm((SLOT, LANES), F32), vm((SLOT, width), BF16), vm((heads, BLK, LANES), F32),
        vm((LANES, VALID), F32), vm((SLOT, wide), BF16), vm((wide, depth), BF16), vm((width, depth), BF16),
        vm((depth, ff), BF16), vm((ff, depth), BF16), vm((1, wide), F32), vm((16, depth), F32), vm((8, depth), F32),
        vm((SHARD, depth), BF16), vm((SHARD, depth), BF16),
        *ring_refs(a_rows, 4), *ring_refs(b_rows, 5),
        vm((4, BLK, depth), BF16), vm((2, BLK, depth), BF16), vm((4, BLK, depth), BF16), vm((2, BLK, depth), BF16),
        vm((4, 32, depth), BF16),
        dma((8,)), dma((12,)), dma((12,)), dma((4, 4, 8)), dma((4, 4)), dma((5, 4, 8)), dma((5, 4)),
        dma((6,)), dma((6,)), dma((6,)), dma((6,)), dma((2,)), dma((2,)),
    ]
    return pl.pallas_call(
        partial(layer_kernel, heads),
        out_shape=(
            sh((SHARD, depth), BF16), sh((SHARD, depth), BF16), sh((a_rows, depth), BF16), sh((b_rows, depth), BF16),
        ),
        in_specs=[SM, ANY, ANY] + [VM] * 13 + [ANY, VM, ANY],
        out_specs=[ANY] * 4,
        scratch_shapes=scratch,
        compiler_params=pltpu.CompilerParams(vmem_limit_bytes=67043328, collective_id=0, has_side_effects=True),
        name="layer",
    )(doc, tokens, grads, *small, wu, bu, wd)


def final_kernel(
    heads, ff,
    bout_hbm, ingrad_hbm, fa_hbm, fb_hbm, ag_in, as_in, mg_in, ms_in,
    bout_out, ingrad_out, attn_gain, attn_shift, qw_out, qb_out, kw_out, kb_out, vw_out, vb_out, ow_out, ob_out,
    mlp_gain, mlp_shift, uw_out, ub_out, dw_out, db_out,
    blocks, fa, fb, up, down, out, qw, kw, vw, turned, sem,
):
    depth = fa.shape[1]
    used = heads * HD
    pairs = (heads + 1) // 2
    width = pairs * LANES
    misc = Q_ROW + used
    loads = [
        pltpu.make_async_copy(fa_hbm.at[pl.ds(ff, depth), :], fa.at[pl.ds(ff, depth), :], sem.at[0]),
        pltpu.make_async_copy(fb_hbm, fb, sem.at[1]),
        pltpu.make_async_copy(fa_hbm.at[pl.ds(0, ff), :], fa.at[pl.ds(0, ff), :], sem.at[2]),
        pltpu.make_async_copy(bout_hbm, blocks.at[0], sem.at[3]),
        pltpu.make_async_copy(ingrad_hbm, blocks.at[1], sem.at[4]),
    ]
    for c in loads:
        c.start()
    row = lambda ref: ref[...].reshape(1, depth)
    ag, as_, mg, ms = row(ag_in), row(as_in), row(mg_in), row(ms_in)
    turned[...] = jnp.transpose(jnp.concatenate([mg, ms, jnp.zeros((6, depth), F32)], axis=0))
    loads[1].wait()
    extra = fb[used : used + 16, :].astype(F32)
    g_sum, up_bias = extra[:1], extra[1:2]
    ob_out[...] = g_sum.reshape(depth)
    db_out[...] = g_sum.reshape(depth)
    ub_out[...] = up_bias.reshape(ff)
    last = fb[misc : misc + 16, :].astype(F32)
    for n, ref in enumerate((attn_gain, attn_shift, mlp_gain, mlp_shift)):
        ref[...] = last[9 + n : 10 + n].reshape(depth)
    kv_bias = last[8:9, :LANES]
    kb_out[...] = kv_bias[:, :HD].reshape(HD)
    vb_out[...] = kv_bias[:, HD:].reshape(HD)
    biases = last[:1, :width]
    qb_out[...] = biases[:, :used].reshape(used)
    loads[0].wait()
    stores = []

    def store(src, dst):
        copy = pltpu.make_async_copy(src, dst, sem.at[5 + len(stores)])
        copy.start()
        stores.append(copy)

    piece = depth // 4
    for n in range(4):
        def scale(r, carry):
            at = rows_of(n * piece + r * 32, 32)
            v = fa[rows_of(ff + n * piece + r * 32, 32), :].astype(F32)
            up[at, :] = v * turned[at, 0:1] + turned[at, 1:2] * up_bias
            return carry

        lax.fori_loop(0, piece // 32, scale, 0)
        store(up.at[pl.ds(n * piece, piece), :], uw_out.at[pl.ds(n * piece, piece), :])
    for n in (3, 4):
        loads[n].wait()
    store(blocks.at[0], bout_out)
    store(blocks.at[1], ingrad_out)
    loads[2].wait()
    piece = ff // 4
    for n in range(4):
        def widen(r, carry):
            at = rows_of(n * piece + r * 32, 32)
            down[at, :] = fa[at, :].astype(F32)
            return carry

        lax.fori_loop(0, piece // 32, widen, 0)
        store(down.at[pl.ds(n * piece, piece), :], dw_out.at[pl.ds(n * piece, piece), :])
    out[...] = fb[:used, :].astype(F32)
    store(out, ow_out)

    def outer(vector, other):
        a, b = top_and_rest(vector)
        c, e = top_and_rest(other)
        return t_dot(jnp.concatenate([a, a, b, b], axis=0), jnp.concatenate([c, e, c, e], axis=0))

    qw[...] = fb[Q_ROW:misc, :].astype(F32) * ag + outer(biases[:, :used], as_)
    store(qw, qw_out)
    kv = fb[KV_ROW : KV_ROW + LANES, :].astype(F32) * ag + outer(kv_bias, as_)
    kw[...] = kv[:HD]
    vw[...] = kv[HD:]
    store(kw, kw_out)
    store(vw, vw_out)
    for c in stores:
        c.wait()


def run_final(heads, ff, block_out, input_grad, fa, fb, gains):
    shard, depth = block_out.shape
    used = heads * HD
    sh = jax.ShapeDtypeStruct
    vm = pltpu.VMEM
    line = lambda n: sh((n,), F32)
    return pl.pallas_call(
        partial(final_kernel, heads, ff),
        out_shape=(
            sh((shard, depth), BF16), sh((shard, depth), BF16), line(depth), line(depth), sh((used, depth), F32), line(used),
            sh((HD, depth), F32), line(HD), sh((HD, depth), F32), line(HD), sh((used, depth), F32), line(depth),
            line(depth), line(depth), sh((depth, ff), F32), line(ff), sh((ff, depth), F32), line(depth),
        ),
        in_specs=[ANY] * 4 + [VM] * 4,
        out_specs=[ANY, ANY, VM, VM, ANY, VM, ANY, VM, ANY, VM, ANY, VM, VM, VM, ANY, VM, ANY, VM],
        scratch_shapes=[
            vm((2, shard, depth), BF16), vm(fa.shape, fa.dtype), vm(fb.shape, fb.dtype), vm((depth, ff), F32), vm((ff, depth), F32),
            vm((used, depth), F32), vm((used, depth), F32), vm((HD, depth), F32), vm((HD, depth), F32), vm((depth, 8), F32),
            pltpu.SemaphoreType.DMA((24,)),
        ],
        compiler_params=pltpu.CompilerParams(vmem_limit_bytes=67043328),
        name="final",
    )(block_out, input_grad, fa, fb, *gains)


def per_device(
    ways,
    tokens, doc_lengths, attn_gain, attn_shift, query_weight, query_bias, key_weight, key_bias, value_weight, value_bias,
    out_weight, out_bias, mlp_gain, mlp_shift, up_weight, up_bias, down_weight, down_bias, out_grad,
):
    heads = query_weight.shape[1] // HD
    small = (
        attn_gain, attn_shift, query_weight.T, query_bias, key_weight.T, key_bias, value_weight.T, value_bias,
        out_weight, out_bias, down_bias, mlp_gain, mlp_shift,
    )
    block_out, input_grad, fa, fb = run_layer(
        heads, doc_lengths, tokens, out_grad, small, up_weight, up_bias, down_weight
    )
    if ways > RING:
        groups = [[i + RING * o for o in range(ways // RING)] for i in range(RING)]
        fa, fb = lax.psum((fa.astype(F32), fb.astype(F32)), "dp", axis_index_groups=groups)
    (
        block_out, input_grad, attn_gain_grad, attn_shift_grad, qw, qb, kw, kb, vw, vb, ow, ob, mlp_gain_grad, mlp_shift_grad,
        uw, ub, dw, db,
    ) = run_final(
        heads, up_weight.shape[1], block_out, input_grad, fa, fb, (attn_gain, attn_shift, mlp_gain, mlp_shift)
    )
    return (
        block_out, input_grad, attn_gain_grad, attn_shift_grad, qw.T, qb, kw.T, kb, vw.T, vb, ow, ob, mlp_gain_grad,
        mlp_shift_grad, uw, ub, dw, db,
    )


def solution(mesh):
    rows = P(("dp", "mp"), None)
    placed = (
        rows, P("dp", None), P(), P(), P(None, "mp"), P("mp"), P(), P(), P(), P(), P("mp", None), P(), P(), P(),
        P(None, "mp"), P("mp"), P("mp", None), P(), rows,
    )
    outs = (
        rows, rows, P(), P(), P(None, "mp"), P("mp"), P(), P(), P(), P(), P("mp", None), P(), P(), P(),
        P(None, "mp"), P("mp"), P("mp", None), P(),
    )
    return jax.shard_map(partial(per_device, mesh.shape["dp"]), mesh=mesh, in_specs=placed, out_specs=outs, check_vma=False)
```

time: 226 us -> 162 us (0.72)
  Pallas kernels: 195 us -> 161 us
  local copies, waits for them, and re-layouts: 22.8 us -> 0 us
  other arithmetic: 6.85 us -> 0 us
    pallas_call x1, Pallas kernels: 195 us -> 153 us  [run_layer(): pl.pallas_call(partial(layer_kernel, heads), out_shape=(sh((SHARD, depth)...]
    unnamed x35 -> x0, local copies, waits for them, and re-layouts: 10.4 us -> none
    pallas_call x0 -> x1, Pallas kernels: none -> 7.73 us  [run_final(): pl.pallas_call(partial(final_kernel, heads, ff), out_shape=(sh((shard, de...]
    reshape x6 -> x0, local copies, waits for them, and re-layouts: 6.92 us -> none  [per_device(): row = lambda v: v.reshape(1, -1)]
    slice x5 -> x0, local copies, waits for them, and re-layouts: 4.69 us -> none  [the longest x1 1.54 us: per_device(): g_sum, bup = (gout[used], gout[used + 1])]
    convert_element_type x3 -> x0, other arithmetic: 3.83 us -> none  [per_device(): gdown, gup, gout, gqkv = (v.astype(F32) for v in (gdown, gup, gout, gqkv))]
    add x4 -> x0, other arithmetic: 3.02 us -> none  [the longest x1 1.78 us: per_device(): up_weight_grad = mlp_gain[:, None] * gup + mlp_shift[:, None] * bup]
where the time goes in v3:
time: 162 us
  Pallas kernels  161 us (99%)
    pallas_call x1, Pallas kernels, run_layer(): pl.pallas_call(partial(layer_kernel, heads), out_shape=(sh((SHARD, depth)...  153 us
    pallas_call x1, Pallas kernels, run_final(): pl.pallas_call(partial(final_kernel, heads, ff), out_shape=(sh((shard, de...  7.73 us

profile of v3, /device:TPU:0, one launch (start us, length us, event | category | flops | bytes accessed | tf_op | source)
XLA Modules:
  0.0 161.5 jit_solution(12121432808100829870)
XLA Ops:
  0.7 152.9 %layer.1 = (bf16[512,768]{1,0:T(8,128)(2,1)}, bf16[512,768]{1,0:T(8,128)(2,1)}, bf16[1536,768]{1,0:T(8,128)(2,1)}, bf16[640,768]{1,0:T(8,128)(2,1)}) custom-call(s32[1,4]{1,0:T(1,128)} %doc_ref.1, bf16[512,768]{1,0:T(8,128)(2,1)} %tok_hbm.1, bf16[512,768]{1,0:T(8,128)(2,1)} %grad_hbm.1, f32[768]{0:T(1024)} %ag_in.3, f32[768]{0:T(1024)} %as_in.3, ...), custom_call_target="tpu_custom_call" | custom-call | tf_op jit(solution)/shard_map/layer/pallas_call | solution.py:848
  153.6 7.7 %final.1 = (bf16[512,768]{1,0:T(8,128)(2,1)}, bf16[512,768]{1,0:T(8,128)(2,1)}, f32[768]{0:T(1024)}, f32[768]{0:T(1024)}, f32[192,768]{1,0:T(8,128)}, /*index=5*...) custom-call(bf16[512,768]{1,0:T(8,128)(2,1)} %get-tuple-element.40.b, ...), custom_call_target="tpu_custom_call" | custom-call | tf_op jit(solution)/shard_map/final/pallas_call | solution.py:956

commit v4 on v3

--- a/solution.py
+++ b/solution.py
@@ -15,6 +15,8 @@
 LONGEST = 1024
 DOCS = 4
 BIG = 1e30
+SPARE = 16
+OUT_EVERY = 6
 EPS = 1e-05
 BLK = 256
 NBLK = SLOT // BLK
@@ -49,7 +51,7 @@
 
 
 SLOTS = {}
-for _i in range(NBLK):
+for _i in range(PADBLK):
     for _j in key_blocks(_i):
         SLOTS[(_i, _j)] = len(SLOTS)
 NSLOT = len(SLOTS)
@@ -262,10 +264,10 @@
     doc_ref, tok_hbm, grad_hbm, ag_in, as_in, wq_ref, bq_in, wk_ref, bk_in, wv_ref, bv_in, wo_ref, ob_in, db_in, mg_in, ms_in,
     wu_hbm, bu_in, wd_hbm,
     bout_hbm, ingrad_hbm, fa_hbm, fb_hbm,
-    xs, gm, outp, em, ga, gb, q, qt, kx, vx, dctx, dct, left_in, cos, sine, ctx, dqh, dkv, dqkv, wqkv, wo, wu, wd, bqkv, gsum, rows_in,
-    own_x, io,
-    st_a, sl_a, f_a, st_b, sl_b, f_b,
-    mo, co, me_, ce, swap,
+    xs, gm, outp, em, ga, gb, q, qt, kx, vx, dctx, dct, left_in, cos, sine, dqh, dkv, dqkv, wqkv, wo, wu, wd, bqkv, gsum, rows_in, dsum,
+    min_,
+    st_a, sl_a, dg, st_b, sl_b, f_b,
+    mo, co, hid, ce, swap,
     loc, ag_send, ag_recv, ra_r, ra_s, rb_r, rb_s, so_s, so_r, se_s, se_r, bf_s, bf_r,
 ):
     pairs = (heads + 1) // 2
@@ -286,15 +288,15 @@
         return outer * RING + jnp.where(p < RING // 2, 2 * p, 2 * (RING - 1 - p) + 1)
 
     right, left = seat((place + 1) % RING), seat((place + RING - 1) % RING)
-    rings_a = Rings(ga, st_a, sl_a, f_a, ra_r, ra_s, place, right, left)
+    rings_a = Rings(ga, st_a, sl_a, dg, ra_r, ra_s, place, right, left)
     rings_b = Rings(gb, st_b, sl_b, f_b, rb_r, rb_s, place, right, left)
 
     local = [
         pltpu.make_async_copy(tok_hbm, xs.at[rows_of(m * SHARD, SHARD), :], loc.at[0]),
         pltpu.make_async_copy(wu_hbm, wu, loc.at[1]),
         pltpu.make_async_copy(wd_hbm, wd, loc.at[2]),
-        pltpu.make_async_copy(tok_hbm, own_x, loc.at[3]),
     ]
+    own_tokens = pltpu.make_async_copy(tok_hbm, min_, loc.at[3])
     for c in local:
         c.start()
     local_g = [
@@ -350,6 +352,11 @@
         @pl.when(valid(m, k))
         def _():
             g_mate(m, k).start()
+    for k in range(2):
+        @pl.when(valid(m, k))
+        def _():
+            g_cross(m, k).start()
+
     build_tables(doc_ref, cos, sine)
     for n, ref in enumerate((ag_in, as_in, mg_in, ms_in, bu_in)):
         rows_in[n : n + 1, :] = ref[...].reshape(1, depth)
@@ -369,11 +376,15 @@
     ga[...] = jnp.zeros_like(ga)
     gb[...] = jnp.zeros_like(gb)
     gsum[...] = jnp.zeros_like(gsum)
+    dsum[...] = jnp.zeros_like(dsum)
     dqkv[VALID:, :] = jnp.zeros((SLOT - VALID, width + LANES), BF16)
     fwd_steps = NBLK * heads
     bwd_steps = PADBLK * heads
     steps = fwd_steps + bwd_steps
-    lead = MP
+    lead = 3
+    chip = m // 2
+    hooks_in_loop = lead + steps - NBLK // 2 * heads
+    spare = SPARE
     down_at, up_at = pl.ds(0, ff), pl.ds(ff, depth)
 
     def times(vector, weight, product):
@@ -384,34 +395,62 @@
 
     def early_rings(t):
         total = 4 * EVENTS
-        hooks = lead + steps
+        hooks = hooks_in_loop + spare
 
         def one(n, carry):
             rings_a.event(n % 4, n // 4)
             return carry
 
-        lax.fori_loop(t * total // hooks, (t + 1) * total // hooks, one, 0)
-
-    def feed_forward(ain, min_, hp, hid, dg):
-        def forward(c, which):
-            half = which % 2
+        lax.fori_loop(jnp.maximum(t, 0) * total // hooks, jnp.maximum(t + 1, 0) * total // hooks, one, 0)
+
+    scat_o = Scatter(outp, mo, co, so_s, so_r, m, mate, cross)
+    scat_e = Scatter(em, hid, ce, se_s, se_r, m, mate, cross)
+    ends = doc_ends(doc_ref)
+    lane = lax.broadcasted_iota(jnp.int32, (BLK, LANES), 1)
+    low = lane < HD
+
+    def body(hp, probs, total):
+        half_lanes = depth // 2
+
+        def attn_in():
+            return jnp.concatenate([dqkv[:SHARD, :], dqkv[SHARD : 2 * SHARD, :]], axis=1)
+
+        def ff_forward(c):
             first = pl.multiple_of(c * SHARD, SHARD)
             here = pl.ds(first, SHARD)
+
+            def moments(r, carry):
+                for part in range(8):
+                    at = rows_of(first + r * 128 + part * 16, 16)
+                    v = xs[at, :].astype(F32)
+                    mean = jnp.mean(v, axis=-1, keepdims=True)
+                    v = v - mean
+                    inv = lax.rsqrt(jnp.mean(v * v, axis=-1, keepdims=True) + EPS)
+                    to = pl.ds(part * 16, 16)
+                    dkv[to, rows_of(r * LANES, LANES)] = jnp.broadcast_to(mean, (16, LANES))
+                    dkv[to, rows_of((4 + r) * LANES, LANES)] = jnp.broadcast_to(inv, (16, LANES))
+                return carry
+
+            lax.fori_loop(0, SHARD // 128, moments, 0)
 
             def norm(r, carry):
                 at = rows_of(first + r * 32, 32)
                 to = rows_of(r * 32, 32)
-                v = xs[at, :].astype(F32)
-                v = v - jnp.mean(v, axis=-1, keepdims=True)
-                v = v * lax.rsqrt(jnp.mean(v * v, axis=-1, keepdims=True) + EPS)
+                sub = rows_of(lax.rem(r * 32, LANES), 32)
+                mean = jnp.concatenate([dkv[sub, rows_of(r // 4 * LANES, LANES)]] * (depth // LANES), axis=1)
+                inv = jnp.concatenate([dkv[sub, rows_of((4 + r // 4) * LANES, LANES)]] * (depth // LANES), axis=1)
+                v = (xs[at, :].astype(F32) - mean) * inv
                 xs[at, :] = v.astype(BF16)
-                ain[to, :] = (v * ag_row[...] + as_row[...]).astype(BF16)
+                a = (v * ag_row[...] + as_row[...]).astype(BF16)
+                dqkv[to, :] = a[:, :half_lanes]
+                dqkv[rows_of(SHARD + r * 32, 32), :] = a[:, half_lanes:]
                 min_[to, :] = (v * mg_row[...] + ms_row[...]).astype(BF16)
                 return carry
 
             lax.fori_loop(0, SHARD // 32, norm, 0)
             ct, st = cos[here, :], sine[here, :]
-            qf = dot_t(ain[...], wqkv[:width, :]) + bqkv[:, :width]
+            ain = attn_in()
+            qf = dot_t(ain, wqkv[:width, :]) + bqkv[:, :width]
             slot = first + lax.broadcasted_iota(jnp.int32, (SHARD, LANES), 0)
             lane = lax.broadcasted_iota(jnp.int32, (SHARD, LANES), 1)
             low = lane < HD
@@ -426,7 +465,7 @@
                 q[2 * p, here, :] = jnp.where(low, v, mark).astype(BF16)
                 if 2 * p + 1 < heads:
                     q[2 * p + 1, here, :] = jnp.where(low, mark, v).astype(BF16)
-            kvf = dot_t(ain[...], wqkv[width:, :]) + bqkv[:, width:]
+            kvf = dot_t(ain, wqkv[width:, :]) + bqkv[:, width:]
             keys = rope(kvf, ct, st)
             other = jnp.where(same | (lane % HD > DOCS), 0.0, 1.0)
             kx[0, here, :] = jnp.where(low, keys, other).astype(BF16)
@@ -436,175 +475,68 @@
             hp[...] = dot(min_[...], wu[...])
 
             def act(r, carry):
-                to = rows_of(r * 16, 16)
+                to = rows_of(r * 32, 32)
                 v = hp[to, :] + bu_row[...]
                 cdf = 0.5 * (1.0 + lax.erf(v * (0.5**0.5)))
                 pdf = jnp.exp(-0.5 * v * v) * (2.0 * jnp.pi) ** -0.5
-                hid[half, to, :] = (v * cdf).astype(BF16)
-                dg[which, to, :] = (cdf + v * pdf).astype(BF16)
+                hid[c % 2 * 2 + r // (BLK // 32), rows_of(lax.rem(r * 32, BLK), 32), :] = (v * cdf).astype(BF16)
+                dg[rows_of(first + r * 32, 32), :] = (cdf + v * pdf).astype(BF16)
                 return carry
 
-            lax.fori_loop(0, SHARD // 16, act, 0)
-            outp[here, :] = dot(hid[half], wd[...]).astype(BF16)
-
-        def backward(c, which):
-            first = pl.multiple_of(c * SHARD, SHARD)
-            here = pl.ds(first, SHARD)
-            g = gm[here, :]
-            hp[...] = dot_t(g, wd[...])
+            lax.fori_loop(0, SHARD // 32, act, 0)
+            outp[here, :] = dot(hid[pl.ds(c % 2 * 2, 2)].reshape(SHARD, ff), wd[...]).astype(BF16)
+
+        def ff_backward(c, k):
+            first = pl.multiple_of(c * SHARD + k * BLK, BLK)
+            hp[:BLK, :] = dot_t(gm[pl.ds(first, BLK), :], wd[...])
 
             def back(r, carry):
                 acc, gacc = carry
-                to = rows_of(r * 16, 16)
-                v = hp[to, :] * dg[which, to, :].astype(F32)
-                dg[which, to, :] = v.astype(BF16)
-                gv = gm[rows_of(first + r * 16, 16), :].astype(F32)
-                return acc + v[:8] + v[8:], gacc + gv[:8] + gv[8:]
-
-            acc, gacc = lax.fori_loop(0, SHARD // 16, back, (jnp.zeros((8, ff), F32), jnp.zeros((8, depth), F32)))
+                at = rows_of(first + r * 32, 32)
+                v = hp[rows_of(r * 32, 32), :] * dg[at, :].astype(F32)
+                dg[at, :] = v.astype(BF16)
+                gv = gm[at, :].astype(F32)
+                acc = acc + (v[:8] + v[8:16]) + (v[16:24] + v[24:])
+                return acc, gacc + (gv[:8] + gv[8:16]) + (gv[16:24] + gv[24:])
+
+            acc, gacc = lax.fori_loop(0, BLK // 32, back, (jnp.zeros((8, ff), F32), jnp.zeros((8, depth), F32)))
             gsum[:8, :] += gacc
             gsum[8:, :] += acc
-            ga[down_at, :] += t_dot(hid[which % 2], g)
-            ga[up_at, :] += t_dot(xs[here, :], dg[which])
+
+        def weights(chip):
+            rows = rows_of(chip * 2 * SHARD, 2 * SHARD)
+            ga[down_at, :] += t_dot(hid[...].reshape(2 * SHARD, ff), gm[rows, :])
+            ga[up_at, :] += t_dot(xs[rows, :], dg[rows, :])
 
         def shard_of(which):
             return jnp.where(which == 0, m, jnp.where(which == 1, mate, jnp.where(which == 2, cross, far)))
 
-        def after(which, hook):
-            hook(0)
-            here = rows_of(shard_of(which) * SHARD, SHARD)
-            em[here, :] = (dot_t(dg[which], wu[...]) * mg_row[...]).astype(BF16)
-            hook(1)
+        def after(shard):
+            here = rows_of(shard * SHARD, SHARD)
+            em[here, :] = (dot_t(dg[here, :], wu[...]) * mg_row[...]).astype(BF16)
             dc = dot_t(gm[here, :], wo[...]).astype(BF16)
             for p in range(pairs):
                 dctx[p, here, :] = dc[:, p * LANES : (p + 1) * LANES]
 
-        def step(s, carry):
-            early = s < 4
-            which = jnp.where(early, s // 2, 2 + s % 2)
-            is_forward = jnp.where(early, s % 2 == 0, s < 6)
-            shard = shard_of(which)
-
-            @pl.when(s == 0)
-            def _():
-                for c in local:
-                    c.wait()
-
-            @pl.when(s == 1)
-            def _():
-                for k in range(2):
-                    @pl.when(valid(m, k))
-                    def _():
-                        local_g[k].wait()
-
-            @pl.when(s == 2)
-            def _():
-                for k in range(2):
-                    x_mate(mate, k).wait_recv()
-
-            @pl.when(s == 3)
-            def _():
-                for k in range(2):
-                    x_cross(m, k).wait_send()
-
-                    @pl.when(valid(m, k))
-                    def _():
-                        g_cross(m, k).start()
-
-                for k in range(2):
-                    x_cross(cross, k).wait_recv()
-                    x_pass(cross, k).start()
-                for k in range(2):
-                    @pl.when(valid(mate, k))
-                    def _():
-                        g_mate(mate, k).wait_recv()
-
-            @pl.when(s == 5)
-            def _():
-                for k in range(2):
-                    x_pass(far, k).wait_recv()
-
-            @pl.when(s == 4)
-            def _():
-                for k in range(2):
-                    x_pass(cross, k).wait_send()
-
-            @pl.when(s == 6)
-            def _():
-                def ahead(which, carry):
-                    after(which, lambda n: None)
-                    return carry
-
-                lax.fori_loop(0, 2, ahead, 0)
-                for k in range(2):
-                    @pl.when(valid(cross, k))
-                    def _():
-                        g_cross(cross, k).wait_recv()
-                        g_pass(cross, k).start()
-
-            @pl.when(s == 7)
-            def _():
-                for k in range(2):
-                    @pl.when(valid(far, k))
-                    def _():
-                        g_pass(far, k).wait_recv()
-
-            @pl.when(is_forward)
-            def _():
-                forward(shard, which)
-
-            @pl.when(jnp.logical_not(is_forward))
-            def _():
-                backward(shard, which)
-
-            return carry
-
-        lax.fori_loop(0, 8, step, 0)
-        up_bias = jnp.sum(gsum[8:, :], axis=0, keepdims=True)
-        gb[used : used + 8, :] = jnp.concatenate(
-            [jnp.sum(gsum[:8, :], axis=0, keepdims=True), up_bias, jnp.zeros((6, depth), F32)], axis=0
-        )
-        ones = jnp.ones((8, LANES), BF16)
-        gain = jnp.zeros((8, depth), F32)
-        for c in range(0, ff, LANES):
-            for part in top_and_rest(wu[:, c : c + LANES].astype(F32) * ga[up_at, c : c + LANES]):
-                gain = gain + dot_t(ones, part)
-        gb[misc + 11 : misc + 12, :] = gain[:1]
-        gb[misc + 12 : misc + 13, :] = times(up_bias, wu, dot_t)
-
-        def behind(which, carry):
-            after(which, lambda n: early_rings(2 * (which - 2) + n))
-            return carry
-
-        lax.fori_loop(2, MP, behind, 0)
-
-    sh16 = pltpu.VMEM((SHARD, depth), BF16)
-    pl.run_scoped(
-        feed_forward, sh16, sh16, pltpu.VMEM((SHARD, ff), F32), pltpu.VMEM((2, SHARD, ff), BF16), pltpu.VMEM((MP, SHARD, ff), BF16),
-    )
-    for k in range(2):
-        x_mate(m, k).wait_send()
-
-        @pl.when(valid(m, k))
-        def _():
-            g_cross(m, k).wait_send()
-            g_mate(m, k).wait_send()
-
-        @pl.when(valid(cross, k))
-        def _():
-            g_pass(cross, k).wait_send()
-
-    scat_o = Scatter(outp, mo, co, so_s, so_r, m, mate, cross)
-    scat_e = Scatter(em, me_, ce, se_s, se_r, m, mate, cross)
-    ends = doc_ends(doc_ref)
-    lane = lax.broadcasted_iota(jnp.int32, (BLK, LANES), 1)
-    low = lane < HD
-
-    def attention(probs, scores, total):
-        dkv[...] = jnp.zeros_like(dkv)
+        def norm_grads():
+            up_bias = jnp.sum(gsum[8:, :], axis=0, keepdims=True)
+            gb[used : used + 8, :] = jnp.concatenate(
+                [jnp.sum(gsum[:8, :], axis=0, keepdims=True), up_bias, jnp.zeros((6, depth), F32)], axis=0
+            )
+            ones = jnp.ones((8, LANES), BF16)
+            gain = jnp.zeros((8, depth), F32)
+            for c in range(0, ff, LANES):
+                for part in top_and_rest(wu[:, c : c + LANES].astype(F32) * ga[up_at, c : c + LANES]):
+                    gain = gain + dot_t(ones, part)
+            gb[misc + 11 : misc + 12, :] = gain[:1]
+            gb[misc + 12 : misc + 13, :] = times(up_bias, wu, dot_t)
+
         causal = lax.broadcasted_iota(jnp.int32, (BLK, BLK), 1) <= lax.broadcasted_iota(jnp.int32, (BLK, BLK), 0)
 
-        def forward(i, h):
+        def scores(n):
+            return hp.at[pl.ds(n // 3 * BLK, BLK), pl.ds(n % 3 * BLK, BLK)]
+
+        def att_forward(i, h):
             at = pl.ds(i * BLK, BLK)
             blocks = key_blocks(i)
             qb = q[h, at, :]
@@ -614,13 +546,14 @@
                 s = dot_t(qb, kx[half, pl.ds(j * BLK, BLK), :])
                 if i == j:
                     s = jnp.where(causal, s, -BIG)
-                scores[:, n * BLK : (n + 1) * BLK] = s
+                scores(n)[...] = s
                 peak = s if peak is None else jnp.maximum(peak, s)
             top = jnp.max(peak, axis=-1, keepdims=True)
             acc = jnp.zeros((BLK, LANES), F32)
             for n, j in enumerate(blocks):
-                e = jnp.exp(scores[:, n * BLK : (n + 1) * BLK] - top).astype(BF16)
-                probs[h, SLOTS[(i, j)]] = e
+                e = jnp.exp(scores(n)[...] - top).astype(BF16)
+                if i < PADBLK:
+                    probs[h, SLOTS[(i, j)]] = e
                 acc = acc + dot(e, vx[half, pl.ds(j * BLK, BLK), :])
             total[h] = acc
 
@@ -634,7 +567,6 @@
                     norm = 1.0 / norm
                     c = jnp.where(low, first, second if full else 0.0) * norm
                     context.append(c.astype(BF16))
-                    ctx[at, p * LANES : (p + 1) * LANES] = context[p]
                     if i < PADBLK:
                         scaled = dctx[p, at, :].astype(F32) * norm
                         dcs = scaled.astype(BF16).astype(F32)
@@ -646,12 +578,19 @@
                             r_top = r.astype(BF16).astype(F32)
                             extra = jnp.where(lane % HD == 0, r_top, jnp.where(lane % HD == 1, r - r_top, 0.0))
                             left_in[2 * p + side, at, :] = jnp.where(inside, dcs, extra).astype(BF16)
+                for p in range(pairs):
+                    dctx[p, at, :] = context[p]
                 outp[at, :] = (dot(jnp.concatenate(context, axis=1), wo[...]) + outp[at, :].astype(F32)).astype(BF16)
                 scat_o.offer(i)
-                if i > 0:
-                    scat_o.collect(i - 1)
-
-        def backward(i, h):
+                before = (i - 1) % NBLK
+                if i % (NBLK // 2) > 0:
+                    scat_o.collect(before)
+                else:
+                    @pl.when(chip != i // (NBLK // 2))
+                    def _():
+                        scat_o.collect(before)
+
+        def att_backward(i, h):
             at = pl.ds(i * BLK, BLK)
             half = h % 2
             lhs = left_in[h, at, :]
@@ -676,49 +615,159 @@
                     dqkv[at, p * LANES : (p + 1) * LANES] = (unrope(v, ct, st) * HD**-0.5).astype(BF16)
                 v = jnp.transpose(dkv[:, at])
                 dqkv[at, width:] = jnp.where(low, unrope(v, ct, st), v).astype(BF16)
+                dsum[:1, :] += jnp.sum(dqkv[at, :].astype(F32), axis=0, keepdims=True)
                 em[at, :] = (dot(dqkv[at, :], wqkv[...]) * ag_row[...] + em[at, :].astype(F32)).astype(BF16)
                 scat_e.offer(i)
                 if i < PADBLK - 1:
                     scat_e.collect(i + 1)
 
         def out_rings(n):
-            @pl.when(n < 2 * EVENTS)
-            def _():
-                rings_b.event(n % 2, n // 2)
-
-        def step(t, carry):
-            early_rings(lead + t)
-
-            @pl.when(t < fwd_steps)
-            def _():
-                lax.switch(t // heads, [partial(forward, i) for i in range(NBLK)], t % heads)
-
-            @pl.when(t == fwd_steps)
-            def _():
-                scat_o.collect(NBLK - 1)
-                gb[:used, :] = t_dot(ctx[...], gm[...])[:used, :]
-
-            @pl.when(t >= fwd_steps)
+            @pl.when(n % OUT_EVERY == 0)
+            def _():
+                def one(r, carry):
+                    rings_b.event(r, n // OUT_EVERY)
+                    return carry
+
+                lax.fori_loop(0, 2, one, 0)
+
+        plan = [(0, 0, 0), (1, 0, 0), (1, 0, 1), (0, 1, 0), (1, 1, 0), (1, 1, 1), (2, 0, 0), (3, 0, 0), (3, 1, 0), (0, 2, 0), (0, 3, 0)]
+        plan += [(1, 2, 0), (1, 2, 1), (1, 3, 0), (1, 3, 1), (2, 2, 0), (3, 2, 0), (3, 3, 0), (4, 0, 0)]
+        before = 11
+        early = NBLK // 2 * heads
+        after_all = len(plan) + early
+        hooked = 16 + early
+
+        def pick(s, column):
+            value = plan[0][column]
+            for n, entry in enumerate(plan):
+                if entry[column] != plan[0][column]:
+                    value = jnp.where(s == n, entry[column], value)
+            return value
+
+        def at_step(n):
+            return lambda action: pl.when(step_now[0] == n)(action)
+
+        step_now = [None]
+
+        def step(s, carry):
+            planned = (s < before) | ((s >= before + early) & (s < after_all))
+            p = jnp.where(s < before, s, s - early)
+            step_now[0] = jnp.where(planned, p, -1)
+            t = jnp.where(s < after_all, s - before, s - after_all + early)
+            early_rings(s - hooked)
+
+            @at_step(0)
+            def _():
+                for c in local:
+                    c.wait()
+
+            @at_step(1)
+            def _():
+                for k in range(2):
+                    @pl.when(valid(m, k))
+                    def _():
+                        local_g[k].wait()
+
+            @at_step(3)
+            def _():
+                for k in range(2):
+                    x_mate(mate, k).wait_recv()
+
+            @at_step(4)
+            def _():
+                for k in range(2):
+                    @pl.when(valid(mate, k))
+                    def _():
+                        g_mate(mate, k).wait_recv()
+
+            @at_step(7)
+            def _():
+                for k in range(2):
+                    x_cross(m, k).wait_send()
+                    x_cross(cross, k).wait_recv()
+                    x_pass(cross, k).start()
+
+            @at_step(9)
+            def _():
+                for k in range(2):
+                    x_pass(cross, k).wait_send()
+
+            @at_step(10)
+            def _():
+                for k in range(2):
+                    x_pass(far, k).wait_recv()
+
+            for k in range(2):
+                @at_step(11 + k)
+                def _():
+                    @pl.when(valid(cross, k))
+                    def _():
+                        g_cross(cross, k).wait_recv()
+                        g_pass(cross, k).start()
+
+                @at_step(13 + k)
+                def _():
+                    @pl.when(valid(far, k))
+                    def _():
+                        g_pass(far, k).wait_recv()
+
+            @pl.when(jnp.logical_not(planned) & (t == fwd_steps))
+            def _():
+                own_tokens.start()
+                dkv[...] = jnp.zeros_like(dkv)
+                for b in (NBLK // 2 - 1, NBLK - 1):
+                    @pl.when(chip != b // (NBLK // 2))
+                    def _():
+                        scat_o.collect(b)
+                for p in range(pairs):
+                    some = min(used - p * LANES, LANES)
+                    gb[p * LANES : p * LANES + some, :] = t_dot(dctx[p], gm[...])[:some, :]
+
+            @pl.when(jnp.logical_not(planned) & (t >= fwd_steps))
             def _():
                 out_rings(t - fwd_steps)
-                lax.switch((t - fwd_steps) // heads, [partial(backward, i) for i in reversed(range(PADBLK))], (t - fwd_steps) % heads)
-
+
+            shard = shard_of(pick(p, 1))
+            half = pick(p, 2)
+            h = t % heads
+            forward_block = (t // heads + chip * (NBLK // 2)) % NBLK
+            backward_block = (t - fwd_steps) // heads
+            kind = jnp.where(planned, pick(p, 0), jnp.where(t < fwd_steps, 5, 6))
+            lax.switch(
+                kind,
+                [
+                    lambda: ff_forward(shard), lambda: ff_backward(shard, half), lambda: weights(shard // 2), lambda: after(shard),
+                    norm_grads,
+                    lambda: lax.switch(forward_block, [partial(att_forward, i) for i in range(NBLK)], h),
+                    lambda: lax.switch(backward_block, [partial(att_backward, i) for i in reversed(range(PADBLK))], h),
+                ],
+            )
             return carry
 
-        lax.fori_loop(0, steps, step, 0)
+        lax.fori_loop(0, after_all + steps - early, step, 0)
 
     pl.run_scoped(
-        attention, pltpu.VMEM((heads, NSLOT, BLK, BLK), BF16), pltpu.VMEM((BLK, (BAND + 1) * BLK), F32),
-        pltpu.VMEM((heads, BLK, LANES), F32),
+        body, pltpu.VMEM((SHARD, ff), F32), pltpu.VMEM((heads, NSLOT, BLK, BLK), BF16), pltpu.VMEM((heads, BLK, LANES), F32),
     )
-
-    out_a = pltpu.make_async_copy(f_a, fa_hbm, loc.at[0])
-    out_a.start()
+    for k in range(2):
+        x_mate(m, k).wait_send()
+
+        @pl.when(valid(m, k))
+        def _():
+            g_cross(m, k).wait_send()
+            g_mate(m, k).wait_send()
+
+        @pl.when(valid(cross, k))
+        def _():
+            g_pass(cross, k).wait_send()
+
     scat_e.collect(0)
     rows = VALID
     gb[KV_ROW : KV_ROW + LANES, :] = t_dot(dqkv[:rows, width:], xs[:rows, :])
+    rings_b.event(2, 0)
     gb[Q_ROW:misc, :] = t_dot(dqkv[:rows, :width], xs[:rows, :])[:used, :]
-    sums = jnp.sum(dqkv[:rows, :].astype(F32), axis=0, keepdims=True)
+    rings_b.event(3, 0)
+    sums = dsum[:1, :]
     gb[misc : misc + 1, : width + LANES] = sums
     gb[misc + 8 : misc + 9, :LANES] = sums[:, width:]
     gain = jnp.sum(wqkv[:used, :].astype(F32) * gb[Q_ROW:misc, :], axis=0, keepdims=True)
@@ -726,82 +775,120 @@
         wqkv[width:, :].astype(F32) * gb[KV_ROW : KV_ROW + LANES, :], axis=0, keepdims=True
     )
     gb[misc + 10 : misc + 11, :] = times(sums, wqkv, dot)
-
-    def tail(n, carry):
-        rings_b.event(2 + n % 3, n // 3)
-        return carry
-
-    def advance(first, last):
-        lax.fori_loop(3 * first, 3 * last, tail, 0)
-
-    advance(0, 1)
-    for k in range(2):
-        scat_o.arrived(k)
-
-        def finish_out(r, carry):
-            at = pl.multiple_of(r * 32, 32)
-            v = own_x[rows_of(k * BLK + at, 32), :].astype(F32) + scat_o.total(k, at) + rows_in[5:6, :]
-            io[rows_of(k * BLK + at, 32), :] = v.astype(BF16)
-            return carry
-
-        lax.fori_loop(0, BLK // 32, finish_out, 0)
-    out_block = pltpu.make_async_copy(io, bout_hbm, loc.at[1])
-    out_block.start()
-    advance(1, 4)
-
-    rings_b.settle(2)
-    rings_b.settle(4)
-    swap[0, :16, :] = f_b[rings_b.at(2, 0), :]
-    swap[0, 16:, :] = f_b[rings_b.at(4, 0), :]
+    rings_b.event(4, 0)
 
     def exchange(stage, to):
-        copy = pltpu.make_async_remote_copy(
+        return pltpu.make_async_remote_copy(
             src_ref=swap.at[2 * stage], dst_ref=swap.at[2 * stage + 1], send_sem=bf_s.at[stage], recv_sem=bf_r.at[stage],
             device_id={"mp": to}, device_id_type=MESH,
         )
-        copy.start()
-        return copy
-
-    copy = exchange(0, mate)
-    rings_b.event(3, 4)
-    copy.wait()
-    swap[2] = (swap[0].astype(F32) + swap[1].astype(F32)).astype(BF16)
-    exchange(1, cross).wait()
-    both = swap[2].astype(F32) + swap[3].astype(F32)
-    f_b[rings_b.at(2, 0), :] = both[:16].astype(BF16)
-    last = lax.broadcasted_iota(jnp.int32, (16, depth), 0) >= jnp.where(place == used // 16 % RING, 8, 16)
-    f_b[rings_b.at(4, 0), :] = jnp.where(last, both[16:], swap[0, 16:, :].astype(F32)).astype(BF16)
-    rings_b.release(2)
-    rings_b.release(4)
-    advance(5, 6)
-    for k in range(2):
-        @pl.when(valid(m, k))
-        def _():
-            scat_e.arrived(k)
-
-            def finish_in(r, carry):
-                at = pl.multiple_of(r * 32, 32)
-                v = own_x[rows_of(k * BLK + at, 32), :].astype(F32)
-                v = v - jnp.mean(v, axis=-1, keepdims=True)
-                inv = lax.rsqrt(jnp.mean(v * v, axis=-1, keepdims=True) + EPS)
-                v = v * inv
-                e = scat_e.total(k, at)
-                e = inv * (e - jnp.mean(e, axis=-1, keepdims=True) - v * jnp.mean(e * v, axis=-1, keepdims=True))
-                g = gm[rows_of((2 * m + k) * BLK + at, 32), :].astype(F32)
-                own_x[rows_of(k * BLK + at, 32), :] = (e + g).astype(BF16)
-                return carry
-
-            lax.fori_loop(0, BLK // 32, finish_in, 0)
-
-        @pl.when(jnp.logical_not(valid(m, k)))
-        def _():
-            own_x[pl.ds(k * BLK, BLK), :] = jnp.zeros((BLK, depth), BF16)
-    out_in = pltpu.make_async_copy(own_x, ingrad_hbm, loc.at[2])
-    out_in.start()
-    advance(6, EVENTS)
+
+    def finish_out(r, carry):
+        at = pl.multiple_of(r * 32, 32)
+        v = min_[rows_of(at, 32), :].astype(F32) + scat_o.total(r // (BLK // 32), lax.rem(at, BLK)) + rows_in[5:6, :]
+        outp[rows_of(m * SHARD + at, 32), :] = v.astype(BF16)
+        return carry
+
+    def finish_in(r, carry):
+        at = pl.multiple_of(r * 32, 32)
+        v = min_[rows_of(at, 32), :].astype(F32)
+        v = v - jnp.mean(v, axis=-1, keepdims=True)
+        inv = lax.rsqrt(jnp.mean(v * v, axis=-1, keepdims=True) + EPS)
+        v = v * inv
+        e = scat_e.total(r // (BLK // 32), lax.rem(at, BLK))
+        e = inv * (e - jnp.mean(e, axis=-1, keepdims=True) - v * jnp.mean(e * v, axis=-1, keepdims=True))
+        g = gm[rows_of(m * SHARD + at, 32), :].astype(F32)
+        min_[rows_of(at, 32), :] = (e + g).astype(BF16)
+        return carry
+
+    out_block = pltpu.make_async_copy(outp.at[rows_of(m * SHARD, SHARD), :], bout_hbm, loc.at[1])
+    out_in = pltpu.make_async_copy(min_, ingrad_hbm, loc.at[2])
+
+    done = (bwd_steps - 1) // OUT_EVERY
+
+    def tail(e, carry):
+        def late(n, carry):
+            early_rings(hooks_in_loop + n)
+            return carry
+
+        def one(r, carry):
+            step = jnp.where(r < 2, e + done, e)
+
+            @pl.when(jnp.where(r < 2, step < EVENTS, (e != 4) | (r == 3)))
+            def _():
+                rings_b.event(r, step)
+
+            return carry
+
+        @pl.when(e == 4)
+        def _():
+            rings_b.settle(2)
+            rings_b.settle(4)
+            swap[0, :16, :] = f_b[rings_b.at(2, 0), :]
+            swap[0, 16:, :] = f_b[rings_b.at(4, 0), :]
+            exchange(0, mate).start()
+
+        lax.fori_loop(0, 5, one, 0)
+
+        @pl.when(e == 4)
+        def _():
+            exchange(0, mate).wait()
+            swap[2] = (swap[0].astype(F32) + swap[1].astype(F32)).astype(BF16)
+            exchange(1, cross).start()
+
+        lax.fori_loop((e - 1) * spare // (EVENTS - 1), e * spare // (EVENTS - 1), late, 0)
+
+        @pl.when(e == 4)
+        def _():
+            exchange(1, cross).wait()
+            both = swap[2].astype(F32) + swap[3].astype(F32)
+            f_b[rings_b.at(2, 0), :] = both[:16].astype(BF16)
+            last = lax.broadcasted_iota(jnp.int32, (16, depth), 0) >= jnp.where(place == used // 16 % RING, 8, 16)
+            f_b[rings_b.at(4, 0), :] = jnp.where(last, both[16:], swap[0, 16:, :].astype(F32)).astype(BF16)
+            rings_b.release(2)
+            rings_b.release(4)
+
+        @pl.when(e == 1)
+        def _():
+            own_tokens.wait()
+            for k in range(2):
+                scat_o.arrived(k)
+
+        @pl.when(e <= 4)
+        def _():
+            lax.fori_loop((e - 1) * (SHARD // 128), e * (SHARD // 128), finish_out, 0)
+
+        @pl.when(e == 4)
+        def _():
+            out_block.start()
+
+        @pl.when(e == 5)
+        def _():
+            for k in range(2):
+                @pl.when(valid(m, k))
+                def _():
+                    scat_e.arrived(k)
+
+            @pl.when(jnp.logical_not(valid(m, 1)))
+            def _():
+                min_[BLK:, :] = jnp.zeros((BLK, depth), BF16)
+
+        @pl.when((e >= 5) & (e < 8))
+        def _():
+            limit = jnp.where(valid(m, 1), SHARD, BLK) // 32
+            lax.fori_loop((e - 5) * limit // 3, (e - 4) * limit // 3, finish_in, 0)
+
+        @pl.when(e == 7)
+        def _():
+            out_in.start()
+
+        return carry
+
+    lax.fori_loop(1, EVENTS, tail, 0)
+    out_a = pltpu.make_async_copy(dg.at[: ff + depth, :], fa_hbm, loc.at[0])
+    out_a.start()
     out_b = pltpu.make_async_copy(f_b, fb_hbm, loc.at[3])
     out_b.start()
-
     for b in range(NBLK):
         scat_o.drain(b)
         if b < PADBLK:
@@ -835,11 +922,11 @@
         vm((a_rows, depth), F32), vm((b_rows, depth), F32),
         vm((heads, SLOT, LANES), BF16), vm((width, SLOT), BF16), vm((2, SLOT, LANES), BF16), vm((2, SLOT, LANES), BF16),
         vm((pairs, SLOT, LANES), BF16), vm((width, VALID), BF16), vm((heads, VALID, LANES), BF16),
-        vm((SLOT, LANES), F32), vm((SLOT, LANES), F32), vm((SLOT, width), BF16), vm((heads, BLK, LANES), F32),
+        vm((SLOT, LANES), F32), vm((SLOT, LANES), F32), vm((heads, BLK, LANES), F32),
         vm((LANES, VALID), F32), vm((SLOT, wide), BF16), vm((wide, depth), BF16), vm((width, depth), BF16),
-        vm((depth, ff), BF16), vm((ff, depth), BF16), vm((1, wide), F32), vm((16, depth), F32), vm((8, depth), F32),
-        vm((SHARD, depth), BF16), vm((SHARD, depth), BF16),
-        *ring_refs(a_rows, 4), *ring_refs(b_rows, 5),
+        vm((depth, ff), BF16), vm((ff, depth), BF16), vm((1, wide), F32), vm((16, depth), F32), vm((8, depth), F32), vm((8, wide), F32),
+        vm((SHARD, depth), BF16),
+        *ring_refs(a_rows, 4)[:2], vm((SLOT, ff), BF16), *ring_refs(b_rows, 5),
         vm((4, BLK, depth), BF16), vm((2, BLK, depth), BF16), vm((4, BLK, depth), BF16), vm((2, BLK, depth), BF16),
         vm((4, 32, depth), BF16),
         dma((8,)), dma((12,)), dma((12,)), dma((4, 4, 8)), dma((4, 4)), dma((5, 4, 8)), dma((5, 4)),
@@ -863,73 +950,56 @@
     bout_hbm, ingrad_hbm, fa_hbm, fb_hbm, ag_in, as_in, mg_in, ms_in,
     bout_out, ingrad_out, attn_gain, attn_shift, qw_out, qb_out, kw_out, kb_out, vw_out, vb_out, ow_out, ob_out,
     mlp_gain, mlp_shift, uw_out, ub_out, dw_out, db_out,
-    blocks, fa, fb, up, down, out, qw, kw, vw, turned, sem,
+    blocks, fa, fb, wide, out, qw, kw, vw, turned, sem,
 ):
     depth = fa.shape[1]
     used = heads * HD
     pairs = (heads + 1) // 2
     width = pairs * LANES
     misc = Q_ROW + used
-    loads = [
-        pltpu.make_async_copy(fa_hbm.at[pl.ds(ff, depth), :], fa.at[pl.ds(ff, depth), :], sem.at[0]),
-        pltpu.make_async_copy(fb_hbm, fb, sem.at[1]),
-        pltpu.make_async_copy(fa_hbm.at[pl.ds(0, ff), :], fa.at[pl.ds(0, ff), :], sem.at[2]),
-        pltpu.make_async_copy(bout_hbm, blocks.at[0], sem.at[3]),
-        pltpu.make_async_copy(ingrad_hbm, blocks.at[1], sem.at[4]),
-    ]
-    for c in loads:
-        c.start()
+    stores = []
+
+    def load(src, dst, n):
+        copy = pltpu.make_async_copy(src, dst, sem.at[n])
+        copy.start()
+        return copy
+
+    def store(src, dst):
+        copy = pltpu.make_async_copy(src, dst, sem.at[12 + len(stores)])
+        copy.start()
+        stores.append(copy)
+
+    piece = 384
+    parts = (ff + depth) // piece
+    small = load(fb_hbm, fb, 0)
+    loads = [load(fa_hbm.at[pl.ds(n * piece, piece), :], fa.at[pl.ds(n * piece, piece), :], 1 + n) for n in range(parts)]
+    passed = [load(ref, blocks.at[n], 8 + n) for n, ref in enumerate((bout_hbm, ingrad_hbm))]
     row = lambda ref: ref[...].reshape(1, depth)
     ag, as_, mg, ms = row(ag_in), row(as_in), row(mg_in), row(ms_in)
     turned[...] = jnp.transpose(jnp.concatenate([mg, ms, jnp.zeros((6, depth), F32)], axis=0))
-    loads[1].wait()
+    small.wait()
     extra = fb[used : used + 16, :].astype(F32)
     g_sum, up_bias = extra[:1], extra[1:2]
-    ob_out[...] = g_sum.reshape(depth)
-    db_out[...] = g_sum.reshape(depth)
-    ub_out[...] = up_bias.reshape(ff)
-    last = fb[misc : misc + 16, :].astype(F32)
-    for n, ref in enumerate((attn_gain, attn_shift, mlp_gain, mlp_shift)):
-        ref[...] = last[9 + n : 10 + n].reshape(depth)
-    kv_bias = last[8:9, :LANES]
-    kb_out[...] = kv_bias[:, :HD].reshape(HD)
-    vb_out[...] = kv_bias[:, HD:].reshape(HD)
-    biases = last[:1, :width]
-    qb_out[...] = biases[:, :used].reshape(used)
-    loads[0].wait()
-    stores = []
-
-    def store(src, dst):
-        copy = pltpu.make_async_copy(src, dst, sem.at[5 + len(stores)])
-        copy.start()
-        stores.append(copy)
-
-    piece = depth // 4
-    for n in range(4):
-        def scale(r, carry):
-            at = rows_of(n * piece + r * 32, 32)
-            v = fa[rows_of(ff + n * piece + r * 32, 32), :].astype(F32)
-            up[at, :] = v * turned[at, 0:1] + turned[at, 1:2] * up_bias
-            return carry
-
-        lax.fori_loop(0, piece // 32, scale, 0)
-        store(up.at[pl.ds(n * piece, piece), :], uw_out.at[pl.ds(n * piece, piece), :])
-    for n in (3, 4):
+    for n in range(parts):
         loads[n].wait()
-    store(blocks.at[0], bout_out)
-    store(blocks.at[1], ingrad_out)
-    loads[2].wait()
-    piece = ff // 4
-    for n in range(4):
-        def widen(r, carry):
-            at = rows_of(n * piece + r * 32, 32)
-            down[at, :] = fa[at, :].astype(F32)
-            return carry
-
-        lax.fori_loop(0, piece // 32, widen, 0)
-        store(down.at[pl.ds(n * piece, piece), :], dw_out.at[pl.ds(n * piece, piece), :])
+        at = n * piece
+        if at < ff:
+            wide[pl.ds(at, piece), :] = fa[pl.ds(at, piece), :].astype(F32)
+            store(wide.at[pl.ds(at, piece), :], dw_out.at[pl.ds(at, piece), :])
+        else:
+            to = at - ff
+            wide[pl.ds(at, piece), :] = (
+                fa[pl.ds(at, piece), :].astype(F32) * turned[to : to + piece, 0:1] + turned[to : to + piece, 1:2] * up_bias
+            )
+            store(wide.at[pl.ds(at, piece), :], uw_out.at[pl.ds(to, piece), :])
+    for n, dst in enumerate((bout_out, ingrad_out)):
+        passed[n].wait()
+        store(blocks.at[n], dst)
     out[...] = fb[:used, :].astype(F32)
     store(out, ow_out)
+    last = fb[misc : misc + 16, :].astype(F32)
+    kv_bias = last[8:9, :LANES]
+    biases = last[:1, :width]
 
     def outer(vector, other):
         a, b = top_and_rest(vector)
@@ -943,6 +1013,14 @@
     vw[...] = kv[HD:]
     store(kw, kw_out)
     store(vw, vw_out)
+    for n, ref in enumerate((attn_gain, attn_shift, mlp_gain, mlp_shift)):
+        ref[...] = last[9 + n : 10 + n].reshape(depth)
+    kb_out[...] = kv_bias[:, :HD].reshape(HD)
+    vb_out[...] = kv_bias[:, HD:].reshape(HD)
+    qb_out[...] = biases[:, :used].reshape(used)
+    ob_out[...] = g_sum.reshape(depth)
+    db_out[...] = g_sum.reshape(depth)
+    ub_out[...] = up_bias.reshape(ff)
     for c in stores:
         c.wait()
 
@@ -963,7 +1041,7 @@
         in_specs=[ANY] * 4 + [VM] * 4,
         out_specs=[ANY, ANY, VM, VM, ANY, VM, ANY, VM, ANY, VM, ANY, VM, VM, VM, ANY, VM, ANY, VM],
         scratch_shapes=[
-            vm((2, shard, depth), BF16), vm(fa.shape, fa.dtype), vm(fb.shape, fb.dtype), vm((depth, ff), F32), vm((ff, depth), F32),
+            vm((2, shard, depth), BF16), vm(fa.shape, fa.dtype), vm(fb.shape, fb.dtype), vm((ff + depth, depth), F32),
             vm((used, depth), F32), vm((used, depth), F32), vm((HD, depth), F32), vm((HD, depth), F32), vm((depth, 8), F32),
             pltpu.SemaphoreType.DMA((24,)),
         ],

time: 162 us -> 153 us (0.944)
  Pallas kernels: 161 us -> 152 us
    pallas_call x1, Pallas kernels: 153 us -> 146 us  [run_layer(): pl.pallas_call(partial(layer_kernel, heads), out_shape=(sh((SHARD, depth)...]
where the time goes in v4:
time: 153 us
  Pallas kernels  152 us (99%)
    pallas_call x1, Pallas kernels, run_layer(): pl.pallas_call(partial(layer_kernel, heads), out_shape=(sh((SHARD, depth)...  146 us
    pallas_call x1, Pallas kernels, run_final(): pl.pallas_call(partial(final_kernel, heads, ff), out_shape=(sh((shard, de...  6.13 us

profile of v4, /device:TPU:0, one launch (start us, length us, event | category | flops | bytes accessed | tf_op | source)
XLA Modules:
  0.0 152.8 jit_solution(7686474067567922600)
XLA Ops:
  0.7 145.8 %layer.1 = (bf16[512,768]{1,0:T(8,128)(2,1)}, bf16[512,768]{1,0:T(8,128)(2,1)}, bf16[1536,768]{1,0:T(8,128)(2,1)}, bf16[640,768]{1,0:T(8,128)(2,1)}) custom-call(s32[1,4]{1,0:T(1,128)} %doc_ref.1, bf16[512,768]{1,0:T(8,128)(2,1)} %tok_hbm.1, bf16[512,768]{1,0:T(8,128)(2,1)} %grad_hbm.1, f32[768]{0:T(1024)} %ag_in.3, f32[768]{0:T(1024)} %as_in.3, ...), custom_call_target="tpu_custom_call" | custom-call | tf_op jit(solution)/shard_map/layer/pallas_call | solution.py:935
  146.5 6.1 %final.1 = (bf16[512,768]{1,0:T(8,128)(2,1)}, bf16[512,768]{1,0:T(8,128)(2,1)}, f32[768]{0:T(1024)}, f32[768]{0:T(1024)}, f32[192,768]{1,0:T(8,128)}, /*index=5*...) custom-call(bf16[512,768]{1,0:T(8,128)(2,1)} %get-tuple-element.40.b, ...), custom_call_target="tpu_custom_call" | custom-call | tf_op jit(solution)/shard_map/final/pallas_call | solution.py:1034

commit v5 on v4

--- a/solution.py
+++ b/solution.py
@@ -15,8 +15,7 @@
 LONGEST = 1024
 DOCS = 4
 BIG = 1e30
-SPARE = 16
-OUT_EVERY = 6
+RATE = 11
 EPS = 1e-05
 BLK = 256
 NBLK = SLOT // BLK
@@ -241,10 +240,10 @@
                 lax.fori_loop(0, BLK // 32, add, 0)
                 self.to_cross(b).start()
 
-    def total(self, k, at):
-        own = self.part[rows_of((2 * self.m + k) * BLK + at, 32), :].astype(F32)
+    def total(self, k, at, count=32):
+        own = self.part[rows_of((2 * self.m + k) * BLK + at, count), :].astype(F32)
         index = (self.m // 2) * 2 + k
-        return own + self.mate_in[index, rows_of(at, 32), :].astype(F32) + self.cross_in[k, rows_of(at, 32), :].astype(F32)
+        return own + self.mate_in[index, rows_of(at, count), :].astype(F32) + self.cross_in[k, rows_of(at, count), :].astype(F32)
 
     def arrived(self, k):
         self.copy(self.mate_in.at[0], self.cross_in.at[k], 4 + k, self.cross).wait_recv()
@@ -267,7 +266,7 @@
     xs, gm, outp, em, ga, gb, q, qt, kx, vx, dctx, dct, left_in, cos, sine, dqh, dkv, dqkv, wqkv, wo, wu, wd, bqkv, gsum, rows_in, dsum,
     min_,
     st_a, sl_a, dg, st_b, sl_b, f_b,
-    mo, co, hid, ce, swap,
+    mo, co, hid, ce, swap, io,
     loc, ag_send, ag_recv, ra_r, ra_s, rb_r, rb_s, so_s, so_r, se_s, se_r, bf_s, bf_r,
 ):
     pairs = (heads + 1) // 2
@@ -352,11 +351,6 @@
         @pl.when(valid(m, k))
         def _():
             g_mate(m, k).start()
-    for k in range(2):
-        @pl.when(valid(m, k))
-        def _():
-            g_cross(m, k).start()
-
     build_tables(doc_ref, cos, sine)
     for n, ref in enumerate((ag_in, as_in, mg_in, ms_in, bu_in)):
         rows_in[n : n + 1, :] = ref[...].reshape(1, depth)
@@ -384,7 +378,7 @@
     lead = 3
     chip = m // 2
     hooks_in_loop = lead + steps - NBLK // 2 * heads
-    spare = SPARE
+    spare = max(0, -(-4 * EVENTS * 16 // RATE) - hooks_in_loop)
     down_at, up_at = pl.ds(0, ff), pl.ds(ff, depth)
 
     def times(vector, weight, product):
@@ -394,14 +388,14 @@
         return acc[:1]
 
     def early_rings(t):
-        total = 4 * EVENTS
-        hooks = hooks_in_loop + spare
-
         def one(n, carry):
-            rings_a.event(n % 4, n // 4)
+            rings_a.event(lax.rem(n, 4), lax.div(n, 4))
             return carry
 
-        lax.fori_loop(jnp.maximum(t, 0) * total // hooks, jnp.maximum(t + 1, 0) * total // hooks, one, 0)
+        def due(t):
+            return jnp.minimum(lax.div(jnp.maximum(t, 0) * RATE, 16), 4 * EVENTS)
+
+        lax.fori_loop(due(t), due(t + 1), one, 0)
 
     scat_o = Scatter(outp, mo, co, so_s, so_r, m, mate, cross)
     scat_e = Scatter(em, hid, ce, se_s, se_r, m, mate, cross)
@@ -524,11 +518,13 @@
                 [jnp.sum(gsum[:8, :], axis=0, keepdims=True), up_bias, jnp.zeros((6, depth), F32)], axis=0
             )
             ones = jnp.ones((8, LANES), BF16)
-            gain = jnp.zeros((8, depth), F32)
-            for c in range(0, ff, LANES):
-                for part in top_and_rest(wu[:, c : c + LANES].astype(F32) * ga[up_at, c : c + LANES]):
-                    gain = gain + dot_t(ones, part)
-            gb[misc + 11 : misc + 12, :] = gain[:1]
+            for r in range(0, depth, LANES):
+                folded = jnp.zeros((LANES, LANES), F32)
+                for c in range(0, ff, LANES):
+                    folded = folded + wu[r : r + LANES, c : c + LANES].astype(F32) * ga[ff + r : ff + r + LANES, c : c + LANES]
+                top, rest = top_and_rest(folded)
+                gain = dot_t(ones, top) + dot_t(ones, rest)
+                gb[misc + 11 : misc + 12, r : r + LANES] = gain[:1]
             gb[misc + 12 : misc + 13, :] = times(up_bias, wu, dot_t)
 
         causal = lax.broadcasted_iota(jnp.int32, (BLK, BLK), 1) <= lax.broadcasted_iota(jnp.int32, (BLK, BLK), 0)
@@ -621,11 +617,11 @@
                 if i < PADBLK - 1:
                     scat_e.collect(i + 1)
 
-        def out_rings(n):
-            @pl.when(n % OUT_EVERY == 0)
+        def out_rings(blocks):
+            @pl.when(lax.rem(blocks, 2) == 0)
             def _():
                 def one(r, carry):
-                    rings_b.event(r, n // OUT_EVERY)
+                    rings_b.event(r, lax.div(blocks, 2))
                     return carry
 
                 lax.fori_loop(0, 2, one, 0)
@@ -637,12 +633,11 @@
         after_all = len(plan) + early
         hooked = 16 + early
 
-        def pick(s, column):
-            value = plan[0][column]
-            for n, entry in enumerate(plan):
-                if entry[column] != plan[0][column]:
-                    value = jnp.where(s == n, entry[column], value)
-            return value
+        def pick(p):
+            code = jnp.int32(0)
+            for n, (what, whose, part) in enumerate(plan):
+                code = jnp.where(p == n, what + 8 * whose + 32 * part, code)
+            return lax.rem(code, 8), lax.rem(lax.div(code, 8), 4), lax.div(code, 32)
 
         def at_step(n):
             return lambda action: pl.when(step_now[0] == n)(action)
@@ -650,10 +645,10 @@
         step_now = [None]
 
         def step(s, carry):
+            block, h = carry
             planned = (s < before) | ((s >= before + early) & (s < after_all))
             p = jnp.where(s < before, s, s - early)
             step_now[0] = jnp.where(planned, p, -1)
-            t = jnp.where(s < after_all, s - before, s - after_all + early)
             early_rings(s - hooked)
 
             @at_step(0)
@@ -684,6 +679,12 @@
             def _():
                 for k in range(2):
                     x_cross(m, k).wait_send()
+
+                    @pl.when(valid(m, k))
+                    def _():
+                        g_cross(m, k).start()
+
+                for k in range(2):
                     x_cross(cross, k).wait_recv()
                     x_pass(cross, k).start()
 
@@ -711,7 +712,7 @@
                     def _():
                         g_pass(far, k).wait_recv()
 
-            @pl.when(jnp.logical_not(planned) & (t == fwd_steps))
+            @pl.when(jnp.logical_not(planned) & (block == NBLK) & (h == 0))
             def _():
                 own_tokens.start()
                 dkv[...] = jnp.zeros_like(dkv)
@@ -723,28 +724,29 @@
                     some = min(used - p * LANES, LANES)
                     gb[p * LANES : p * LANES + some, :] = t_dot(dctx[p], gm[...])[:some, :]
 
-            @pl.when(jnp.logical_not(planned) & (t >= fwd_steps))
-            def _():
-                out_rings(t - fwd_steps)
-
-            shard = shard_of(pick(p, 1))
-            half = pick(p, 2)
-            h = t % heads
-            forward_block = (t // heads + chip * (NBLK // 2)) % NBLK
-            backward_block = (t - fwd_steps) // heads
-            kind = jnp.where(planned, pick(p, 0), jnp.where(t < fwd_steps, 5, 6))
+            @pl.when(jnp.logical_not(planned) & (block >= NBLK) & (h == 0))
+            def _():
+                out_rings(block - NBLK)
+
+            what, whose, half = pick(p)
+            shard = shard_of(whose)
+            forward_block = lax.rem(block + chip * (NBLK // 2), NBLK)
+            backward_block = jnp.maximum(block - NBLK, 0)
+            kind = jnp.where(planned, what, jnp.where(block < NBLK, 5, 6))
             lax.switch(
                 kind,
                 [
-                    lambda: ff_forward(shard), lambda: ff_backward(shard, half), lambda: weights(shard // 2), lambda: after(shard),
+                    lambda: ff_forward(shard), lambda: ff_backward(shard, half), lambda: weights(lax.div(shard, 2)), lambda: after(shard),
                     norm_grads,
                     lambda: lax.switch(forward_block, [partial(att_forward, i) for i in range(NBLK)], h),
                     lambda: lax.switch(backward_block, [partial(att_backward, i) for i in reversed(range(PADBLK))], h),
                 ],
             )
-            return carry
-
-        lax.fori_loop(0, after_all + steps - early, step, 0)
+            last = h == heads - 1
+            following = jnp.where(last, block + 1, block), jnp.where(last, 0, h + 1)
+            return jnp.where(planned, block, following[0]), jnp.where(planned, h, following[1])
+
+        lax.fori_loop(0, after_all + steps - early, step, (jnp.int32(0), jnp.int32(0)))
 
     pl.run_scoped(
         body, pltpu.VMEM((SHARD, ff), F32), pltpu.VMEM((heads, NSLOT, BLK, BLK), BF16), pltpu.VMEM((heads, BLK, LANES), F32),
@@ -790,21 +792,25 @@
         return carry
 
     def finish_in(r, carry):
-        at = pl.multiple_of(r * 32, 32)
-        v = min_[rows_of(at, 32), :].astype(F32)
-        v = v - jnp.mean(v, axis=-1, keepdims=True)
-        inv = lax.rsqrt(jnp.mean(v * v, axis=-1, keepdims=True) + EPS)
-        v = v * inv
-        e = scat_e.total(r // (BLK // 32), lax.rem(at, BLK))
-        e = inv * (e - jnp.mean(e, axis=-1, keepdims=True) - v * jnp.mean(e * v, axis=-1, keepdims=True))
-        g = gm[rows_of(m * SHARD + at, 32), :].astype(F32)
-        min_[rows_of(at, 32), :] = (e + g).astype(BF16)
+        for part in range(4):
+            at = pl.multiple_of(r * 64 + part * 16, 16)
+            rows = rows_of(at, 16)
+            v = min_[rows, :].astype(F32)
+            v = v - jnp.mean(v, axis=-1, keepdims=True)
+            inv = lax.rsqrt(jnp.mean(v * v, axis=-1, keepdims=True) + EPS)
+            v = v * inv
+            e = scat_e.total(r // (BLK // 64), lax.rem(at, BLK), 16)
+            e = inv * (e - jnp.mean(e, axis=-1, keepdims=True) - v * jnp.mean(e * v, axis=-1, keepdims=True))
+            g = gm[rows_of(m * SHARD + at, 16), :].astype(F32)
+            io[part] = (e + g).astype(BF16)
+        for part in range(4):
+            min_[rows_of(r * 64 + part * 16, 16), :] = io[part]
         return carry
 
     out_block = pltpu.make_async_copy(outp.at[rows_of(m * SHARD, SHARD), :], bout_hbm, loc.at[1])
     out_in = pltpu.make_async_copy(min_, ingrad_hbm, loc.at[2])
 
-    done = (bwd_steps - 1) // OUT_EVERY
+    done = (PADBLK - 1) // 2
 
     def tail(e, carry):
         def late(n, carry):
@@ -836,7 +842,7 @@
             swap[2] = (swap[0].astype(F32) + swap[1].astype(F32)).astype(BF16)
             exchange(1, cross).start()
 
-        lax.fori_loop((e - 1) * spare // (EVENTS - 1), e * spare // (EVENTS - 1), late, 0)
+        lax.fori_loop(lax.div((e - 1) * spare, EVENTS - 1), lax.div(e * spare, EVENTS - 1), late, 0)
 
         @pl.when(e == 4)
         def _():
@@ -875,7 +881,7 @@
 
         @pl.when((e >= 5) & (e < 8))
         def _():
-            limit = jnp.where(valid(m, 1), SHARD, BLK) // 32
+            limit = jnp.where(valid(m, 1), SHARD, BLK) // 64
             lax.fori_loop((e - 5) * limit // 3, (e - 4) * limit // 3, finish_in, 0)
 
         @pl.when(e == 7)
@@ -928,7 +934,7 @@
         vm((SHARD, depth), BF16),
         *ring_refs(a_rows, 4)[:2], vm((SLOT, ff), BF16), *ring_refs(b_rows, 5),
         vm((4, BLK, depth), BF16), vm((2, BLK, depth), BF16), vm((4, BLK, depth), BF16), vm((2, BLK, depth), BF16),
-        vm((4, 32, depth), BF16),
+        vm((4, 32, depth), BF16), vm((4, 16, depth), BF16),
         dma((8,)), dma((12,)), dma((12,)), dma((4, 4, 8)), dma((4, 4)), dma((5, 4, 8)), dma((5, 4)),
         dma((6,)), dma((6,)), dma((6,)), dma((6,)), dma((2,)), dma((2,)),
     ]

time: 153 us -> 150 us (0.980)
  Pallas kernels: 152 us -> 149 us
    pallas_call x1, Pallas kernels: 146 us -> 143 us  [run_layer(): pl.pallas_call(partial(layer_kernel, heads), out_shape=(sh((SHARD, depth)...]
where the time goes in v5:
time: 150 us
  Pallas kernels  149 us (99%)
    pallas_call x1, Pallas kernels, run_layer(): pl.pallas_call(partial(layer_kernel, heads), out_shape=(sh((SHARD, depth)...  143 us
    pallas_call x1, Pallas kernels, run_final(): pl.pallas_call(partial(final_kernel, heads, ff), out_shape=(sh((shard, de...  6.13 us

profile of v5, /device:TPU:0, one launch (start us, length us, event | category | flops | bytes accessed | tf_op | source)
XLA Modules:
  0.0 149.7 jit_solution(16387541280596877771)
XLA Ops:
  0.7 142.8 %layer.1 = (bf16[512,768]{1,0:T(8,128)(2,1)}, bf16[512,768]{1,0:T(8,128)(2,1)}, bf16[1536,768]{1,0:T(8,128)(2,1)}, bf16[640,768]{1,0:T(8,128)(2,1)}) custom-call(s32[1,4]{1,0:T(1,128)} %doc_ref.1, bf16[512,768]{1,0:T(8,128)(2,1)} %tok_hbm.1, bf16[512,768]{1,0:T(8,128)(2,1)} %grad_hbm.1, f32[768]{0:T(1024)} %ag_in.3, f32[768]{0:T(1024)} %as_in.3, ...), custom_call_target="tpu_custom_call" | custom-call | tf_op jit(solution)/shard_map/layer/pallas_call | solution.py:941
  143.4 6.1 %final.1 = (bf16[512,768]{1,0:T(8,128)(2,1)}, bf16[512,768]{1,0:T(8,128)(2,1)}, f32[768]{0:T(1024)}, f32[768]{0:T(1024)}, f32[192,768]{1,0:T(8,128)}, /*index=5*...) custom-call(bf16[512,768]{1,0:T(8,128)(2,1)} %get-tuple-element.40.b, ...), custom_call_target="tpu_custom_call" | custom-call | tf_op jit(solution)/shard_map/final/pallas_call | solution.py:1040

commit v6 on v5

--- a/solution.py
+++ b/solution.py
@@ -15,7 +15,7 @@
 LONGEST = 1024
 DOCS = 4
 BIG = 1e30
-RATE = 11
+RATE = 12
 EPS = 1e-05
 BLK = 256
 NBLK = SLOT // BLK
@@ -455,7 +455,7 @@
             mark = jnp.where(same, -BIG, 0.0)
             for p in range(pairs):
                 v = rope(qf[:, p * LANES : (p + 1) * LANES], ct, st) * HD**-0.5
-                qt[p * LANES : (p + 1) * LANES, here] = jnp.transpose(v).astype(BF16)
+                qt[p * LANES : (p + 1) * LANES, here] = jnp.transpose(v.astype(BF16))
                 q[2 * p, here, :] = jnp.where(low, v, mark).astype(BF16)
                 if 2 * p + 1 < heads:
                     q[2 * p + 1, here, :] = jnp.where(low, mark, v).astype(BF16)
@@ -482,6 +482,14 @@
 
         def ff_backward(c, k):
             first = pl.multiple_of(c * SHARD + k * BLK, BLK)
+            here = pl.ds(first, BLK)
+            pl.when(valid(c, k))(lambda: hidden_grads(first))
+
+            @pl.when(jnp.logical_not(valid(c, k)))
+            def _():
+                dg[here, :] = jnp.zeros((BLK, ff), BF16)
+
+        def hidden_grads(first):
             hp[:BLK, :] = dot_t(gm[pl.ds(first, BLK), :], wd[...])
 
             def back(r, carry):
@@ -566,7 +574,7 @@
                     if i < PADBLK:
                         scaled = dctx[p, at, :].astype(F32) * norm
                         dcs = scaled.astype(BF16).astype(F32)
-                        dct[p * LANES : (p + 1) * LANES, at] = jnp.transpose(dcs).astype(BF16)
+                        dct[p * LANES : (p + 1) * LANES, at] = jnp.transpose(dcs.astype(BF16))
                         prod = dcs * c
                         for side in range(2 if full else 1):
                             inside = low if side == 0 else ~low

time: 150 us -> 149 us (level)
  no operation moved by 1% of the time
where the time goes in v6:
time: 149 us; the launch traced here: 148 us
  Pallas kernels  148 us (99%)
    pallas_call x1, Pallas kernels, run_layer(): pl.pallas_call(partial(layer_kernel, heads), out_shape=(sh((SHARD, depth)...  141 us
    pallas_call x1, Pallas kernels, run_final(): pl.pallas_call(partial(final_kernel, heads, ff), out_shape=(sh((shard, de...  6.13 us

profile of v6, /device:TPU:0, one launch (start us, length us, event | category | flops | bytes accessed | tf_op | source)
XLA Modules:
  0.0 148.4 jit_solution(3441746405510779271)
XLA Ops:
  0.7 141.4 %layer.1 = (bf16[512,768]{1,0:T(8,128)(2,1)}, bf16[512,768]{1,0:T(8,128)(2,1)}, bf16[1536,768]{1,0:T(8,128)(2,1)}, bf16[640,768]{1,0:T(8,128)(2,1)}) custom-call(s32[1,4]{1,0:T(1,128)} %doc_ref.1, bf16[512,768]{1,0:T(8,128)(2,1)} %tok_hbm.1, bf16[512,768]{1,0:T(8,128)(2,1)} %grad_hbm.1, f32[768]{0:T(1024)} %ag_in.3, f32[768]{0:T(1024)} %as_in.3, ...), custom_call_target="tpu_custom_call" | custom-call | tf_op jit(solution)/shard_map/layer/pallas_call | solution.py:949
  142.1 6.1 %final.1 = (bf16[512,768]{1,0:T(8,128)(2,1)}, bf16[512,768]{1,0:T(8,128)(2,1)}, f32[768]{0:T(1024)}, f32[768]{0:T(1024)}, f32[192,768]{1,0:T(8,128)}, /*index=5*...) custom-call(bf16[512,768]{1,0:T(8,128)(2,1)} %get-tuple-element.40.b, ...), custom_call_target="tpu_custom_call" | custom-call | tf_op jit(solution)/shard_map/final/pallas_call | solution.py:1048
